TPU v7x, 32 devices: a whole 2x2x4 slice. The times are simulated.
32 devices in a mesh: shard: 4 (over y, x), context: 2 (over core), tensor: 4 (over z).
Axes of the slice: x: 2, y: 2, z: 4, core: 2. Of those that a mesh axis runs over, the one named last changes fastest.
Arguments:
- tokens: bfloat16 [16, 1024, 768], P('shard', ('context', 'tensor')), may hold values from -6 to 6
- lengths: int32 [16], P('shard'), may hold values from 256 to 1024, as said below
- features: bfloat16 [12, 256, 64], P('tensor'), may hold values from -3 to 3, as said below
- w_qkv: bfloat16 [768, 3, 12, 64], P('shard', None, 'tensor'), may hold values from -0.3125 to 0.3125
- b_qkv: bfloat16 [3, 12, 64], P(None, 'tensor', 'shard'), may hold values from -1.5 to 1.5
- w_out: bfloat16 [768, 768], P('tensor', 'shard'), may hold values from -1.75 to 1.75
- b_out: bfloat16 [768], P('shard'), may hold values from -3 to 3
- gain_one: bfloat16 [768], P('shard'), may hold values from 0.099609375 to 1.8984375
- shift_one: bfloat16 [768], P('shard'), may hold values from -3 to 3
- w_up: bfloat16 [768, 3072], P('shard', 'tensor'), may hold values from -0.21875 to 0.21875
- b_up: bfloat16 [24, 128], P('tensor', 'shard'), may hold values from -3 to 3
- w_down: bfloat16 [3072, 768], P('tensor', 'shard'), may hold values from -0.109375 to 0.109375
- b_down: bfloat16 [768], P('shard'), may hold values from -3 to 3
- gain_two: bfloat16 [768], P('shard'), may hold values from 0.099609375 to 1.8984375
- shift_two: bfloat16 [768], P('shard'), may hold values from -3 to 3
- cotangent: bfloat16 [16, 1024, 768], P('shard', ('context', 'tensor')), may hold values from -6 to 6
Outputs:
- out: bfloat16 [16, 1024, 768], P('shard', ('context', 'tensor'))
- grad_tokens: float32 [16, 1024, 768], P('shard', ('context', 'tensor'))
- grad_w_qkv: float32 [768, 3, 12, 64], P('shard', None, 'tensor')
- grad_b_qkv: float32 [3, 12, 64], P(None, 'tensor', 'shard')
- grad_w_out: float32 [768, 768], P('tensor', 'shard')
- grad_b_out: float32 [768], P('shard')
- grad_gain_one: float32 [768], P('shard')
- grad_shift_one: float32 [768], P('shard')
- grad_w_up: float32 [768, 3072], P('shard', 'tensor')
- grad_b_up: float32 [24, 128], P('tensor', 'shard')
- grad_w_down: float32 [3072, 768], P('tensor', 'shard')
- grad_b_down: float32 [768], P('shard')
- grad_gain_two: float32 [768], P('shard')
- grad_shift_two: float32 [768], P('shard')
Inputs may be any that keep to these rules, and one draw needn't show every extreme that they name: `lengths`: at least one sequence is valid in all 1024 slots and at least one in a quarter of them. `features`: independent entries of mean 0 and variance about 1.
All inputs are finite; a program needn't handle non-finite values.
Results may differ from a plain program's by a relative error of at most 0.034.
Values may be sent and summed in bfloat16 or wider, within the bound.
No kernel may reach another device: no remote copies, remote signals or barrier semaphores. Data moves between devices by JAX's collectives and lax.ppermute only.
A program may use at most 192 MiB of HBM per device.

v0:
```python
import jax
import jax.numpy as jnp
from jax import lax
from jax.sharding import PartitionSpec as P


def layer_stats(residual):
    average = jnp.mean(residual, axis=-1, keepdims=True)
    centered = residual - average
    variance = jnp.mean(centered * centered, axis=-1, keepdims=True)
    inverse = lax.rsqrt(variance + 1e-05)
    return (centered * inverse, inverse)


def layer_back(normal, inverse, gain, upstream):
    scaled = upstream * gain
    inner = (
        scaled
        - jnp.mean(scaled, axis=-1, keepdims=True)
        - normal * jnp.mean(scaled * normal, axis=-1, keepdims=True)
    )
    return (
        inner * inverse,
        jnp.sum(upstream * normal, axis=(0, 1)),
        jnp.sum(upstream, axis=(0, 1)),
    )


def rows_full(share):
    return lax.all_gather(share, "tensor", axis=1, tiled=True)


def rows_part(partial_value):
    return lax.psum_scatter(
        partial_value.astype(jnp.bfloat16), "tensor", scatter_dimension=1, tiled=True
    ).astype(jnp.float32)


def on_device(
    tokens,
    lengths,
    features,
    w_qkv,
    b_qkv,
    w_out,
    b_out,
    gain_one,
    shift_one,
    w_up,
    b_up,
    w_down,
    b_down,
    gain_two,
    shift_two,
    cotangent,
):
    single = jnp.float32
    half = jnp.bfloat16
    whole = (
        lax.all_gather(w_qkv, "shard", axis=0, tiled=True),
        lax.all_gather(b_qkv, "shard", axis=2, tiled=True),
        lax.all_gather(w_out, "shard", axis=1, tiled=True),
        lax.all_gather(b_out, "shard", axis=0, tiled=True),
        lax.all_gather(gain_one, "shard", axis=0, tiled=True),
        lax.all_gather(shift_one, "shard", axis=0, tiled=True),
        lax.all_gather(w_up, "shard", axis=0, tiled=True),
        lax.all_gather(b_up, "shard", axis=1, tiled=True),
        lax.all_gather(w_down, "shard", axis=1, tiled=True),
        lax.all_gather(b_down, "shard", axis=0, tiled=True),
        lax.all_gather(gain_two, "shard", axis=0, tiled=True),
        lax.all_gather(shift_two, "shard", axis=0, tiled=True),
    )
    (
        qkv_weight,
        qkv_bias,
        out_weight,
        out_bias,
        gain_first,
        offset_first,
        up_weight,
        up_bias,
        down_weight,
        down_bias,
        gain_second,
        offset_second,
    ) = whole
    heads = features.shape[0]
    head_size = features.shape[2]
    width = tokens.shape[2]
    feature_scale = head_size ** (-0.25)
    full_rows = rows_full(tokens)
    span = full_rows.shape[1]
    qkv = jnp.einsum(
        "brd,dchk->brchk", full_rows, qkv_weight, preferred_element_type=single
    ) + qkv_bias.astype(single)
    queries = (qkv[:, :, 0] * feature_scale).astype(half)
    key_rows = (qkv[:, :, 1] * feature_scale).astype(half)
    values = qkv[:, :, 2].astype(half)
    position = lax.axis_index("context") * span + jnp.arange(span)
    validity = position[None, :] < lengths[:, None]
    mask_four = validity[:, :, None, None]
    query_wide = queries.astype(single)
    key_wide = key_rows.astype(single)
    query_dash = jnp.einsum(
        "brhk,hmk->brhm", queries, features, preferred_element_type=single
    ) - 0.5 * jnp.sum(query_wide * query_wide, axis=-1, keepdims=True)
    key_dash = jnp.einsum(
        "brhk,hmk->brhm", key_rows, features, preferred_element_type=single
    ) - 0.5 * jnp.sum(key_wide * key_wide, axis=-1, keepdims=True)
    query_exp = jnp.exp(query_dash - jnp.floor(jnp.max(query_dash, axis=-1, keepdims=True)))
    local_top = jnp.max(jnp.where(mask_four, key_dash, -1e30), axis=(1, 3))
    key_stab = jnp.floor(lax.pmax(local_top, "context"))
    key_exp = jnp.exp(
        jnp.where(mask_four, key_dash - key_stab[:, None, :, None], -60.0)
    ) * mask_four.astype(single)
    query_feat = query_exp.astype(half)
    key_feat = key_exp.astype(half)
    key_state = jnp.einsum("brhm,brhk->bhmk", key_feat, values, preferred_element_type=single)
    key_total = jnp.sum(key_feat, axis=1, dtype=single)
    key_state, key_total = (
        lax.psum(key_state.astype(jnp.bfloat16), "context").astype(jnp.float32),
        lax.psum(key_total.astype(jnp.bfloat16), "context").astype(jnp.float32),
    )
    state_low = key_state.astype(half)
    total_low = key_total.astype(half)
    numerator = jnp.einsum("brhm,bhmk->brhk", query_feat, state_low, preferred_element_type=single)
    denominator = jnp.einsum("brhm,bhm->brh", query_feat, total_low, preferred_element_type=single)
    ratio = numerator / denominator[..., None]
    mixed_heads = ratio.astype(half)
    out_three = out_weight.reshape(heads, head_size, width)
    attention = jnp.einsum("brhk,hkd->brd", mixed_heads, out_three, preferred_element_type=single)
    res_first = rows_part(attention) + out_bias.astype(single) + tokens.astype(single)
    normal_first, inverse_first = layer_stats(res_first)
    normed = normal_first * gain_first.astype(single) + offset_first.astype(single)
    normed_rows = rows_full(normed.astype(half))
    up_input = jnp.einsum(
        "brd,df->brf", normed_rows, up_weight, preferred_element_type=single
    ) + up_bias.reshape(-1).astype(single)
    activated = jax.nn.gelu(up_input, approximate=False).astype(half)
    feedforward = jnp.einsum("brf,fd->brd", activated, down_weight, preferred_element_type=single)
    res_second = rows_part(feedforward) + down_bias.astype(single) + normed
    normal_second, inverse_second = layer_stats(res_second)
    result = (normal_second * gain_second.astype(single) + offset_second.astype(single)).astype(
        half
    )
    whole = (
        lax.all_gather(w_qkv, "shard", axis=0, tiled=True),
        lax.all_gather(b_qkv, "shard", axis=2, tiled=True),
        lax.all_gather(w_out, "shard", axis=1, tiled=True),
        lax.all_gather(b_out, "shard", axis=0, tiled=True),
        lax.all_gather(gain_one, "shard", axis=0, tiled=True),
        lax.all_gather(shift_one, "shard", axis=0, tiled=True),
        lax.all_gather(w_up, "shard", axis=0, tiled=True),
        lax.all_gather(b_up, "shard", axis=1, tiled=True),
        lax.all_gather(w_down, "shard", axis=1, tiled=True),
        lax.all_gather(b_down, "shard", axis=0, tiled=True),
        lax.all_gather(gain_two, "shard", axis=0, tiled=True),
        lax.all_gather(shift_two, "shard", axis=0, tiled=True),
    )
    (
        qkv_weight,
        qkv_bias,
        out_weight,
        out_bias,
        gain_first,
        offset_first,
        up_weight,
        up_bias,
        down_weight,
        down_bias,
        gain_second,
        offset_second,
    ) = whole
    out_three = out_weight.reshape(heads, head_size, width)
    upstream = cotangent.astype(single)
    d_res_second, grad_gain_two, grad_shift_two = layer_back(
        normal_second, inverse_second, gain_second.astype(single), upstream
    )
    grad_b_down = jnp.sum(d_res_second, axis=(0, 1))
    ffn_rows = rows_full(d_res_second.astype(half))
    grad_w_down = jnp.einsum("brf,brd->fd", activated, ffn_rows, preferred_element_type=single)
    d_act = jnp.einsum("brd,fd->brf", ffn_rows, down_weight, preferred_element_type=single)
    slope = (
        0.5 * (1.0 + lax.erf(up_input * 0.7071067811865476))
        + up_input * jnp.exp(-0.5 * up_input * up_input) * 0.3989422804014327
    )
    d_up = (d_act * slope).astype(half)
    grad_w_up = jnp.einsum("brd,brf->df", normed_rows, d_up, preferred_element_type=single)
    grad_b_up = jnp.sum(d_up, axis=(0, 1), dtype=single).reshape(up_bias.shape)
    d_normed = (
        rows_part(jnp.einsum("brf,df->brd", d_up, up_weight, preferred_element_type=single))
        + d_res_second
    )
    d_res_first, grad_gain_one, grad_shift_one = layer_back(
        normal_first, inverse_first, gain_first.astype(single), d_normed
    )
    grad_b_out = jnp.sum(d_res_first, axis=(0, 1))
    attn_rows = rows_full(d_res_first.astype(half))
    grad_w_out = jnp.einsum(
        "brhk,brd->hkd", mixed_heads, attn_rows, preferred_element_type=single
    ).reshape(out_weight.shape)
    d_mixed = (
        jnp.einsum("brd,hkd->brhk", attn_rows, out_three, preferred_element_type=single)
        .astype(half)
        .astype(single)
    )
    d_num = d_mixed / denominator[..., None]
    d_den = -jnp.sum(d_mixed * ratio, axis=-1) / denominator
    d_state = jnp.einsum("brhm,brhk->bhmk", query_feat, d_num, preferred_element_type=single)
    d_total = jnp.einsum("brhm,brh->bhm", query_feat, d_den, preferred_element_type=single)
    d_state, d_total = (
        lax.psum(d_state.astype(jnp.bfloat16), "context").astype(jnp.float32),
        lax.psum(d_total.astype(jnp.bfloat16), "context").astype(jnp.float32),
    )
    d_query_dash = (
        jnp.einsum("brhk,bhmk->brhm", d_num, state_low, preferred_element_type=single)
        + d_den[..., None] * total_low[:, None].astype(single)
    ) * query_exp
    d_key_dash = (
        jnp.einsum("brhk,bhmk->brhm", values, d_state, preferred_element_type=single)
        + d_total[:, None]
    ) * key_exp
    d_values = jnp.einsum("brhm,bhmk->brhk", key_feat, d_state, preferred_element_type=single)
    d_queries = jnp.einsum(
        "brhm,hmk->brhk", d_query_dash.astype(half), features, preferred_element_type=single
    ) - query_wide * jnp.sum(d_query_dash, axis=-1, keepdims=True)
    d_keys = jnp.einsum(
        "brhm,hmk->brhk", d_key_dash.astype(half), features, preferred_element_type=single
    ) - key_wide * jnp.sum(d_key_dash, axis=-1, keepdims=True)
    d_qkv = jnp.stack([d_queries * feature_scale, d_keys * feature_scale, d_values], axis=2).astype(
        half
    )
    grad_w_qkv = jnp.einsum("brd,brchk->dchk", full_rows, d_qkv, preferred_element_type=single)
    grad_b_qkv = jnp.sum(d_qkv, axis=(0, 1), dtype=single)
    grad_tokens = (
        rows_part(jnp.einsum("brchk,dchk->brd", d_qkv, qkv_weight, preferred_element_type=single))
        + d_res_first
    )
    summed = (
        lax.psum(grad_w_qkv.astype(jnp.bfloat16), "context").astype(jnp.float32),
        lax.psum(grad_b_qkv.astype(jnp.bfloat16), "context").astype(jnp.float32),
        lax.psum(grad_w_out.astype(jnp.bfloat16), "context").astype(jnp.float32),
        lax.psum(grad_b_out.astype(jnp.bfloat16), "context").astype(jnp.float32),
        lax.psum(grad_gain_one.astype(jnp.bfloat16), "context").astype(jnp.float32),
        lax.psum(grad_shift_one.astype(jnp.bfloat16), "context").astype(jnp.float32),
        lax.psum(grad_w_up.astype(jnp.bfloat16), "context").astype(jnp.float32),
        lax.psum(grad_b_up.astype(jnp.bfloat16), "context").astype(jnp.float32),
        lax.psum(grad_w_down.astype(jnp.bfloat16), "context").astype(jnp.float32),
        lax.psum(grad_b_down.astype(jnp.bfloat16), "context").astype(jnp.float32),
        lax.psum(grad_gain_two.astype(jnp.bfloat16), "context").astype(jnp.float32),
        lax.psum(grad_shift_two.astype(jnp.bfloat16), "context").astype(jnp.float32),
    )
    owned = (
        lax.psum_scatter(
            summed[0].astype(jnp.bfloat16), "shard", scatter_dimension=0, tiled=True
        ).astype(jnp.float32),
        lax.psum_scatter(
            summed[1].astype(jnp.bfloat16), "shard", scatter_dimension=2, tiled=True
        ).astype(jnp.float32),
        lax.psum_scatter(
            summed[2].astype(jnp.bfloat16), "shard", scatter_dimension=1, tiled=True
        ).astype(jnp.float32),
        lax.psum_scatter(
            summed[3].astype(jnp.bfloat16), "shard", scatter_dimension=0, tiled=True
        ).astype(jnp.float32),
        lax.psum_scatter(
            summed[4].astype(jnp.bfloat16), "shard", scatter_dimension=0, tiled=True
        ).astype(jnp.float32),
        lax.psum_scatter(
            summed[5].astype(jnp.bfloat16), "shard", scatter_dimension=0, tiled=True
        ).astype(jnp.float32),
        lax.psum_scatter(
            summed[6].astype(jnp.bfloat16), "shard", scatter_dimension=0, tiled=True
        ).astype(jnp.float32),
        lax.psum_scatter(
            summed[7].astype(jnp.bfloat16), "shard", scatter_dimension=1, tiled=True
        ).astype(jnp.float32),
        lax.psum_scatter(
            summed[8].astype(jnp.bfloat16), "shard", scatter_dimension=1, tiled=True
        ).astype(jnp.float32),
        lax.psum_scatter(
            summed[9].astype(jnp.bfloat16), "shard", scatter_dimension=0, tiled=True
        ).astype(jnp.float32),
        lax.psum_scatter(
            summed[10].astype(jnp.bfloat16), "shard", scatter_dimension=0, tiled=True
        ).astype(jnp.float32),
        lax.psum_scatter(
            summed[11].astype(jnp.bfloat16), "shard", scatter_dimension=0, tiled=True
        ).astype(jnp.float32),
    )
    small = lax.psum((owned[3], owned[4], owned[5], owned[9], owned[10], owned[11]), "tensor")
    return (
        result,
        grad_tokens,
        owned[0],
        owned[1],
        owned[2],
        small[0],
        small[1],
        small[2],
        owned[6],
        owned[7],
        owned[8],
        small[3],
        small[4],
        small[5],
    )


def solution(mesh):
    in_specs = (
        P("shard", ("context", "tensor"), None),
        P("shard"),
        P("tensor", None, None),
        P("shard", None, "tensor", None),
        P(None, "tensor", "shard"),
        P("tensor", "shard"),
        P("shard"),
        P("shard"),
        P("shard"),
        P("shard", "tensor"),
        P("tensor", "shard"),
        P("tensor", "shard"),
        P("shard"),
        P("shard"),
        P("shard"),
        P("shard", ("context", "tensor"), None),
    )
    out_specs = (
        P("shard", ("context", "tensor"), None),
        P("shard", ("context", "tensor"), None),
        P("shard", None, "tensor", None),
        P(None, "tensor", "shard"),
        P("tensor", "shard"),
        P("shard"),
        P("shard"),
        P("shard"),
        P("shard", "tensor"),
        P("tensor", "shard"),
        P("tensor", "shard"),
        P("shard"),
        P("shard"),
        P("shard"),
    )
    return jax.shard_map(
        on_device, mesh=mesh, in_specs=in_specs, out_specs=out_specs, check_vma=False
    )
```

profile of v0, /device:TPU:0, one launch (start us, length us, event | category | flops | bytes accessed | tf_op | source)
XLA Modules:
  0.0 801.5 jit_solution(12452690292070927473)
XLA Ops:
  10.1 27.1 %all_gather.55 = bf16[768,3,3,64]{3,2,1,0:T(4,128)(2,1)} all-gather(bf16[192,3,3,64]{3,2,1,0:T(4,128)(2,1)S(1)} %copy.98), channel_id=1, replica_groups=mesh['shard'=4,'context'=2,'tensor'=4] {'shard'}, dimensions={0}, use_global_device_ids=true | all-gather | bytes 1105920 | tf_op jit(solution)/shard_map/all_gather | solution.py:60
  37.2 3.9 copy.99
  41.3 7.4 all_gather.56
  48.9 9.4 %all_gather.57 = bf16[192,768]{0,1:T(8,128)(2,1)S(1)} all-gather(bf16[192,192]{0,1:T(8,128)(2,1)S(1)} %copy.110), channel_id=1, replica_groups=mesh['shard'=4,'context'=2,'tensor'=4] {'shard'}, dimensions={1}, use_global_device_ids=true | all-gather | bytes 368640 | tf_op jit(solution)/shard_map/all_gather | solution.py:62
  58.5 18.1 %all-gather.8.cloned.1.call-done = bf16[4,512,768]{2,1,0:T(8,128)(2,1)} async-done(((bf16[4,128,768]{2,1,0:T(8,128)(2,1)}), bf16[4,512,768]{2,1,0:T(8,128)(2,1)}) %all-gather.8.cloned.1.call-update) | async-done | bytes 3145744 | tf_op jit(solution)/shard_map/all_gather | solution.py:30
  76.6 3.9 broadcast_add_fusion
  81.3 4.6 select_reduce_fusion
  85.9 2.4 pmax.7
  88.4 4.0 fusion.16
  92.8 1.9 fusion.135
  94.8 1.7 copy-done.2
  96.5 2.8 fusion.98
  99.4 5.4 fusion.17
  104.8 2.5 psum.155
  107.3 2.4 fusion.39
  109.7 6.8 all-reduce.22.cloned.1.call-done
  116.6 2.7 bitcast_divide_fusion
  119.3 2.7 bitcast_convert_fusion.1
  125.1 16.9 %all-reduce.15 = (bf16[768]{0:T(1024)(128)(2,1)S(1)}, bf16[768]{0:T(1024)(128)(2,1)S(1)}, bf16[768]{0:T(1024)(128)(2,1)S(1)}, bf16[768]{0:T(1024)(128)(2,1)S(1)}, bf16[768]{0:T(1024)(128)(2,1)S(1)}) all-reduce(bf16[768]{0:T(1024)(128)(2,1)S(1)} %dynamic-update-slice.2, ...), channel_id=1, replica_groups=mesh['shard'=4,'context'=2,'tensor'=4] {'shard'}, use_global_device_ids=true, to_apply=%add.2 | all-reduce | flops 3840 | bytes 15360
  142.1 41.7 %reduce-scatter.17.cloned.1.call-done = bf16[4,128,768]{2,1,0:T(8,128)(2,1)} async-done(((bf16[4,512,768]{2,1,0:T(8,128)(2,1)}), bf16[4,128,768]{2,1,0:T(8,128)(2,1)}) %reduce-scatter.17.cloned.1.call-update) | async-done | bytes 786448 | tf_op jit(solution)/shard_map/reduce_scatter | solution.py:34
  189.0 8.1 %all-gather = bf16[4,32,6]{1,2,0:T(8,128)(2,1)S(1)} all-gather(bf16[1,32,6]{1,2,0:T(8,128)(2,1)S(1)} %bitcast.222), channel_id=1, replica_groups=mesh['shard'=4,'context'=2,'tensor'=4] {'shard'}, dimensions={0}, use_global_device_ids=true | all-gather | bytes 1920 | tf_op jit(solution)/shard_map/all_gather | solution.py:67
  197.1 54.5 %all-gather.10.cloned.1.call-done = bf16[4,512,768]{2,1,0:T(8,128)(2,1)} async-done(((bf16[4,128,768]{2,1,0:T(8,128)(2,1)}), bf16[4,512,768]{2,1,0:T(8,128)(2,1)}) %all-gather.10.cloned.1.call-update) | async-done | bytes 3145744 | tf_op jit(solution)/shard_map/all_gather | solution.py:30
  251.7 6.4 fusion.67
  258.1 2.6 copy-done.13
  260.7 15.2 %fusion.2 = bf16[4,512,768]{2,1,0:T(8,128)(2,1)} fusion(f32[4,512,768]{2,1,0:T(8,128)S(1)} %get-tuple-element.81, f32[768]{0:T(1024)S(1)} %bitcast.219, u8[512,768]{1,0:T(8,128)(4,1)S(1)} %get-tuple-element.15, u8[512,768]{1,0:T(8,128)(4,1)S(1)} %get-tuple-element.14), kind=kLoop, calls=%fused_computation.4 | loop fusion | flops 111673344 | bytes 10226688 | tf_op jit(solution)/shard_map/convert_element_type | solution.py:139
  275.9 3.6 all-gather.14.cloned.1.call-done
  279.5 6.5 convolution_convert_fusion.1
  287.5 59.1 %reduce-scatter.19.cloned.1.call-done = bf16[4,128,768]{2,1,0:T(8,128)(2,1)} async-done(((bf16[4,512,768]{2,1,0:T(8,128)(2,1)}), bf16[4,128,768]{2,1,0:T(8,128)(2,1)}) %reduce-scatter.19.cloned.1.call-update) | async-done | bytes 786448 | tf_op jit(solution)/shard_map/reduce_scatter | solution.py:34
  346.6 2.0 fusion.134
  348.9 2.5 fusion.60
  351.4 1.9 fusion.132
  353.4 63.4 %all-gather.16.cloned.1.call-done = bf16[4,512,768]{2,1,0:T(8,128)(2,1)} async-done(((bf16[4,128,768]{2,1,0:T(8,128)(2,1)}), bf16[4,512,768]{2,1,0:T(8,128)(2,1)}) %all-gather.16.cloned.1.call-update) | async-done | bytes 3145744 | tf_op jit(solution)/shard_map/all_gather | solution.py:30
  416.8 7.6 fusion.143
  426.0 4.0 convolution_convert_fusion
  430.1 59.1 %reduce-scatter.21.cloned.1.call-done = bf16[4,128,768]{2,1,0:T(8,128)(2,1)} async-done(((bf16[4,512,768]{2,1,0:T(8,128)(2,1)}), bf16[4,128,768]{2,1,0:T(8,128)(2,1)}) %reduce-scatter.21.cloned.1.call-update) | async-done | bytes 786448 | tf_op jit(solution)/shard_map/reduce_scatter | solution.py:34
  489.2 3.4 multiply_reduce_fusion
  492.6 2.0 fusion.131
  497.5 62.8 %all-gather.18.cloned.1.call-done = bf16[4,512,768]{2,1,0:T(8,128)(2,1)} async-done(((bf16[4,128,768]{2,1,0:T(8,128)(2,1)}), bf16[4,512,768]{2,1,0:T(8,128)(2,1)}) %all-gather.18.cloned.1.call-update) | async-done | bytes 3145744 | tf_op jit(solution)/shard_map/all_gather | solution.py:30
  560.3 3.2 fusion.61
  564.9 1.8 fusion.95
  566.8 2.8 fusion.101
  569.6 5.7 fusion.140
  576.4 2.7 psum.157
  580.0 3.5 fusion.86
  584.0 5.7 fusion.141
  594.2 2.9 bitcast_convert_fusion.4
  597.1 2.2 copy.161
  599.4 6.6 bitcast_convert_fusion.2
  606.0 6.5 bitcast_convert_fusion.3
  615.2 21.9 %reduce-scatter.29.cloned.1.call-done = bf16[192,576]{1,0:T(8,128)(2,1)} async-done(((bf16[768,576]{1,0:T(8,128)(2,1)}), bf16[192,576]{1,0:T(8,128)(2,1)}) %reduce-scatter.29.cloned.1.call-update) | async-done | bytes 221200
  637.0 1.8 copy.162
  638.8 29.6 %reduce-scatter.27.cloned.1.call-done = bf16[768,192]{0,1:T(8,128)(2,1)} async-done(((bf16[768,768]{0,1:T(8,128)(2,1)}), bf16[768,192]{0,1:T(8,128)(2,1)}) %reduce-scatter.27.cloned.1.call-update) | async-done | bytes 294928 | tf_op jit(solution)/shard_map/reduce_scatter | solution.py:278
  668.5 32.1 %reduce-scatter.25.cloned.1.call-done = bf16[192,768]{1,0:T(8,128)(2,1)} async-done(((bf16[768,768]{1,0:T(8,128)(2,1)}), bf16[192,768]{1,0:T(8,128)(2,1)}) %reduce-scatter.25.cloned.1.call-update) | async-done | bytes 294928 | tf_op jit(solution)/shard_map/reduce_scatter | solution.py:272
  700.9 8.0 bitcast_convert_fusion
  711.7 16.3 %reduce-scatter.33.cloned.1.call-done = bf16[32,6]{1,0:T(8,128)(2,1)} async-done(((bf16[128,6]{1,0:T(8,128)(2,1)}), bf16[32,6]{1,0:T(8,128)(2,1)}) %reduce-scatter.33.cloned.1.call-update) | async-done | bytes 400
  728.7 1.8 fusion.130
  730.6 15.4 %all-reduce.14 = (bf16[768]{0:T(1024)(128)(2,1)S(1)}, bf16[3,3,64]{2,1,0:T(4,128)(2,1)S(1)}, bf16[768]{0:T(1024)(128)(2,1)S(1)}, bf16[768]{0:T(1024)(128)(2,1)S(...) all-reduce(bf16[768]{0:T(1024)(128)(2,1)S(1)} %dynamic-update-slice, ...), channel_id=1, replica_groups=mesh['shard'=4,'context'=2,'tensor'=4] {'shard'}, use_global_device_ids=true, to_apply=%add.5 | all-reduce | flops 5952 | bytes 23808
  746.5 2.5 all-reduce.16
  750.2 13.2 %all-reduce.13 = (f32[192]{0:T(256)}, f32[192]{0:T(256)}, f32[192]{0:T(256)}, f32[192]{0:T(256)}, f32[192]{0:T(256)}, /*index=5*/f32[192]{0:T(256)}) all-reduce(bf16[192]{0:T(256)(128)(2,1)S(1)} %get-tuple-element.44, bf16[192]{0:T(256)(128)(2,1)S(1)} %get-tuple-element.45, ...), channel_id=1, replica_groups=mesh['shard'=4,'context'=2,'tensor'=4] {'tensor'}, use_global_device_ids=true, to_apply=%region_35.36 | all-reduce | flops 1152 | bytes 6912 | tf_op jit(solution)/shard_map/psum | solution.py:291
  764.5 1.8 convert_element_type.304
  766.4 1.8 convert_element_type.316
  768.2 1.8 convert_element_type.320
  771.6 19.4 %reduce-scatter.23.cloned.1.call-done = bf16[4,128,768]{2,1,0:T(8,128)(2,1)} async-done(((bf16[4,512,768]{2,1,0:T(8,128)(2,1)}), bf16[4,128,768]{2,1,0:T(8,128)(2,1)}) %reduce-scatter.23.cloned.1.call-update) | async-done | bytes 786448 | tf_op jit(solution)/shard_map/reduce_scatter | solution.py:34
  791.0 2.4 convert_add_fusion
  (261 shorter events, 35.7 us)
Async XLA Ops:
  8.0 73.3 %copy-start = (bf16[3,256,64]{1,2,0:T(8,128)(2,1)S(1)}, bf16[3,256,64]{1,2,0:T(8,128)(2,1)}, u32[]{:S(2)}) copy-start(bf16[3,256,64]{1,2,0:T(8,128)(2,1)} %param.18) | copy-start | bytes 294916
  8.0 68.6 %all-gather.8.cloned.1.call-start = ((), (), s32[]{:S(2)}) async-start(), calls=%async_computation.9 | async-start | bytes 3932160 | tf_op jit(solution)/shard_map/all_gather | solution.py:30
  8.8 107.8 %all-reduce.22.cloned.1.call-start = ((), (), s32[]{:S(2)}) async-start(), calls=%async_computation.10 | async-start | bytes 786432 | tf_op jit(solution)/shard_map/psum | solution.py:121
  10.1 31.1 %copy-start.60 = (bf16[3,3,16]{2,1,0:T(4,128)(2,1)S(1)}, bf16[3,3,16]{2,1,0:T(4,128)(2,1)}, u32[]{:S(2)}) copy-start(bf16[3,3,16]{2,1,0:T(4,128)(2,1)} %param.20) | copy-start | bytes 868
  10.1 38.7 %copy-start.35 = (bf16[192,192]{1,0:T(8,128)(2,1)S(1)}, bf16[192,192]{1,0:T(8,128)(2,1)}, u32[]{:S(2)}) copy-start(bf16[192,192]{1,0:T(8,128)(2,1)} %param.21) | copy-start | bytes 221188
  10.1 48.3 %copy-start.64 = (s32[4]{0:T(128)S(1)}, s32[4]{0:T(128)}, u32[]{:S(2)}) copy-start(s32[4]{0:T(128)} %param.17) | copy-start | bytes 52
  58.5 33.9 %copy-start.43 = (f32[4,512]{1,0:T(4,128)}, f32[4,512]{1,0:T(4,128)S(1)}, u32[]{:S(2)}) copy-start(f32[4,512]{1,0:T(4,128)S(1)} %get-tuple-element.67) | copy-start | bytes 24580
  58.5 34.0 %copy-start.52 = (pred[4,512]{1,0:T(4,128)(4,1)}, pred[4,512]{1,0:T(4,128)(4,1)S(1)}, u32[]{:S(2)}) copy-start(pred[4,512]{1,0:T(4,128)(4,1)S(1)} %get-tuple-element.68) | copy-start | bytes 6148
  80.5 5.4 copy-start.16
  81.2 4.7 copy-start.20
  81.3 7.1 copy-start.17
  81.3 11.2 %copy-start.32 = (f32[4,512,3]{1,0,2:T(4,128)}, f32[4,512,3]{1,0,2:T(4,128)S(1)}, u32[]{:S(2)}) copy-start(f32[4,512,3]{1,0,2:T(4,128)S(1)} %copy_multiply_fusion.1) | copy-start | bytes 73732
  88.4 11.0 %copy-start.27 = (f32[4,512,3]{1,0,2:T(4,128)}, f32[4,512,3]{1,0,2:T(4,128)S(1)}, u32[]{:S(2)}) copy-start(f32[4,512,3]{1,0,2:T(4,128)S(1)} %copy_multiply_fusion) | copy-start | bytes 73732
  88.4 4.4 copy-start.12
  92.4 7.0 copy-start.34
  99.4 84.4 %reduce-scatter.17.cloned.1.call-start = ((), (), s32[]{:S(2)}) async-start(), calls=%async_computation.11 | async-start | bytes 3932160 | tf_op jit(solution)/shard_map/reduce_scatter | solution.py:34
  109.7 6.9 copy-start.28
  109.7 9.5 %copy-start.45 = (f32[4,3,1,512]{3,1,0,2:T(4,128)}, f32[4,3,1,512]{3,1,0,2:T(4,128)S(1)}, u32[]{:S(2)}) copy-start(f32[4,3,1,512]{3,1,0,2:T(4,128)S(1)} %copy.234) | copy-start | bytes 73732
  122.0 61.8 %copy-start.1 = (bf16[4,128,768]{2,1,0:T(8,128)(2,1)S(1)}, bf16[4,128,768]{2,1,0:T(8,128)(2,1)}, u32[]{:S(2)}) copy-start(bf16[4,128,768]{2,1,0:T(8,128)(2,1)} %param.16) | copy-start | bytes 2359300
  122.0 75.1 %all-gather.12.cloned.1.call-start = ((), (), s32[]{:S(2)}) async-start(), calls=%async_computation.13 | async-start | bytes 1474560 | tf_op jit(solution)/shard_map/all_gather | solution.py:66
  122.6 129.0 %all-gather.10.cloned.1.call-start = ((), (), s32[]{:S(2)}) async-start(), calls=%async_computation.12 | async-start | bytes 3932160 | tf_op jit(solution)/shard_map/all_gather | solution.py:30
  142.1 46.3 %copy-start.42 = (f32[768]{0:T(1024)}, f32[768]{0:T(1024)S(1)}, u32[]{:S(2)}) copy-start(f32[768]{0:T(1024)S(1)} %convert_element_type.275) | copy-start | bytes 9220
  142.1 46.9 %copy-start.61 = (bf16[6,32]{1,0:T(8,128)(2,1)S(1)}, bf16[6,32]{1,0:T(8,128)(2,1)}, u32[]{:S(2)}) copy-start(bf16[6,32]{1,0:T(8,128)(2,1)} %param.26) | copy-start | bytes 1156
  185.3 66.3 %copy-start.36 = (f32[4,128]{1,0:T(4,128)}, f32[4,128]{1,0:T(4,128)S(1)}, u32[]{:S(2)}) copy-start(f32[4,128]{1,0:T(4,128)S(1)} %broadcast_multiply_fusion.5) | copy-start | bytes 6148
  186.9 64.7 %copy-start.39 = (f32[4,128]{1,0:T(4,128)}, f32[4,128]{1,0:T(4,128)S(1)}, u32[]{:S(2)}) copy-start(f32[4,128]{1,0:T(4,128)S(1)} %add_rsqrt_fusion.1) | copy-start | bytes 6148
  188.3 91.2 %all-gather.14.cloned.1.call-start = ((), (), s32[]{:S(2)}) async-start(), calls=%async_computation.14 | async-start | bytes 1474560 | tf_op jit(solution)/shard_map/all_gather | solution.py:68
  188.9 157.7 %reduce-scatter.19.cloned.1.call-start = ((), (), s32[]{:S(2)}) async-start(), calls=%async_computation.15 | async-start | bytes 3932160 | tf_op jit(solution)/shard_map/reduce_scatter | solution.py:34
  197.1 61.0 %copy-start.49 = (f32[128,6]{0,1:T(8,128)}, f32[128,6]{0,1:T(8,128)S(1)}, u32[]{:S(2)}) copy-start(f32[128,6]{0,1:T(8,128)S(1)} %reshape.211) | copy-start | bytes 9220
  286.1 130.7 %all-gather.16.cloned.1.call-start = ((), (), s32[]{:S(2)}) async-start(), calls=%async_computation.16 | async-start | bytes 3932160 | tf_op jit(solution)/shard_map/all_gather | solution.py:30
  346.6 4.8 copy-start.10
  348.6 4.8 copy-start.40
  353.4 135.9 %reduce-scatter.21.cloned.1.call-start = ((), (), s32[]{:S(2)}) async-start(), calls=%async_computation.17 | async-start | bytes 3932160 | tf_op jit(solution)/shard_map/reduce_scatter | solution.py:34
  416.8 9.2 %copy-start.66 = (bf16[768,768]{1,0:T(8,128)(2,1)S(1)}, bf16[768,768]{1,0:T(8,128)(2,1)}, u32[]{:S(2)}) copy-start(bf16[768,768]{1,0:T(8,128)(2,1)} %all-gather.12.cloned.1.call-done) | copy-start | bytes 3538948
  430.1 130.2 %all-gather.18.cloned.1.call-start = ((), (), s32[]{:S(2)}) async-start(), calls=%async_computation.18 | async-start | bytes 3932160 | tf_op jit(solution)/shard_map/all_gather | solution.py:30
  494.7 65.6 %copy-start.15 = (f32[4,512,3,64]{1,3,2,0:T(8,128)S(1)}, f32[4,512,3,64]{1,3,2,0:T(8,128)}, u32[]{:S(2)}) copy-start(f32[4,512,3,64]{1,3,2,0:T(8,128)} %copy-done.14) | copy-start | bytes 4718596
  496.8 87.2 %all-reduce.24.cloned.1.call-start = ((), (), s32[]{:S(2)}) async-start(), calls=%async_computation.19 | async-start | bytes 786432 | tf_op jit(solution)/shard_map/psum | solution.py:212
  560.3 4.6 copy-start.8
  560.3 4.6 copy-start.46
  566.7 46.8 %reduce-scatter.31.cloned.1.call-start = ((), (), s32[]{:S(2)}) async-start(), calls=%async_computation.24 | async-start | bytes 491520
  569.6 5.8 copy-start.9
  569.6 5.8 copy-start.31
  575.4 4.6 copy-start.18
  576.3 7.7 copy-start.33
  576.3 7.7 copy-start.44
  576.3 7.7 copy-start.53
  576.3 7.7 copy-start.58
  583.5 6.2 copy-start.21
  583.5 53.5 %reduce-scatter.29.cloned.1.call-start = ((), (), s32[]{:S(2)}) async-start(), calls=%async_computation.23 | async-start | bytes 1228800
  591.7 5.5 copy-start.23
  599.4 69.1 %reduce-scatter.27.cloned.1.call-start = ((), (), s32[]{:S(2)}) async-start(), calls=%async_computation.22 | async-start | bytes 1474560 | tf_op jit(solution)/shard_map/reduce_scatter | solution.py:278
  606.0 6.7 copy-start.62
  606.0 94.5 %reduce-scatter.25.cloned.1.call-start = ((), (), s32[]{:S(2)}) async-start(), calls=%async_computation.21 | async-start | bytes 1474560 | tf_op jit(solution)/shard_map/reduce_scatter | solution.py:272
  612.6 115.3 %reduce-scatter.33.cloned.1.call-start = ((), (), s32[]{:S(2)}) async-start(), calls=%async_computation.25 | async-start | bytes 40960
  613.4 151.1 %all-reduce.26.cloned.1.call-start = ((), (), s32[]{:S(2)}) async-start(), calls=%async_computation.26 | async-start | bytes 1966080 | tf_op jit(solution)/shard_map/psum | solution.py:240
  700.6 90.4 %reduce-scatter.23.cloned.1.call-start = ((), (), s32[]{:S(2)}) async-start(), calls=%async_computation.20 | async-start | bytes 3932160 | tf_op jit(solution)/shard_map/reduce_scatter | solution.py:34
  708.8 21.7 %copy-start.51 = (bf16[768]{0:T(1024)(128)(2,1)S(1)}, bf16[768]{0:T(1024)(128)(2,1)}, u32[]{:S(2)}) copy-start(bf16[768]{0:T(1024)(128)(2,1)} %get-tuple-element.55) | copy-start | bytes 4612
  708.8 21.7 %copy-start.54 = (bf16[768]{0:T(1024)(128)(2,1)S(1)}, bf16[768]{0:T(1024)(128)(2,1)}, u32[]{:S(2)}) copy-start(bf16[768]{0:T(1024)(128)(2,1)} %get-tuple-element.16) | copy-start | bytes 4612
  708.8 21.7 %copy-start.55 = (bf16[768]{0:T(1024)(128)(2,1)S(1)}, bf16[768]{0:T(1024)(128)(2,1)}, u32[]{:S(2)}) copy-start(bf16[768]{0:T(1024)(128)(2,1)} %get-tuple-element.21) | copy-start | bytes 4612
  708.8 21.7 %copy-start.56 = (bf16[768]{0:T(1024)(128)(2,1)S(1)}, bf16[768]{0:T(1024)(128)(2,1)}, u32[]{:S(2)}) copy-start(bf16[768]{0:T(1024)(128)(2,1)} %get-tuple-element.22) | copy-start | bytes 4612
  708.9 21.7 %copy-start.59 = (bf16[768]{0:T(1024)(128)(2,1)S(1)}, bf16[768]{0:T(1024)(128)(2,1)}, u32[]{:S(2)}) copy-start(bf16[768]{0:T(1024)(128)(2,1)} %get-tuple-element.19) | copy-start | bytes 4612
  708.9 54.5 %copy-start.38 = (f32[768]{0:T(1024)S(1)}, f32[768]{0:T(1024)}, u32[]{:S(2)}) copy-start(f32[768]{0:T(1024)} %convert_element_type.283) | copy-start | bytes 9220
  708.9 54.5 %copy-start.41 = (f32[4,128]{1,0:T(4,128)S(1)}, f32[4,128]{1,0:T(4,128)}, u32[]{:S(2)}) copy-start(f32[4,128]{1,0:T(4,128)} %copy-done.40) | copy-start | bytes 6148
  708.9 54.4 %copy-start.48 = (f32[4,128]{1,0:T(4,128)S(1)}, f32[4,128]{1,0:T(4,128)}, u32[]{:S(2)}) copy-start(f32[4,128]{1,0:T(4,128)} %copy-done.47) | copy-start | bytes 6148
  730.5 60.5 %copy-start.6 = (f32[4,128,768]{2,1,0:T(8,128)S(1)}, f32[4,128,768]{2,1,0:T(8,128)}, u32[]{:S(2)}) copy-start(f32[4,128,768]{2,1,0:T(8,128)} %copy-done.5) | copy-start | bytes 4718596
  (29 other events, 69.1 us)
Sparse Core Ops, SparseCore 0:
  10.4 66.1 all-gather.7
  99.5 17.0 all-reduce.21
  122.2 61.5 reduce-scatter.16
  353.5 63.2 all-gather.15
  496.9 63.2 all-gather.17
  566.9 17.1 all-reduce.23
  700.7 19.4 all-reduce.25
Sparse Core Ops, SparseCore 1:
  124.4 28.7 all-gather.11
  188.4 63.2 all-gather.9
  253.4 26.1 all-gather.13
  286.2 60.4 reduce-scatter.18
  430.2 59.0 reduce-scatter.20
  583.6 23.1 reduce-scatter.30
  609.6 27.3 reduce-scatter.28
  639.8 28.6 reduce-scatter.26
  671.8 28.6 reduce-scatter.24
  703.9 24.0 reduce-scatter.32
  730.1 60.8 reduce-scatter.22
where the time goes:
time: 810 us; the launch traced here: 801 us
  waiting for transfers between devices  491 us (61%)
  blocking collectives  107 us (13%)
  matrix products  97.5 us (12%)
  other arithmetic  56.6 us (7%)
  local copies, waits for them, and re-layouts  28.8 us (4%)
  between operations  19.2 us (2%)
    all_gather x4, waiting for transfers between devices, rows_full(): return lax.all_gather(share, 'tensor', axis=1, tiled=True)  199 us
    reduce_scatter x4, waiting for transfers between devices, rows_part(): lax.psum_scatter(partial_value.astype(jnp.bfloat16), 'tensor', scatter_di...  179 us
    unnamed x21, waiting for transfers between devices  40.1 us
    unnamed x2, blocking collectives  32.3 us
    reduce_scatter x1, waiting for transfers between devices, on_device(): lax.psum_scatter(summed[6].astype(jnp.bfloat16), 'shard', scatter_dimensi...  32.1 us
    reduce_scatter x1, waiting for transfers between devices, on_device(): lax.psum_scatter(summed[8].astype(jnp.bfloat16), 'shard', scatter_dimensi...  29.6 us
    all_gather x1, blocking collectives, on_device(): lax.all_gather(w_qkv, 'shard', axis=0, tiled=True)  27.1 us
    unnamed x179, local copies, waits for them, and re-layouts  23.8 us
  transfers between devices with their start and end apart: 18, of which 15 were waited for; matrix products, arithmetic and copies ran while one was open for 14% of the time, Pallas kernels for 0%

commit v1 on v0

v1 whole, which is shorter than its diff:
```python
import functools

import jax
import jax.numpy as jnp
from jax import lax
from jax.experimental import pallas as pl
from jax.experimental.pallas import tpu as pltpu
from jax.sharding import PartitionSpec as P

F = jnp.float32
B = jnp.bfloat16


def layer_stats(residual):
    average = jnp.mean(residual, axis=-1, keepdims=True)
    centered = residual - average
    variance = jnp.mean(centered * centered, axis=-1, keepdims=True)
    inverse = lax.rsqrt(variance + 1e-05)
    return (centered * inverse, inverse)


def layer_back(normal, inverse, gain, upstream):
    scaled = upstream * gain
    inner = (
        scaled
        - jnp.mean(scaled, axis=-1, keepdims=True)
        - normal * jnp.mean(scaled * normal, axis=-1, keepdims=True)
    )
    return (
        inner * inverse,
        jnp.sum(upstream * normal, axis=0),
        jnp.sum(upstream, axis=0),
    )


def wide_add(*terms):
    total = terms[0].astype(F)
    for term in terms[1:]:
        total = total + term.astype(F)
    return total


class Links:
    def __init__(self, sizes):
        self.sizes = sizes
        self.s = lax.axis_index("shard")
        self.c = lax.axis_index("context")
        self.t = lax.axis_index("tensor")
        self.core = self.c % 2

    def perm_t(self, value, step):
        n = self.sizes["tensor"]
        return lax.ppermute(value, "tensor", [(i, (i + step) % n) for i in range(n)])

    def perm_s(self, value, mask):
        n = self.sizes["shard"]
        return lax.ppermute(value, "shard", [(i, i ^ mask) for i in range(n)])

    def perm_c(self, value, mask=1):
        n = self.sizes["context"]
        return lax.ppermute(value, "context", [(i, i ^ mask) for i in range(n)])

    def deal(self, rows):
        n = self.sizes["tensor"]
        pieces = [lax.dynamic_index_in_dim(rows, self.t, 0, keepdims=False)]
        for d in range(1, n):
            piece = lax.dynamic_index_in_dim(rows, (self.t + d) % n, 0, keepdims=False)
            pieces.append(self.perm_t(piece, d))
        return jnp.concatenate(pieces, axis=0)

    def undeal(self, rows):
        n = self.sizes["tensor"]
        rows = rows.reshape(n, rows.shape[0] // n, rows.shape[1])
        result = jnp.zeros(rows.shape, rows.dtype)
        for d in range(n):
            piece = rows[d] if d == 0 else self.perm_t(rows[d], n - d)
            result = lax.dynamic_update_index_in_dim(result, piece, (self.t + d) % n, 0)
        return result

    def spread(self, local):
        n = self.sizes["tensor"]
        block = jnp.stack([local] + [self.perm_t(local, d) for d in range(1, n)])
        over_x = self.perm_s(block, 1)
        over_y = self.perm_s(block, 2)
        far = (self.perm_s(over_x[: n // 2], 2), self.perm_s(over_y[n // 2 :], 1))
        mine = [block, over_x, over_y, far[0], far[1]]
        other = [self.perm_c(piece) for piece in mine]
        return mine + other

    def half(self, local):
        rows = local.shape[0] // 2
        return lax.dynamic_slice_in_dim(local, self.core * rows, rows, 0)

    def collect(self, grad):
        n, m = self.sizes["tensor"], self.sizes["shard"]
        rows, cols = grad.shape[1] // m, grad.shape[2]
        parts = grad.reshape(n, m, 2, rows // 2, cols)
        keep = lax.dynamic_index_in_dim(parts, self.core, 2, keepdims=False)
        give = lax.dynamic_index_in_dim(parts, 1 - self.core, 2, keepdims=False)
        parts = wide_add(keep, self.perm_c(give)).astype(B)

        def to(mask):
            return lax.dynamic_index_in_dim(parts, self.s ^ mask, 1, keepdims=False)

        near, beside, above, far = to(0), to(1), to(2), to(3)
        h = n // 2
        via_y = self.perm_s(far[:h], 2)
        via_x = self.perm_s(far[h:], 1)
        beside = jnp.concatenate([wide_add(beside[:h], via_y).astype(B), beside[h:]])
        above = jnp.concatenate([above[:h], wide_add(above[h:], via_x).astype(B)])
        parts = wide_add(near, self.perm_s(beside, 1), self.perm_s(above, 2)).astype(B)
        total = wide_add(parts[0], *[self.perm_t(parts[d], n - d) for d in range(1, n)])
        mask = 2
        while mask < self.sizes["context"]:
            low = total.astype(B)
            total = wide_add(low, self.perm_c(low, mask))
            mask *= 2
        low = total.astype(B)
        other = self.perm_c(low)
        first = jnp.where(self.core == 0, low, other)
        second = jnp.where(self.core == 0, other, low)
        return jnp.concatenate([first, second])


def assemble(links, pieces, rows, extra):
    n, m = links.sizes["tensor"], links.sizes["shard"]
    cols = pieces[0].shape[-1]
    where = jnp.stack([links.s, links.core]).astype(jnp.int32)
    count = 2 * (n // 1) * 3 + 2 * n

    def body(where_ref, *refs):
        ins, outs, sems = refs[:10], refs[10:-1], refs[-1]
        s, c = where_ref[0], where_ref[1]
        copies = []
        for i in range(2):
            half = c if i == 0 else 1 - c
            for j in range(m):
                shard = s ^ j
                start = pl.multiple_of(shard * (2 * rows) + half * rows, 8)
                for t in range(n):
                    if j < 3:
                        src = ins[i * 5 + j].at[t]
                    elif t < n // 2:
                        src = ins[i * 5 + 3].at[t]
                    else:
                        src = ins[i * 5 + 4].at[t - n // 2]
                    copies.append((src.at[pl.ds(0, rows)], outs[0].at[t, pl.ds(start, rows)]))
                    if extra and i == 0:
                        copies.append((src.at[pl.ds(rows, extra)], outs[1].at[shard, t]))
        running = [
            pltpu.make_async_copy(a, b, sems.at[k]) for k, (a, b) in enumerate(copies)
        ]
        for r in running:
            r.start()
        for r in running:
            r.wait()

    shapes = [jax.ShapeDtypeStruct((n, m * 2 * rows, cols), B)]
    if extra:
        shapes.append(jax.ShapeDtypeStruct((m, n, extra, cols), B))
    total = 2 * m * n + (m * n if extra else 0)
    return pl.pallas_call(
        body,
        out_shape=shapes,
        in_specs=[pl.BlockSpec(memory_space=pltpu.SMEM)]
        + [pl.BlockSpec(memory_space=pl.ANY)] * 10,
        out_specs=[pl.BlockSpec(memory_space=pl.ANY)] * len(shapes),
        scratch_shapes=[pltpu.SemaphoreType.DMA((total,))],
        name="assemble",
    )(where, *pieces)


def on_device(
    sizes,
    tokens,
    lengths,
    features,
    w_qkv,
    b_qkv,
    w_out,
    b_out,
    gain_one,
    shift_one,
    w_up,
    b_up,
    w_down,
    b_down,
    gain_two,
    shift_two,
    cotangent,
):
    links = Links(sizes)
    n, m = sizes["tensor"], sizes["shard"]
    chunk = tokens.shape[1]
    width = tokens.shape[2]
    heads_local, feats, hd = features.shape
    heads = heads_local * n
    share = width // m
    qkv_cols = 3 * heads_local * hd
    small = jnp.concatenate(
        [b_out, gain_one, shift_one, b_down, gain_two, shift_two, b_qkv.reshape(-1), b_up.reshape(-1)]
    )
    used = small.shape[0]
    small = jnp.pad(small, (0, 8 * qkv_cols - used)).reshape(8, qkv_cols)
    flat_qkv = w_qkv.reshape(share, qkv_cols)
    first = jnp.concatenate([links.half(flat_qkv), small])
    pieces_qkv = links.spread(first)
    x = links.deal(tokens)
    feat_t = features.transpose(2, 0, 1).reshape(hd, heads_local * feats)
    feat_half = links.half(feat_t)
    feat_mine = jnp.stack([feat_half] + [links.perm_t(feat_half, d) for d in range(1, n)])
    feat_other = links.perm_c(feat_mine)
    feat_low = jnp.where(links.core == 0, feat_mine, feat_other)
    feat_high = jnp.where(links.core == 0, feat_other, feat_mine)
    feat = jnp.concatenate([feat_low, feat_high], axis=1)
    feat = feat.reshape(n, hd, heads_local, feats).transpose(0, 2, 1, 3).reshape(heads, hd, feats)
    mid = jnp.concatenate([links.half(w_out.T), links.half(w_up)], axis=1)
    pieces_mid = links.spread(mid)
    pieces_down = links.spread(links.half(w_down.T))
    upstream = links.deal(cotangent).astype(F)
    rows = share // 2
    wq, smalls = assemble(links, pieces_qkv, rows, 8)
    wm = assemble(links, pieces_mid, rows, 0)[0]
    wd = assemble(links, pieces_down, rows, 0)[0]
    smalls = smalls.reshape(m, n, 8 * qkv_cols).astype(F)
    vec = smalls[:, 0, : 6 * share].reshape(m, 6, share).transpose(1, 0, 2).reshape(6, width)
    bias_out, gain_first, offset_first, bias_down, gain_second, offset_second = vec
    a = 6 * share
    bq = b_qkv.size
    bias_qkv = (
        smalls[:, :, a : a + bq]
        .reshape(m, n, 3, heads_local, hd // m)
        .transpose(1, 2, 3, 0, 4)
        .reshape(n, qkv_cols)
    )
    a += bq
    bias_up = (
        smalls[:, :, a : a + b_up.size]
        .reshape((m, n) + b_up.shape)
        .transpose(1, 2, 0, 3)
        .reshape(n, -1)
    )
    hidden = b_up.size * m
    out_cols = heads_local * hd
    w_out_t = wm[:, :, :out_cols]
    w_up_t = wm[:, :, out_cols:]
    length = lax.dynamic_index_in_dim(lengths, links.t, 0, keepdims=False)
    order = (links.t - jnp.arange(n)) % n
    position = (links.c * (n * chunk) + order[:, None] * chunk + jnp.arange(chunk)[None]).reshape(-1)
    mask = (position < length)[:, None, None]
    dot = functools.partial(jnp.einsum, preferred_element_type=F)
    scale = hd ** (-0.25)
    qkv = dot("rd,tdj->rtj", x, wq) + bias_qkv[None]
    span = x.shape[0]
    qkv = qkv.reshape(span, n, 3, heads_local, hd)
    queries = (qkv[:, :, 0] * scale).astype(B).reshape(span, heads, hd)
    keys = (qkv[:, :, 1] * scale).astype(B).reshape(span, heads, hd)
    values = qkv[:, :, 2].astype(B).reshape(span, heads, hd)
    query_wide = queries.astype(F)
    key_wide = keys.astype(F)
    query_dash = dot("rhk,hkm->rhm", queries, feat) - 0.5 * jnp.sum(
        query_wide * query_wide, axis=-1, keepdims=True
    )
    key_dash = dot("rhk,hkm->rhm", keys, feat) - 0.5 * jnp.sum(
        key_wide * key_wide, axis=-1, keepdims=True
    )
    query_exp = jnp.exp(query_dash - jnp.floor(jnp.max(query_dash, axis=-1, keepdims=True)))
    local_top = jnp.max(jnp.where(mask, key_dash, -1e30), axis=(0, 2))
    key_stab = jnp.floor(lax.pmax(local_top, "context"))
    key_exp = jnp.exp(jnp.where(mask, key_dash - key_stab[None, :, None], -60.0)) * mask.astype(F)
    query_feat = query_exp.astype(B)
    key_feat = key_exp.astype(B)
    key_state = dot("rhm,rhk->hmk", key_feat, values)
    key_total = jnp.sum(key_feat, axis=0, dtype=F)
    state_low = lax.psum(key_state.astype(B), "context")
    total_low = lax.psum(key_total.astype(B), "context")
    numerator = dot("rhm,hmk->rhk", query_feat, state_low)
    denominator = dot("rhm,hm->rh", query_feat, total_low)
    ratio = numerator / denominator[..., None]
    mixed = ratio.astype(B)
    mixed_t = mixed.reshape(span, n, out_cols)
    attention = dot("rtk,tdk->rd", mixed_t, w_out_t)
    res_first = attention + bias_out + x.astype(F)
    normal_first, inverse_first = layer_stats(res_first)
    normed = normal_first * gain_first + offset_first
    normed_low = normed.astype(B)
    up_input = dot("rd,tdf->rtf", normed_low, w_up_t) + bias_up[None]
    activated = jax.nn.gelu(up_input, approximate=False).astype(B)
    feedforward = dot("rtf,tdf->rd", activated, wd)
    res_second = feedforward + bias_down + normed
    normal_second, inverse_second = layer_stats(res_second)
    result = links.undeal((normal_second * gain_second + offset_second).astype(B))
    d_res_second, grad_gain_two, grad_shift_two = layer_back(
        normal_second, inverse_second, gain_second, upstream
    )
    grad_b_down = jnp.sum(d_res_second, axis=0)
    d_ffn = d_res_second.astype(B)
    grad_down = dot("rd,rtf->tdf", d_ffn, activated).astype(B)
    own_down = links.collect(grad_down)
    d_act = dot("rd,tdf->rtf", d_ffn, wd)
    slope = (
        0.5 * (1.0 + lax.erf(up_input * 0.7071067811865476))
        + up_input * jnp.exp(-0.5 * up_input * up_input) * 0.3989422804014327
    )
    d_up = (d_act * slope).astype(B)
    grad_up = dot("rd,rtf->tdf", normed_low, d_up).astype(B)
    grad_b_up = jnp.sum(d_up, axis=0, dtype=F)
    d_normed = dot("rtf,tdf->rd", d_up, w_up_t) + d_res_second
    d_res_first, grad_gain_one, grad_shift_one = layer_back(
        normal_first, inverse_first, gain_first, d_normed
    )
    grad_b_out = jnp.sum(d_res_first, axis=0)
    d_attn = d_res_first.astype(B)
    grad_out = dot("rd,rtk->tdk", d_attn, mixed_t).astype(B)
    own_mid = links.collect(jnp.concatenate([grad_out, grad_up], axis=2))
    d_mixed = dot("rd,tdk->rtk", d_attn, w_out_t).astype(B).astype(F).reshape(span, heads, hd)
    d_num = d_mixed / denominator[..., None]
    d_den = -jnp.sum(d_mixed * ratio, axis=-1) / denominator
    d_state = dot("rhm,rhk->hmk", query_feat, d_num)
    d_total = dot("rhm,rh->hm", query_feat, d_den)
    d_state = lax.psum(d_state.astype(B), "context").astype(F)
    d_total = lax.psum(d_total.astype(B), "context").astype(F)
    d_query_dash = (
        dot("rhk,hmk->rhm", d_num, state_low) + d_den[..., None] * total_low[None].astype(F)
    ) * query_exp
    d_key_dash = (dot("rhk,hmk->rhm", values, d_state) + d_total[None]) * key_exp
    d_values = dot("rhm,hmk->rhk", key_feat, d_state)
    d_queries = dot("rhm,hkm->rhk", d_query_dash.astype(B), feat) - query_wide * jnp.sum(
        d_query_dash, axis=-1, keepdims=True
    )
    d_keys = dot("rhm,hkm->rhk", d_key_dash.astype(B), feat) - key_wide * jnp.sum(
        d_key_dash, axis=-1, keepdims=True
    )
    d_qkv = (
        jnp.stack(
            [
                (d_queries * scale).reshape(span, n, heads_local, hd),
                (d_keys * scale).reshape(span, n, heads_local, hd),
                d_values.reshape(span, n, heads_local, hd),
            ],
            axis=2,
        )
        .astype(B)
        .reshape(span, n, qkv_cols)
    )
    grad_qkv = dot("rd,rtj->tdj", x, d_qkv).astype(B)
    grad_b_qkv = jnp.sum(d_qkv, axis=0, dtype=F)
    grad_x = dot("rtj,tdj->rd", d_qkv, wq) + d_res_first
    grad_tokens = links.undeal(grad_x.astype(B)).astype(F)
    vecs = jnp.stack(
        [grad_b_out, grad_gain_one, grad_shift_one, grad_b_down, grad_gain_two, grad_shift_two]
    )
    vecs = vecs.reshape(6, m, share).transpose(1, 0, 2).reshape(m, 6 * share)
    small_qkv = (
        grad_b_qkv.reshape(n, 3, heads_local, m, hd // m).transpose(0, 3, 1, 2, 4).reshape(n, m, -1)
    )
    small_up = (
        grad_b_up.reshape(n, b_up.shape[0], m, b_up.shape[1]).transpose(0, 2, 1, 3).reshape(n, m, -1)
    )
    packed = jnp.concatenate(
        [jnp.broadcast_to(vecs[None], (n, m, 6 * share)), small_qkv, small_up], axis=2
    )
    packed = jnp.pad(packed, ((0, 0), (0, 0), (0, 16 * qkv_cols - used))).reshape(
        n, m, 16, qkv_cols
    )
    grad_qkv = jnp.concatenate(
        [
            grad_qkv.reshape(n, m, 2, rows, qkv_cols),
            packed.astype(B).reshape(n, m, 2, 8, qkv_cols),
        ],
        axis=3,
    ).reshape(n, m * 2 * (rows + 8), qkv_cols)
    own_qkv = links.collect(grad_qkv)
    own_qkv = own_qkv.reshape(2, rows + 8, qkv_cols)
    own_small = own_qkv[:, rows:].reshape(-1)[:used].astype(F)
    own_w_qkv = own_qkv[:, :rows].reshape(share, 3, heads_local, hd).astype(F)
    v = own_small[: 6 * share].reshape(6, share)
    own_b_qkv = own_small[6 * share : 6 * share + bq].reshape(b_qkv.shape)
    own_b_up = own_small[6 * share + bq :].reshape(b_up.shape)
    return (
        result,
        grad_tokens,
        own_w_qkv,
        own_b_qkv,
        own_mid[:, :out_cols].T.astype(F),
        v[0],
        v[1],
        v[2],
        own_mid[:, out_cols:].astype(F),
        own_b_up,
        own_down.T.astype(F),
        v[3],
        v[4],
        v[5],
    )


def solution(mesh):
    sizes = dict(mesh.shape)
    in_specs = (
        P("shard", ("context", "tensor"), None),
        P("shard"),
        P("tensor", None, None),
        P("shard", None, "tensor", None),
        P(None, "tensor", "shard"),
        P("tensor", "shard"),
        P("shard"),
        P("shard"),
        P("shard"),
        P("shard", "tensor"),
        P("tensor", "shard"),
        P("tensor", "shard"),
        P("shard"),
        P("shard"),
        P("shard"),
        P("shard", ("context", "tensor"), None),
    )
    out_specs = (
        P("shard", ("context", "tensor"), None),
        P("shard", ("context", "tensor"), None),
        P("shard", None, "tensor", None),
        P(None, "tensor", "shard"),
        P("tensor", "shard"),
        P("shard"),
        P("shard"),
        P("shard"),
        P("shard", "tensor"),
        P("tensor", "shard"),
        P("tensor", "shard"),
        P("shard"),
        P("shard"),
        P("shard"),
    )
    return jax.shard_map(
        functools.partial(on_device, sizes),
        mesh=mesh,
        in_specs=in_specs,
        out_specs=out_specs,
        check_vma=False,
    )
```

time: 810 us -> 918 us (1.13)
  Pallas kernels: 0 us -> 464 us
  waiting for transfers between devices: 491 us -> 102 us
  blocking collectives: 107 us -> 7.61 us
  starting transfers between devices: 1.18 us -> 99.4 us
  local copies, waits for them, and re-layouts: 28.8 us -> 81.5 us
  matrix products: 97.5 us -> 72.3 us
    pallas_call x0 -> x3, Pallas kernels: none -> 464 us  [assemble(): pl.pallas_call(body, out_shape=shapes, in_specs=[pl.BlockSpec(memory_spac...]
    reduce_scatter x6 -> x0, waiting for transfers between devices: 241 us -> none  [the longest x4 179 us: rows_part(): lax.psum_scatter(partial_value.astype(jnp.bfloat16), 'tensor', scatter_di...]
    all_gather x6 -> x0, waiting for transfers between devices: 202 us -> none  [the longest x4 199 us: rows_full(): return lax.all_gather(share, 'tensor', axis=1, tiled=True)]
    ppermute x0 -> x79, waiting for transfers between devices: none -> 102 us  [the longest x24 66.7 us: perm_s(): return lax.ppermute(value, 'shard', [(i, i ^ mask) for i in range(n)])]
    ppermute x0 -> x79, starting transfers between devices: none -> 99.4 us  [the longest x33 73.5 us: perm_t(): lax.ppermute(value, 'tensor', [(i, (i + step) % n) for i in range(n)])]
    all_gather x4 -> x0, blocking collectives: 51.9 us -> none  [the longest x1 27.1 us: on_device(): lax.all_gather(w_qkv, 'shard', axis=0, tiled=True)]
    unnamed x21 -> x2, waiting for transfers between devices: 40.1 us -> 0.03 us
    unnamed x2 -> x0, blocking collectives: 32.3 us -> none
  transfers between devices with their start and end apart: 18 -> 81, of which waited for: 15 -> 29; matrix products, arithmetic and copies ran while one was open for 14% -> 20% of each run, Pallas kernels for 0% -> 51%
where the time goes in v1:
time: 918 us; the launch traced here: 908 us
  Pallas kernels  464 us (51%)
  waiting for transfers between devices  102 us (11%)
  starting transfers between devices  99.4 us (11%)
  local copies, waits for them, and re-layouts  81.5 us (9%)
  matrix products  72.3 us (8%)
  other arithmetic  65.2 us (7%)
  between operations  15.9 us (2%)
    pallas_call x3, Pallas kernels, assemble(): pl.pallas_call(body, out_shape=shapes, in_specs=[pl.BlockSpec(memory_spac...  464 us
    ppermute x33, starting transfers between devices, perm_t(): lax.ppermute(value, 'tensor', [(i, (i + step) % n) for i in range(n)])  73.5 us
    ppermute x24, waiting for transfers between devices, perm_s(): return lax.ppermute(value, 'shard', [(i, i ^ mask) for i in range(n)])  66.7 us
    ppermute x33, waiting for transfers between devices, perm_t(): lax.ppermute(value, 'tensor', [(i, (i + step) % n) for i in range(n)])  35.1 us
    ppermute x24, starting transfers between devices, perm_s(): return lax.ppermute(value, 'shard', [(i, i ^ mask) for i in range(n)])  22.4 us
  transfers between devices with their start and end apart: 81, of which 29 were waited for; matrix products, arithmetic and copies ran while one was open for 20% of the time, Pallas kernels for 51%

profile of v1, /device:TPU:0, one launch (start us, length us, event | category | flops | bytes accessed | tf_op | source)
XLA Modules:
  0.0 908.4 jit_solution(9833411152669070538)
XLA Ops:
  8.8 4.1 concatenate.62
  13.3 5.1 collective-permute-start.9
  20.4 2.9 collective-permute-start.2
  28.6 4.4 collective-permute-start.33
  35.7 8.9 collective-permute-start
  44.7 3.8 collective-permute-start.21
  57.2 9.8 %collective-permute-done.20 = bf16[96,960]{1,0:T(8,128)(2,1)S(1)} collective-permute-done((bf16[96,960]{1,0:T(8,128)(2,1)S(1)}, bf16[96,960]{1,0:T(8,128)(2,1)S(1)}, u32[]{:S(2)}, u32[]{:S(2)}) %collective-permute-start.20) | collective-permute-done | bytes 184352 | tf_op jit(solution)/shard_map/ppermute | solution.py:53
  75.5 8.0 collective-permute-done.34.refs_1_
  87.6 18.1 %collective-permute-done.12.refs_3_ = bf16[2,104,576]{2,1,0:T(8,128)(2,1)} collective-permute-done((bf16[2,104,576]{2,1,0:T(8,128)(2,1)S(1)}, bf16[2,104,576]{2,1,0:T(8,128)(2,1)}, u32[]{:S(2)}, u32[]{:S(2)}) %collective-permute-start.12) | collective-permute-done | bytes 239648 | tf_op jit(solution)/shard_map/ppermute | solution.py:57
  107.2 5.1 collective-permute-done.13.refs_4_
  112.8 3.5 collective-permute-start.6
  116.3 4.1 collective-permute-start.5
  132.4 126.3 %assemble.3 = (bf16[4,768,576]{2,1,0:T(8,128)(2,1)}, bf16[4,4,8,576]{3,2,1,0:T(8,128)(2,1)}) custom-call(s32[2]{0:T(128)} %pad_add_fusion.where_ref, bf16[4,104,576]{2,1,0:T(8,128)(2,1)} %copy-done.23, bf16[4,104,576]{2,1,0:T(8,128)(2,1)} %copy-done.24, bf16[4,104,576]{2,1,0:T(8,128)(2,1)} %copy-done.25, ...), custom_call_target="tpu_custom_call" | custom-call | tf_op jit(solution)/shard_map/assemble/pallas_call | solution.py:162
  262.3 4.7 broadcast_add_fusion
  268.0 3.6 select_reduce_fusion
  271.6 2.7 pmax.7
  274.3 4.5 fusion.116
  278.8 3.6 fusion.17
  285.5 3.9 fusion.18
  289.5 6.4 collective-permute-done.24.refs_3_
  299.9 2.5 psum.29
  307.6 145.0 %assemble.5 = bf16[4,768,768]{2,1,0:T(8,128)(2,1)} custom-call(s32[2]{0:T(128)} %pad_add_fusion.where_ref, bf16[4,96,768]{2,1,0:T(8,128)(2,1)} %pad_maximum_fusion.6.refs_0_, bf16[4,96,768]{2,1,0:T(8,128)(2,1)} %collective-permute-done.34.refs_1_, bf16[4,96,768]{2,1,0:T(8,128)(2,1)} %collective-permute-done.35.refs_2_, ...), custom_call_target="tpu_custom_call" | custom-call | tf_op jit(solution)/shard_map/assemble/pallas_call | solution.py:162
  452.6 3.1 fusion.125
  458.2 192.6 %assemble.4 = bf16[4,768,960]{2,1,0:T(8,128)(2,1)} custom-call(s32[2]{0:T(128)} %pad_add_fusion.where_ref, bf16[4,96,960]{2,1,0:T(8,128)(2,1)} %pad_maximum_fusion.2.refs_0_, bf16[4,96,960]{2,1,0:T(8,128)(2,1)} %collective-permute-done.22.refs_1_, bf16[4,96,960]{2,1,0:T(8,128)(2,1)} %collective-permute-done.23.refs_2_, ...), custom_call_target="tpu_custom_call" | custom-call | tf_op jit(solution)/shard_map/assemble/pallas_call | solution.py:162
  650.9 2.9 slice.382
  653.8 3.1 fusion.126
  657.3 4.8 fusion.52
  662.1 15.0 %fusion.2 = bf16[512,4,768]{2,0,1:T(8,128)(2,1)S(1)} fusion(f32[512,4,768]{2,0,1:T(8,128)S(1)} %get-tuple-element.179, f32[4,768]{1,0:T(4,128)S(1)} %add.385, u8[512,768]{1,0:T(8,128)(4,1)S(1)} %get-tuple-element.75, u8[512,768]{1,0:T(8,128)(4,1)S(1)} %get-tuple-element.74), kind=kLoop, calls=%fused_computation.4 | loop fusion | flops 111673344 | bytes 10235904 | tf_op jit(solution)/shard_map/convert_element_type | solution.py:288
  677.2 2.9 fusion.127
  682.3 2.3 fusion.113
  684.7 4.6 fusion.130
  689.3 4.6 multiply_reduce_fusion
  693.9 4.6 convert_bitcast_fusion
  698.6 4.5 convolution_convert_fusion
  703.9 3.3 collective-permute-start.43
  708.3 2.5 copy.132
  710.8 2.5 fusion.115
  721.7 2.5 psum.31
  725.1 5.7 pad_maximum_fusion
  730.8 8.4 copy.149
  739.1 4.1 dynamic-slice_bitcast_fusion
  743.4 2.8 constant_dynamic-slice_fusion.1
  748.3 2.5 fusion.129
  758.2 5.8 fusion.128
  769.1 4.9 convert_bitcast_fusion.1
  774.0 6.1 copy.139
  784.7 4.4 fusion.46
  789.1 3.8 collective-permute-start.49
  793.1 5.2 collective-permute-done.49
  798.3 9.4 %collective-permute-start.51 = (bf16[128,768]{1,0:T(8,128)(2,1)S(1)}, bf16[128,768]{1,0:T(8,128)(2,1)S(1)}, u32[]{:S(2)}, u32[]{:S(2)}) collective-permute-start(bf16[128,768]{1,0:T(8,128)(2,1)S(1)} %get-tuple-element.128), channel_id=1, source_target_pairs={{0,1},{1,2},{2,3},{3,0},{4,5},{5,6},{6,7},{7,4},{8,9},{9,10},{10,1... | collective-permute-start | bytes 589832 | tf_op jit(solution)/shard_map/ppermute | solution.py:53
  807.7 3.1 collective-permute-done.50
  815.0 2.5 fusion.19
  819.8 2.4 collective-permute-done.53
  824.6 3.9 collective-permute-done.71
  831.5 3.4 fusion.9
  835.0 4.9 collective-permute-done.56
  841.6 2.5 collective-permute-start.59
  844.1 2.4 collective-permute-start.57
  849.4 2.5 collective-permute-done.58
  857.2 2.4 collective-permute-start.75
  871.4 7.8 collective-permute-done.65
  884.1 3.0 collective-permute-start.66
  888.4 4.5 collective-permute-done.68
  892.9 4.8 collective-permute-done.67
  (438 shorter events, 142.5 us)
Async XLA Ops:
  7.2 445.4 %all-reduce.5.cloned.1.call-start = ((), (), s32[]{:S(2)}) async-start(), calls=%async_computation | async-start | bytes 786432 | tf_op jit(solution)/shard_map/psum | solution.py:275
  13.3 22.4 %collective-permute-start.9 = (bf16[104,576]{1,0:T(8,128)(2,1)S(1)}, bf16[104,576]{1,0:T(8,128)(2,1)S(1)}, u32[]{:S(2)}, u32[]{:S(2)}) collective-permute-start(bf16[104,576]{1,0:T(8,128)(2,1)S(1)} %get-tuple-element.163), channel_id=1, source_target_pairs={{0,3},{1,0},{2,1},{3,2},{4,7},{5,4},{6,5},{7,6},{8,11},{9,8},{10,9... | collective-permute-start | bytes 359432 | tf_op jit(solution)/shard_map/ppermute | solution.py:53
  18.5 26.2 %collective-permute-start.8 = (bf16[104,576]{1,0:T(8,128)(2,1)S(1)}, bf16[104,576]{1,0:T(8,128)(2,1)S(1)}, u32[]{:S(2)}, u32[]{:S(2)}) collective-permute-start(bf16[104,576]{1,0:T(8,128)(2,1)S(1)} %get-tuple-element.163), channel_id=1, source_target_pairs={{0,2},{1,3},{2,0},{3,1},{4,6},{5,7},{6,4},{7,5},{8,10},{9,11},{10,... | collective-permute-start | bytes 359432 | tf_op jit(solution)/shard_map/ppermute | solution.py:53
  18.5 26.3 %collective-permute-start.7 = (bf16[104,576]{1,0:T(8,128)(2,1)S(1)}, bf16[104,576]{1,0:T(8,128)(2,1)S(1)}, u32[]{:S(2)}, u32[]{:S(2)}) collective-permute-start(bf16[104,576]{1,0:T(8,128)(2,1)S(1)} %get-tuple-element.163), channel_id=1, source_target_pairs={{0,1},{1,2},{2,3},{3,0},{4,5},{5,6},{6,7},{7,4},{8,9},{9,10},{10,1... | collective-permute-start | bytes 359432 | tf_op jit(solution)/shard_map/ppermute | solution.py:53
  23.3 9.8 %collective-permute-start.1 = (bf16[32,768]{1,0:T(8,128)(2,1)S(1)}, bf16[32,768]{1,0:T(8,128)(2,1)S(1)}, u32[]{:S(2)}, u32[]{:S(2)}) collective-permute-start(bf16[32,768]{1,0:T(8,128)(2,1)S(1)} %constant_dynamic-slice_fusion.5), channel_id=1, source_target_pairs={{0,2},{1,3},{2,0},{3,1},{4,6},{5,7},{6,4},{7,5},{8,10},{9,11},{10,... | collective-permute-start | bytes 147464 | tf_op jit(solution)/shard_map/ppermute | solution.py:53
  28.6 21.8 %collective-permute-start.33 = (bf16[96,768]{1,0:T(8,128)(2,1)S(1)}, bf16[96,768]{1,0:T(8,128)(2,1)S(1)}, u32[]{:S(2)}, u32[]{:S(2)}) collective-permute-start(bf16[96,768]{1,0:T(8,128)(2,1)S(1)} %get-tuple-element.157), channel_id=1, source_target_pairs={{0,3},{1,0},{2,1},{3,2},{4,7},{5,4},{6,5},{7,6},{8,11},{9,8},{10,9... | collective-permute-start | bytes 442376 | tf_op jit(solution)/shard_map/ppermute | solution.py:53
  33.1 17.3 %collective-permute-start.32 = (bf16[96,768]{1,0:T(8,128)(2,1)S(1)}, bf16[96,768]{1,0:T(8,128)(2,1)S(1)}, u32[]{:S(2)}, u32[]{:S(2)}) collective-permute-start(bf16[96,768]{1,0:T(8,128)(2,1)S(1)} %get-tuple-element.157), channel_id=1, source_target_pairs={{0,2},{1,3},{2,0},{3,1},{4,6},{5,7},{6,4},{7,5},{8,10},{9,11},{10,... | collective-permute-start | bytes 442376 | tf_op jit(solution)/shard_map/ppermute | solution.py:53
  35.7 12.9 %collective-permute-start = (bf16[32,768]{1,0:T(8,128)(2,1)S(1)}, bf16[32,768]{1,0:T(8,128)(2,1)S(1)}, u32[]{:S(2)}, u32[]{:S(2)}) collective-permute-start(bf16[32,768]{1,0:T(8,128)(2,1)S(1)} %constant_dynamic-slice_fusion.5), channel_id=1, source_target_pairs={{0,1},{1,2},{2,3},{3,0},{4,5},{5,6},{6,7},{7,4},{8,9},{9,10},{10,1... | collective-permute-start | bytes 147464 | tf_op jit(solution)/shard_map/ppermute | solution.py:53
  48.7 18.3 %collective-permute-start.20 = (bf16[96,960]{1,0:T(8,128)(2,1)S(1)}, bf16[96,960]{1,0:T(8,128)(2,1)S(1)}, u32[]{:S(2)}, u32[]{:S(2)}) collective-permute-start(bf16[96,960]{1,0:T(8,128)(2,1)S(1)} %get-tuple-element.161), channel_id=1, source_target_pairs={{0,2},{1,3},{2,0},{3,1},{4,6},{5,7},{6,4},{7,5},{8,10},{9,11},{10,... | collective-permute-start | bytes 552968 | tf_op jit(solution)/shard_map/ppermute | solution.py:53
  50.4 18.1 %collective-permute-start.19 = (bf16[96,960]{1,0:T(8,128)(2,1)S(1)}, bf16[96,960]{1,0:T(8,128)(2,1)S(1)}, u32[]{:S(2)}, u32[]{:S(2)}) collective-permute-start(bf16[96,960]{1,0:T(8,128)(2,1)S(1)} %get-tuple-element.161), channel_id=1, source_target_pairs={{0,1},{1,2},{2,3},{3,0},{4,5},{5,6},{6,7},{7,4},{8,9},{9,10},{10,1... | collective-permute-start | bytes 552968 | tf_op jit(solution)/shard_map/ppermute | solution.py:53
  50.4 20.7 %collective-permute-start.10 = (bf16[4,104,576]{2,1,0:T(8,128)(2,1)S(1)}, bf16[4,104,576]{2,1,0:T(8,128)(2,1)S(1)}, u32[]{:S(2)}, u32[]{:S(2)}) collective-permute-start(bf16[4,104,576]{2,1,0:T(8,128)(2,1)S(1)} %pad_maximum_fusion.9.refs_0_), channel_id=1, source_target_pairs={{0,8},{8,0},{16,24},{24,16},{1,9},{9,1},{17,25},{25,17},{2,10},{10... | collective-permute-start | bytes 1437704 | tf_op jit(solution)/shard_map/ppermute | solution.py:57
  53.3 16.7 %collective-permute-start.3 = (bf16[4,32,768]{2,1,0:T(8,128)(2,1)S(1)}, bf16[4,32,768]{2,1,0:T(8,128)(2,1)S(1)}, u32[]{:S(2)}, u32[]{:S(2)}) collective-permute-start(bf16[4,32,768]{2,1,0:T(8,128)(2,1)S(1)} %pad_maximum_fusion.15), channel_id=1, source_target_pairs={{0,4},{4,0},{1,5},{5,1},{2,6},{6,2},{3,7},{7,3},{8,12},{12,8},{9,1... | collective-permute-start | bytes 589832 | tf_op jit(solution)/shard_map/ppermute | solution.py:61
  53.8 18.5 %collective-permute-start.11 = (bf16[4,104,576]{2,1,0:T(8,128)(2,1)S(1)}, bf16[4,104,576]{2,1,0:T(8,128)(2,1)S(1)}, u32[]{:S(2)}, u32[]{:S(2)}) collective-permute-start(bf16[4,104,576]{2,1,0:T(8,128)(2,1)S(1)} %pad_maximum_fusion.9.refs_0_), channel_id=1, source_target_pairs={{0,16},{8,24},{16,0},{24,8},{1,17},{9,25},{17,1},{25,9},{2,18},{10... | collective-permute-start | bytes 1437704 | tf_op jit(solution)/shard_map/ppermute | solution.py:57
  66.9 16.5 %collective-permute-start.34 = (bf16[4,96,768]{2,1,0:T(8,128)(2,1)}, bf16[4,96,768]{2,1,0:T(8,128)(2,1)}, u32[]{:S(2)}, u32[]{:S(2)}) collective-permute-start(bf16[4,96,768]{2,1,0:T(8,128)(2,1)} %pad_maximum_fusion.6.refs_0_), channel_id=1, source_target_pairs={{0,8},{8,0},{16,24},{24,16},{1,9},{9,1},{17,25},{25,17},{2,10},{10... | collective-permute-start | bytes 1769480 | tf_op jit(solution)/shard_map/ppermute | solution.py:57
  68.4 16.5 %collective-permute-start.35 = (bf16[4,96,768]{2,1,0:T(8,128)(2,1)}, bf16[4,96,768]{2,1,0:T(8,128)(2,1)}, u32[]{:S(2)}, u32[]{:S(2)}) collective-permute-start(bf16[4,96,768]{2,1,0:T(8,128)(2,1)} %pad_maximum_fusion.6.refs_0_), channel_id=1, source_target_pairs={{0,16},{8,24},{16,0},{24,8},{1,17},{9,25},{17,1},{25,9},{2,18},{10... | collective-permute-start | bytes 1769480 | tf_op jit(solution)/shard_map/ppermute | solution.py:57
  71.1 41.2 %collective-permute-start.22 = (bf16[4,96,960]{2,1,0:T(8,128)(2,1)}, bf16[4,96,960]{2,1,0:T(8,128)(2,1)}, u32[]{:S(2)}, u32[]{:S(2)}) collective-permute-start(bf16[4,96,960]{2,1,0:T(8,128)(2,1)} %pad_maximum_fusion.2.refs_0_), channel_id=1, source_target_pairs={{0,8},{8,0},{16,24},{24,16},{1,9},{9,1},{17,25},{25,17},{2,10},{10... | collective-permute-start | bytes 2211848 | tf_op jit(solution)/shard_map/ppermute | solution.py:57
  72.4 40.4 %collective-permute-start.23 = (bf16[4,96,960]{2,1,0:T(8,128)(2,1)}, bf16[4,96,960]{2,1,0:T(8,128)(2,1)}, u32[]{:S(2)}, u32[]{:S(2)}) collective-permute-start(bf16[4,96,960]{2,1,0:T(8,128)(2,1)} %pad_maximum_fusion.2.refs_0_), channel_id=1, source_target_pairs={{0,16},{8,24},{16,0},{24,8},{1,17},{9,25},{17,1},{25,9},{2,18},{10... | collective-permute-start | bytes 2211848 | tf_op jit(solution)/shard_map/ppermute | solution.py:57
  73.9 31.8 %collective-permute-start.12 = (bf16[2,104,576]{2,1,0:T(8,128)(2,1)S(1)}, bf16[2,104,576]{2,1,0:T(8,128)(2,1)}, u32[]{:S(2)}, u32[]{:S(2)}) collective-permute-start(bf16[2,104,576]{2,1,0:T(8,128)(2,1)S(1)} %slice.374), channel_id=1, source_target_pairs={{0,16},{8,24},{16,0},{24,8},{1,17},{9,25},{17,1},{25,9},{2,18},{10... | collective-permute-start | bytes 718856 | tf_op jit(solution)/shard_map/ppermute | solution.py:57
  83.5 32.9 %collective-permute-start.15 = (bf16[4,104,576]{2,1,0:T(8,128)(2,1)S(1)}, bf16[4,104,576]{2,1,0:T(8,128)(2,1)S(1)}, u32[]{:S(2)}, u32[]{:S(2)}) collective-permute-start(bf16[4,104,576]{2,1,0:T(8,128)(2,1)S(1)} %collective-permute-done.10.refs_1_), channel_id=1, source_target_pairs={{0,4},{4,0},{1,5},{5,1},{2,6},{6,2},{3,7},{7,3},{8,12},{12,8},{9,1... | collective-permute-start | bytes 1437704 | tf_op jit(solution)/shard_map/ppermute | solution.py:61
  84.9 35.4 %collective-permute-start.16 = (bf16[4,104,576]{2,1,0:T(8,128)(2,1)S(1)}, bf16[4,104,576]{2,1,0:T(8,128)(2,1)S(1)}, u32[]{:S(2)}, u32[]{:S(2)}) collective-permute-start(bf16[4,104,576]{2,1,0:T(8,128)(2,1)S(1)} %collective-permute-done.11.refs_2_), channel_id=1, source_target_pairs={{0,4},{4,0},{1,5},{5,1},{2,6},{6,2},{3,7},{7,3},{8,12},{12,8},{9,1... | collective-permute-start | bytes 1437704 | tf_op jit(solution)/shard_map/ppermute | solution.py:61
  112.3 17.2 %collective-permute-start.17 = (bf16[2,104,576]{2,1,0:T(8,128)(2,1)}, bf16[2,104,576]{2,1,0:T(8,128)(2,1)S(1)}, u32[]{:S(2)}, u32[]{:S(2)}) collective-permute-start(bf16[2,104,576]{2,1,0:T(8,128)(2,1)} %collective-permute-done.12.refs_3_), channel_id=1, source_target_pairs={{0,4},{4,0},{1,5},{5,1},{2,6},{6,2},{3,7},{7,3},{8,12},{12,8},{9,1... | collective-permute-start | bytes 718856 | tf_op jit(solution)/shard_map/ppermute | solution.py:61
  112.3 17.2 %collective-permute-start.18 = (bf16[2,104,576]{2,1,0:T(8,128)(2,1)S(1)}, bf16[2,104,576]{2,1,0:T(8,128)(2,1)S(1)}, u32[]{:S(2)}, u32[]{:S(2)}) collective-permute-start(bf16[2,104,576]{2,1,0:T(8,128)(2,1)S(1)} %collective-permute-done.13.refs_4_), channel_id=1, source_target_pairs={{0,4},{4,0},{1,5},{5,1},{2,6},{6,2},{3,7},{7,3},{8,12},{12,8},{9,1... | collective-permute-start | bytes 718856 | tf_op jit(solution)/shard_map/ppermute | solution.py:61
  112.8 147.3 %collective-permute-start.6 = (bf16[128,768]{1,0:T(8,128)(2,1)}, bf16[128,768]{1,0:T(8,128)(2,1)}, u32[]{:S(2)}, u32[]{:S(2)}) collective-permute-start(bf16[128,768]{1,0:T(8,128)(2,1)} %get-tuple-element.140), channel_id=1, source_target_pairs={{0,3},{1,0},{2,1},{3,2},{4,7},{5,4},{6,5},{7,6},{8,11},{9,8},{10,9... | collective-permute-start | bytes 589832 | tf_op jit(solution)/shard_map/ppermute | solution.py:53
  116.3 145.4 %collective-permute-start.5 = (bf16[128,768]{1,0:T(8,128)(2,1)}, bf16[128,768]{1,0:T(8,128)(2,1)}, u32[]{:S(2)}, u32[]{:S(2)}) collective-permute-start(bf16[128,768]{1,0:T(8,128)(2,1)} %get-tuple-element.141), channel_id=1, source_target_pairs={{0,2},{1,3},{2,0},{3,1},{4,6},{5,7},{6,4},{7,5},{8,10},{9,11},{10,... | collective-permute-start | bytes 589832 | tf_op jit(solution)/shard_map/ppermute | solution.py:53
  120.4 141.4 %collective-permute-start.4 = (bf16[128,768]{1,0:T(8,128)(2,1)}, bf16[128,768]{1,0:T(8,128)(2,1)}, u32[]{:S(2)}, u32[]{:S(2)}) collective-permute-start(bf16[128,768]{1,0:T(8,128)(2,1)} %get-tuple-element.139), channel_id=1, source_target_pairs={{0,1},{1,2},{2,3},{3,0},{4,5},{5,6},{6,7},{7,4},{8,9},{9,10},{10,1... | collective-permute-start | bytes 589832 | tf_op jit(solution)/shard_map/ppermute | solution.py:53
  129.5 154.9 %collective-permute-start.38 = (bf16[4,96,768]{2,1,0:T(8,128)(2,1)}, bf16[4,96,768]{2,1,0:T(8,128)(2,1)}, u32[]{:S(2)}, u32[]{:S(2)}) collective-permute-start(bf16[4,96,768]{2,1,0:T(8,128)(2,1)} %pad_maximum_fusion.6.refs_0_), channel_id=1, source_target_pairs={{0,4},{4,0},{1,5},{5,1},{2,6},{6,2},{3,7},{7,3},{8,12},{12,8},{9,1... | collective-permute-start | bytes 1769480 | tf_op jit(solution)/shard_map/ppermute | solution.py:61
  130.9 154.1 %collective-permute-start.36 = (bf16[2,96,768]{2,1,0:T(8,128)(2,1)}, bf16[2,96,768]{2,1,0:T(8,128)(2,1)}, u32[]{:S(2)}, u32[]{:S(2)}) collective-permute-start(bf16[2,96,768]{2,1,0:T(8,128)(2,1)} %slice.386), channel_id=1, source_target_pairs={{0,16},{8,24},{16,0},{24,8},{1,17},{9,25},{17,1},{25,9},{2,18},{10... | collective-permute-start | bytes 884744 | tf_op jit(solution)/shard_map/ppermute | solution.py:57
  260.2 29.3 %collective-permute-start.37 = (bf16[2,96,768]{2,1,0:T(8,128)(2,1)}, bf16[2,96,768]{2,1,0:T(8,128)(2,1)}, u32[]{:S(2)}, u32[]{:S(2)}) collective-permute-start(bf16[2,96,768]{2,1,0:T(8,128)(2,1)} %slice.387), channel_id=1, source_target_pairs={{0,8},{8,0},{16,24},{24,16},{1,9},{9,1},{17,25},{25,17},{2,10},{10... | collective-permute-start | bytes 884744 | tf_op jit(solution)/shard_map/ppermute | solution.py:57
  261.8 41.2 %collective-permute-start.39 = (bf16[4,96,768]{2,1,0:T(8,128)(2,1)}, bf16[4,96,768]{2,1,0:T(8,128)(2,1)}, u32[]{:S(2)}, u32[]{:S(2)}) collective-permute-start(bf16[4,96,768]{2,1,0:T(8,128)(2,1)} %collective-permute-done.34.refs_1_), channel_id=1, source_target_pairs={{0,4},{4,0},{1,5},{5,1},{2,6},{6,2},{3,7},{7,3},{8,12},{12,8},{9,1... | collective-permute-start | bytes 1769480 | tf_op jit(solution)/shard_map/ppermute | solution.py:61
  261.8 41.5 %collective-permute-start.40 = (bf16[4,96,768]{2,1,0:T(8,128)(2,1)}, bf16[4,96,768]{2,1,0:T(8,128)(2,1)}, u32[]{:S(2)}, u32[]{:S(2)}) collective-permute-start(bf16[4,96,768]{2,1,0:T(8,128)(2,1)} %collective-permute-done.35.refs_2_), channel_id=1, source_target_pairs={{0,4},{4,0},{1,5},{5,1},{2,6},{6,2},{3,7},{7,3},{8,12},{12,8},{9,1... | collective-permute-start | bytes 1769480 | tf_op jit(solution)/shard_map/ppermute | solution.py:61
  284.3 473.8 %all-reduce.7.cloned.1.call-start = ((), (), s32[]{:S(2)}) async-start(), calls=%async_computation.1 | async-start | bytes 786432 | tf_op jit(solution)/shard_map/psum | solution.py:321
  284.4 11.6 %collective-permute-start.24 = (bf16[2,96,960]{2,1,0:T(8,128)(2,1)}, bf16[2,96,960]{2,1,0:T(8,128)(2,1)}, u32[]{:S(2)}, u32[]{:S(2)}) collective-permute-start(bf16[2,96,960]{2,1,0:T(8,128)(2,1)} %slice.380), channel_id=1, source_target_pairs={{0,16},{8,24},{16,0},{24,8},{1,17},{9,25},{17,1},{25,9},{2,18},{10... | collective-permute-start | bytes 1105928 | tf_op jit(solution)/shard_map/ppermute | solution.py:57
  285.0 11.2 %collective-permute-start.25 = (bf16[2,96,960]{2,1,0:T(8,128)(2,1)}, bf16[2,96,960]{2,1,0:T(8,128)(2,1)}, u32[]{:S(2)}, u32[]{:S(2)}) collective-permute-start(bf16[2,96,960]{2,1,0:T(8,128)(2,1)} %slice.381), channel_id=1, source_target_pairs={{0,8},{8,0},{16,24},{24,16},{1,9},{9,1},{17,25},{25,17},{2,10},{10... | collective-permute-start | bytes 1105928 | tf_op jit(solution)/shard_map/ppermute | solution.py:57
  289.5 166.2 %collective-permute-start.26 = (bf16[4,96,960]{2,1,0:T(8,128)(2,1)}, bf16[4,96,960]{2,1,0:T(8,128)(2,1)}, u32[]{:S(2)}, u32[]{:S(2)}) collective-permute-start(bf16[4,96,960]{2,1,0:T(8,128)(2,1)} %pad_maximum_fusion.2.refs_0_), channel_id=1, source_target_pairs={{0,4},{4,0},{1,5},{5,1},{2,6},{6,2},{3,7},{7,3},{8,12},{12,8},{9,1... | collective-permute-start | bytes 2211848 | tf_op jit(solution)/shard_map/ppermute | solution.py:61
  296.0 161.6 %collective-permute-start.27 = (bf16[4,96,960]{2,1,0:T(8,128)(2,1)}, bf16[4,96,960]{2,1,0:T(8,128)(2,1)}, u32[]{:S(2)}, u32[]{:S(2)}) collective-permute-start(bf16[4,96,960]{2,1,0:T(8,128)(2,1)} %collective-permute-done.22.refs_1_), channel_id=1, source_target_pairs={{0,4},{4,0},{1,5},{5,1},{2,6},{6,2},{3,7},{7,3},{8,12},{12,8},{9,1... | collective-permute-start | bytes 2211848 | tf_op jit(solution)/shard_map/ppermute | solution.py:61
  296.2 161.4 %collective-permute-start.28 = (bf16[4,96,960]{2,1,0:T(8,128)(2,1)}, bf16[4,96,960]{2,1,0:T(8,128)(2,1)}, u32[]{:S(2)}, u32[]{:S(2)}) collective-permute-start(bf16[4,96,960]{2,1,0:T(8,128)(2,1)} %collective-permute-done.23.refs_2_), channel_id=1, source_target_pairs={{0,4},{4,0},{1,5},{5,1},{2,6},{6,2},{3,7},{7,3},{8,12},{12,8},{9,1... | collective-permute-start | bytes 2211848 | tf_op jit(solution)/shard_map/ppermute | solution.py:61
  307.1 151.2 %collective-permute-start.29 = (bf16[2,96,960]{2,1,0:T(8,128)(2,1)}, bf16[2,96,960]{2,1,0:T(8,128)(2,1)}, u32[]{:S(2)}, u32[]{:S(2)}) collective-permute-start(bf16[2,96,960]{2,1,0:T(8,128)(2,1)} %collective-permute-done.24.refs_3_), channel_id=1, source_target_pairs={{0,4},{4,0},{1,5},{5,1},{2,6},{6,2},{3,7},{7,3},{8,12},{12,8},{9,1... | collective-permute-start | bytes 1105928 | tf_op jit(solution)/shard_map/ppermute | solution.py:61
  307.3 150.9 %collective-permute-start.30 = (bf16[2,96,960]{2,1,0:T(8,128)(2,1)}, bf16[2,96,960]{2,1,0:T(8,128)(2,1)}, u32[]{:S(2)}, u32[]{:S(2)}) collective-permute-start(bf16[2,96,960]{2,1,0:T(8,128)(2,1)} %collective-permute-done.25.refs_4_), channel_id=1, source_target_pairs={{0,4},{4,0},{1,5},{5,1},{2,6},{6,2},{3,7},{7,3},{8,12},{12,8},{9,1... | collective-permute-start | bytes 1105928 | tf_op jit(solution)/shard_map/ppermute | solution.py:61
  455.7 224.7 %collective-permute-start.48 = (bf16[128,768]{1,0:T(8,128)(2,1)}, bf16[128,768]{1,0:T(8,128)(2,1)}, u32[]{:S(2)}, u32[]{:S(2)}) collective-permute-start(bf16[128,768]{1,0:T(8,128)(2,1)} %get-tuple-element.133), channel_id=1, source_target_pairs={{0,3},{1,0},{2,1},{3,2},{4,7},{5,4},{6,5},{7,6},{8,11},{9,8},{10,9... | collective-permute-start | bytes 589832 | tf_op jit(solution)/shard_map/ppermute | solution.py:53
  457.6 222.8 %collective-permute-start.47 = (bf16[128,768]{1,0:T(8,128)(2,1)}, bf16[128,768]{1,0:T(8,128)(2,1)}, u32[]{:S(2)}, u32[]{:S(2)}) collective-permute-start(bf16[128,768]{1,0:T(8,128)(2,1)} %get-tuple-element.134), channel_id=1, source_target_pairs={{0,2},{1,3},{2,0},{3,1},{4,6},{5,7},{6,4},{7,5},{8,10},{9,11},{10,... | collective-permute-start | bytes 589832 | tf_op jit(solution)/shard_map/ppermute | solution.py:53
  457.6 222.8 %collective-permute-start.46 = (bf16[128,768]{1,0:T(8,128)(2,1)}, bf16[128,768]{1,0:T(8,128)(2,1)}, u32[]{:S(2)}, u32[]{:S(2)}) collective-permute-start(bf16[128,768]{1,0:T(8,128)(2,1)} %get-tuple-element.132), channel_id=1, source_target_pairs={{0,1},{1,2},{2,3},{3,0},{4,5},{5,6},{6,7},{7,4},{8,9},{9,10},{10,1... | collective-permute-start | bytes 589832 | tf_op jit(solution)/shard_map/ppermute | solution.py:53
  703.9 51.0 %collective-permute-start.43 = (bf16[128,768]{1,0:T(8,128)(2,1)}, bf16[128,768]{1,0:T(8,128)(2,1)}, u32[]{:S(2)}, u32[]{:S(2)}) collective-permute-start(bf16[128,768]{1,0:T(8,128)(2,1)} %get-tuple-element.137), channel_id=1, source_target_pairs={{0,3},{1,0},{2,1},{3,2},{4,7},{5,4},{6,5},{7,6},{8,11},{9,8},{10,9... | collective-permute-start | bytes 589832 | tf_op jit(solution)/shard_map/ppermute | solution.py:53
  707.1 49.4 %collective-permute-start.44 = (bf16[128,768]{1,0:T(8,128)(2,1)S(1)}, bf16[128,768]{1,0:T(8,128)(2,1)}, u32[]{:S(2)}, u32[]{:S(2)}) collective-permute-start(bf16[128,768]{1,0:T(8,128)(2,1)S(1)} %get-tuple-element.136), channel_id=1, source_target_pairs={{0,2},{1,3},{2,0},{3,1},{4,6},{5,7},{6,4},{7,5},{8,10},{9,11},{10,... | collective-permute-start | bytes 589832 | tf_op jit(solution)/shard_map/ppermute | solution.py:53
  708.2 74.9 %collective-permute-start.45 = (bf16[128,768]{1,0:T(8,128)(2,1)}, bf16[128,768]{1,0:T(8,128)(2,1)}, u32[]{:S(2)}, u32[]{:S(2)}) collective-permute-start(bf16[128,768]{1,0:T(8,128)(2,1)} %get-tuple-element.135), channel_id=1, source_target_pairs={{0,1},{1,2},{2,3},{3,0},{4,5},{5,6},{6,7},{7,4},{8,9},{9,10},{10,1... | collective-permute-start | bytes 589832 | tf_op jit(solution)/shard_map/ppermute | solution.py:53
  743.2 88.3 %collective-permute-start.61 = (bf16[4,4,96,960]{3,2,1,0:T(8,128)(2,1)}, bf16[4,4,96,960]{3,2,1,0:T(8,128)(2,1)}, u32[]{:S(2)}, u32[]{:S(2)}) collective-permute-start(bf16[4,4,96,960]{3,2,1,0:T(8,128)(2,1)} %dynamic-slice_bitcast_fusion), channel_id=1, source_target_pairs={{0,4},{4,0},{1,5},{5,1},{2,6},{6,2},{3,7},{7,3},{8,12},{12,8},{9,1... | collective-permute-start | bytes 8847368 | tf_op jit(solution)/shard_map/ppermute | solution.py:61
  747.9 67.1 %collective-permute-start.70 = (bf16[4,4,96,768]{3,2,0,1:T(8,128)(2,1)}, bf16[4,4,96,768]{3,2,0,1:T(8,128)(2,1)}, u32[]{:S(2)}, u32[]{:S(2)}) collective-permute-start(bf16[4,4,96,768]{3,2,0,1:T(8,128)(2,1)} %bitcast.381), channel_id=1, source_target_pairs={{0,4},{4,0},{1,5},{5,1},{2,6},{6,2},{3,7},{7,3},{8,12},{12,8},{9,1... | collective-permute-start | bytes 7077896 | tf_op jit(solution)/shard_map/ppermute | solution.py:61
  782.8 29.4 %collective-permute-start.52 = (bf16[4,4,104,576]{3,2,1,0:T(8,128)(2,1)S(1)}, bf16[4,4,104,576]{3,2,1,0:T(8,128)(2,1)S(1)}, u32[]{:S(2)}, u32[]{:S(2)}) collective-permute-start(bf16[4,4,104,576]{3,2,1,0:T(8,128)(2,1)S(1)} %fusion.34), channel_id=1, source_target_pairs={{0,4},{4,0},{1,5},{5,1},{2,6},{6,2},{3,7},{7,3},{8,12},{12,8},{9,1... | collective-permute-start | bytes 5750792 | tf_op jit(solution)/shard_map/ppermute | solution.py:61
  793.0 17.8 %collective-permute-start.50 = (bf16[128,768]{1,0:T(8,128)(2,1)S(1)}, bf16[128,768]{1,0:T(8,128)(2,1)S(1)}, u32[]{:S(2)}, u32[]{:S(2)}) collective-permute-start(bf16[128,768]{1,0:T(8,128)(2,1)S(1)} %get-tuple-element.129), channel_id=1, source_target_pairs={{0,2},{1,3},{2,0},{3,1},{4,6},{5,7},{6,4},{7,5},{8,10},{9,11},{10,... | collective-permute-start | bytes 589832 | tf_op jit(solution)/shard_map/ppermute | solution.py:53
  798.3 12.6 %collective-permute-start.51 = (bf16[128,768]{1,0:T(8,128)(2,1)S(1)}, bf16[128,768]{1,0:T(8,128)(2,1)S(1)}, u32[]{:S(2)}, u32[]{:S(2)}) collective-permute-start(bf16[128,768]{1,0:T(8,128)(2,1)S(1)} %get-tuple-element.128), channel_id=1, source_target_pairs={{0,1},{1,2},{2,3},{3,0},{4,5},{5,6},{6,7},{7,4},{8,9},{9,10},{10,1... | collective-permute-start | bytes 589832 | tf_op jit(solution)/shard_map/ppermute | solution.py:53
  817.6 10.9 %collective-permute-start.71 = (bf16[2,96,768]{2,1,0:T(8,128)(2,1)S(1)}, bf16[2,96,768]{2,1,0:T(8,128)(2,1)S(1)}, u32[]{:S(2)}, u32[]{:S(2)}) collective-permute-start(bf16[2,96,768]{2,1,0:T(8,128)(2,1)S(1)} %get-tuple-element.114), channel_id=1, source_target_pairs={{0,16},{8,24},{16,0},{24,8},{1,17},{9,25},{17,1},{25,9},{2,18},{10... | collective-permute-start | bytes 884744 | tf_op jit(solution)/shard_map/ppermute | solution.py:57
  818.2 11.7 %collective-permute-start.73 = (bf16[2,96,768]{2,1,0:T(8,128)(2,1)S(1)}, bf16[2,96,768]{2,1,0:T(8,128)(2,1)S(1)}, u32[]{:S(2)}, u32[]{:S(2)}) collective-permute-start(bf16[2,96,768]{2,1,0:T(8,128)(2,1)S(1)} %get-tuple-element.116), channel_id=1, source_target_pairs={{0,8},{8,0},{16,24},{24,16},{1,9},{9,1},{17,25},{25,17},{2,10},{10... | collective-permute-start | bytes 884744 | tf_op jit(solution)/shard_map/ppermute | solution.py:57
  823.8 16.1 %collective-permute-start.56 = (bf16[4,104,576]{2,1,0:T(8,128)(2,1)S(1)}, bf16[4,104,576]{2,1,0:T(8,128)(2,1)S(1)}, u32[]{:S(2)}, u32[]{:S(2)}) collective-permute-start(bf16[4,104,576]{2,1,0:T(8,128)(2,1)S(1)} %pad_maximum_fusion.11), channel_id=1, source_target_pairs={{0,16},{8,24},{16,0},{24,8},{1,17},{9,25},{17,1},{25,9},{2,18},{10... | collective-permute-start | bytes 1437704 | tf_op jit(solution)/shard_map/ppermute | solution.py:57
  824.5 16.8 %collective-permute-start.54 = (bf16[4,104,576]{2,1,0:T(8,128)(2,1)S(1)}, bf16[4,104,576]{2,1,0:T(8,128)(2,1)S(1)}, u32[]{:S(2)}, u32[]{:S(2)}) collective-permute-start(bf16[4,104,576]{2,1,0:T(8,128)(2,1)S(1)} %pad_maximum_fusion.10), channel_id=1, source_target_pairs={{0,8},{8,0},{16,24},{24,16},{1,9},{9,1},{17,25},{25,17},{2,10},{10... | collective-permute-start | bytes 1437704 | tf_op jit(solution)/shard_map/ppermute | solution.py:57
  830.1 22.8 %collective-permute-start.74 = (bf16[4,96,768]{2,1,0:T(8,128)(2,1)S(1)}, bf16[4,96,768]{2,1,0:T(8,128)(2,1)S(1)}, u32[]{:S(2)}, u32[]{:S(2)}) collective-permute-start(bf16[4,96,768]{2,1,0:T(8,128)(2,1)S(1)} %pad_maximum_fusion.8), channel_id=1, source_target_pairs={{0,16},{8,24},{16,0},{24,8},{1,17},{9,25},{17,1},{25,9},{2,18},{10... | collective-permute-start | bytes 1769480 | tf_op jit(solution)/shard_map/ppermute | solution.py:57
  830.8 23.2 %collective-permute-start.72 = (bf16[4,96,768]{2,1,0:T(8,128)(2,1)S(1)}, bf16[4,96,768]{2,1,0:T(8,128)(2,1)S(1)}, u32[]{:S(2)}, u32[]{:S(2)}) collective-permute-start(bf16[4,96,768]{2,1,0:T(8,128)(2,1)S(1)} %pad_maximum_fusion.7), channel_id=1, source_target_pairs={{0,8},{8,0},{16,24},{24,16},{1,9},{9,1},{17,25},{25,17},{2,10},{10... | collective-permute-start | bytes 1769480 | tf_op jit(solution)/shard_map/ppermute | solution.py:57
  848.7 11.0 %collective-permute-start.62 = (bf16[2,96,960]{2,1,0:T(8,128)(2,1)S(1)}, bf16[2,96,960]{2,1,0:T(8,128)(2,1)S(1)}, u32[]{:S(2)}, u32[]{:S(2)}) collective-permute-start(bf16[2,96,960]{2,1,0:T(8,128)(2,1)S(1)} %get-tuple-element.109), channel_id=1, source_target_pairs={{0,16},{8,24},{16,0},{24,8},{1,17},{9,25},{17,1},{25,9},{2,18},{10... | collective-permute-start | bytes 1105928 | tf_op jit(solution)/shard_map/ppermute | solution.py:57
  855.0 29.1 %collective-permute-start.77 = (bf16[96,768]{1,0:T(8,128)(2,1)}, bf16[96,768]{1,0:T(8,128)(2,1)}, u32[]{:S(2)}, u32[]{:S(2)}) collective-permute-start(bf16[96,768]{1,0:T(8,128)(2,1)} %get-tuple-element.143), channel_id=1, source_target_pairs={{0,1},{1,2},{2,3},{3,0},{4,5},{5,6},{6,7},{7,4},{8,9},{9,10},{10,1... | collective-permute-start | bytes 442376 | tf_op jit(solution)/shard_map/ppermute | solution.py:53
  856.1 31.0 %collective-permute-start.76 = (bf16[96,768]{1,0:T(8,128)(2,1)}, bf16[96,768]{1,0:T(8,128)(2,1)}, u32[]{:S(2)}, u32[]{:S(2)}) collective-permute-start(bf16[96,768]{1,0:T(8,128)(2,1)} %get-tuple-element.144), channel_id=1, source_target_pairs={{0,2},{1,3},{2,0},{3,1},{4,6},{5,7},{6,4},{7,5},{8,10},{9,11},{10,... | collective-permute-start | bytes 442376 | tf_op jit(solution)/shard_map/ppermute | solution.py:53
  857.2 29.9 %collective-permute-start.75 = (bf16[96,768]{1,0:T(8,128)(2,1)}, bf16[96,768]{1,0:T(8,128)(2,1)}, u32[]{:S(2)}, u32[]{:S(2)}) collective-permute-start(bf16[96,768]{1,0:T(8,128)(2,1)} %get-tuple-element.142), channel_id=1, source_target_pairs={{0,3},{1,0},{2,1},{3,2},{4,7},{5,4},{6,5},{7,6},{8,11},{9,8},{10,9... | collective-permute-start | bytes 442376 | tf_op jit(solution)/shard_map/ppermute | solution.py:53
  862.0 17.3 %collective-permute-start.65 = (bf16[4,96,960]{2,1,0:T(8,128)(2,1)}, bf16[4,96,960]{2,1,0:T(8,128)(2,1)}, u32[]{:S(2)}, u32[]{:S(2)}) collective-permute-start(bf16[4,96,960]{2,1,0:T(8,128)(2,1)} %pad_maximum_fusion.5), channel_id=1, source_target_pairs={{0,16},{8,24},{16,0},{24,8},{1,17},{9,25},{17,1},{25,9},{2,18},{10... | collective-permute-start | bytes 2211848 | tf_op jit(solution)/shard_map/ppermute | solution.py:57
  863.5 17.8 %collective-permute-start.63 = (bf16[4,96,960]{2,1,0:T(8,128)(2,1)}, bf16[4,96,960]{2,1,0:T(8,128)(2,1)}, u32[]{:S(2)}, u32[]{:S(2)}) collective-permute-start(bf16[4,96,960]{2,1,0:T(8,128)(2,1)} %pad_maximum_fusion.4), channel_id=1, source_target_pairs={{0,8},{8,0},{16,24},{24,16},{1,9},{9,1},{17,25},{25,17},{2,10},{10... | collective-permute-start | bytes 2211848 | tf_op jit(solution)/shard_map/ppermute | solution.py:57
  883.2 9.7 %collective-permute-start.68 = (bf16[96,960]{1,0:T(8,128)(2,1)S(1)}, bf16[96,960]{1,0:T(8,128)(2,1)S(1)}, u32[]{:S(2)}, u32[]{:S(2)}) collective-permute-start(bf16[96,960]{1,0:T(8,128)(2,1)S(1)} %get-tuple-element.125), channel_id=1, source_target_pairs={{0,1},{1,2},{2,3},{3,0},{4,5},{5,6},{6,7},{7,4},{8,9},{9,10},{10,1... | collective-permute-start | bytes 552968 | tf_op jit(solution)/shard_map/ppermute | solution.py:53
  883.3 14.4 %collective-permute-start.67 = (bf16[96,960]{1,0:T(8,128)(2,1)S(1)}, bf16[96,960]{1,0:T(8,128)(2,1)S(1)}, u32[]{:S(2)}, u32[]{:S(2)}) collective-permute-start(bf16[96,960]{1,0:T(8,128)(2,1)S(1)} %get-tuple-element.126), channel_id=1, source_target_pairs={{0,2},{1,3},{2,0},{3,1},{4,6},{5,7},{6,4},{7,5},{8,10},{9,11},{10,... | collective-permute-start | bytes 552968 | tf_op jit(solution)/shard_map/ppermute | solution.py:53
  884.1 13.6 %collective-permute-start.66 = (bf16[96,960]{1,0:T(8,128)(2,1)S(1)}, bf16[96,960]{1,0:T(8,128)(2,1)S(1)}, u32[]{:S(2)}, u32[]{:S(2)}) collective-permute-start(bf16[96,960]{1,0:T(8,128)(2,1)S(1)} %get-tuple-element.124), channel_id=1, source_target_pairs={{0,3},{1,0},{2,1},{3,2},{4,7},{5,4},{6,5},{7,6},{8,11},{9,8},{10,9... | collective-permute-start | bytes 552968 | tf_op jit(solution)/shard_map/ppermute | solution.py:53
  (83 other events, 1912.6 us)
Sparse Core Ops, SparseCore 0:
  284.4 16.0 all-reduce.4
  719.0 18.7 all-reduce.6

commit v2 on v1

v2 whole, which is shorter than its diff:
```python
import functools

import jax
import jax.numpy as jnp
from jax import lax
from jax.experimental import pallas as pl
from jax.experimental.pallas import tpu as pltpu
from jax.sharding import PartitionSpec as P

F = jnp.float32
B = jnp.bfloat16


def wide_add(*terms):
    total = terms[0].astype(F)
    for term in terms[1:]:
        total = total + term.astype(F)
    return total


class Links:
    def __init__(self, sizes):
        self.sizes = sizes
        self.s = lax.axis_index("shard")
        self.c = lax.axis_index("context")
        self.t = lax.axis_index("tensor")
        self.core = self.c % 2

    def perm_t(self, value, step):
        n = self.sizes["tensor"]
        return lax.ppermute(value, "tensor", [(i, (i + step) % n) for i in range(n)])

    def perm_s(self, value, mask):
        n = self.sizes["shard"]
        return lax.ppermute(value, "shard", [(i, i ^ mask) for i in range(n)])

    def perm_c(self, value, mask=1):
        n = self.sizes["context"]
        return lax.ppermute(value, "context", [(i, i ^ mask) for i in range(n)])

    def deal(self, rows):
        n = self.sizes["tensor"]
        pieces = [lax.dynamic_index_in_dim(rows, self.t, 0, keepdims=False)]
        for d in range(1, n):
            piece = lax.dynamic_index_in_dim(rows, (self.t + d) % n, 0, keepdims=False)
            pieces.append(self.perm_t(piece, d))
        return jnp.concatenate(pieces, axis=0)

    def undeal(self, rows):
        n = self.sizes["tensor"]
        rows = rows.reshape(n, rows.shape[0] // n, rows.shape[1])
        result = jnp.zeros(rows.shape, rows.dtype)
        for d in range(n):
            piece = rows[d] if d == 0 else self.perm_t(rows[d], n - d)
            result = lax.dynamic_update_index_in_dim(result, piece, (self.t + d) % n, 0)
        return result

    def spread(self, local):
        n = self.sizes["tensor"]
        block = jnp.stack([local] + [self.perm_t(local, d) for d in range(1, n)])
        over_x = self.perm_s(block, 1)
        over_y = self.perm_s(block, 2)
        far = (self.perm_s(over_x[: n // 2], 2), self.perm_s(over_y[n // 2 :], 1))
        mine = [block, over_x, over_y, far[0], far[1]]
        other = [self.perm_c(piece) for piece in mine]
        return mine + other

    def half(self, local):
        rows = local.shape[0] // 2
        return lax.dynamic_slice_in_dim(local, self.core * rows, rows, 0)

    def collect(self, keep, give):
        n = self.sizes["tensor"]
        parts = wide_add(keep, self.perm_c(give)).astype(B)
        near, beside, above, far = parts[0], parts[1], parts[2], parts[3]
        h = n // 2
        via_y = self.perm_s(far[:h], 2)
        via_x = self.perm_s(far[h:], 1)
        beside = jnp.concatenate([wide_add(beside[:h], via_y).astype(B), beside[h:]])
        above = jnp.concatenate([above[:h], wide_add(above[h:], via_x).astype(B)])
        parts = wide_add(near, self.perm_s(beside, 1), self.perm_s(above, 2)).astype(B)
        total = wide_add(parts[0], *[self.perm_t(parts[d], n - d) for d in range(1, n)])
        mask = 2
        while mask < self.sizes["context"]:
            low = total.astype(B)
            total = wide_add(low, self.perm_c(low, mask))
            mask *= 2
        low = total.astype(B)
        other = self.perm_c(low)
        first = jnp.where(self.core == 0, low, other)
        second = jnp.where(self.core == 0, other, low)
        return jnp.concatenate([first, second])


def dot(a, b, ca=1, cb=0):
    return lax.dot_general(a, b, (((ca,), (cb,)), ((), ())), preferred_element_type=F)


def iota(shape, axis):
    return lax.broadcasted_iota(jnp.int32, shape, axis)


def block_diagonal(compact, heads):
    k, m = compact.shape[0], compact.shape[1] // heads
    zero = jnp.zeros((k, m), compact.dtype)
    rows = []
    for h in range(heads):
        row = [zero] * heads
        row[h] = compact[:, h * m : (h + 1) * m]
        rows.append(jnp.concatenate(row, axis=1))
    return jnp.concatenate(rows, axis=0)


def diagonal_blocks(full, heads):
    k, m = full.shape[0] // heads, full.shape[1] // heads
    return jnp.concatenate(
        [full[h * k : (h + 1) * k, h * m : (h + 1) * m] for h in range(heads)], axis=1
    )


def stacked(upper, lower, heads):
    a, b = block_diagonal(upper, heads), block_diagonal(lower, heads)
    gap = jnp.zeros((second_start(a.shape[0]) - a.shape[0], a.shape[1]), a.dtype)
    return jnp.concatenate([a, gap, b], axis=0)


def second_start(width):
    return -(-width // 128) * 128


def beside(left, right):
    gap = jnp.zeros((left.shape[0], second_start(left.shape[1]) - left.shape[1]), left.dtype)
    return jnp.concatenate([left, gap, right], axis=1)


def rows_to_lanes(rows, lanes):
    k = rows.shape[1]
    tile = (iota((k, lanes), 1) % k == iota((k, lanes), 0)).astype(F).astype(B)
    spread = dot(rows, tile)
    hit = iota(spread.shape, 1) // k == iota(spread.shape, 0)
    return jnp.sum(jnp.where(hit, spread, 0.0), axis=0, keepdims=True)


class Pieces:
    def __init__(self, n, m, where, refs, dest, sems, start, cols):
        self.n, self.m, self.where, self.refs = n, m, where, refs
        self.dest, self.sems, self.start_col, self.cols = dest, sems, start, cols
        self.rows = refs[0].shape[1]

    def copies(self, t):
        s, c = self.where[0], self.where[1]
        made = []
        for i in range(2):
            half = c if i == 0 else 1 - c
            for j in range(self.m):
                row = pl.multiple_of((s ^ j) * (2 * self.rows) + half * self.rows, 8)
                if j < 3:
                    src = self.refs[i * 5 + j].at[t]
                elif t < self.n // 2:
                    src = self.refs[i * 5 + 3].at[t]
                else:
                    src = self.refs[i * 5 + 4].at[t - self.n // 2]
                src = src.at[:, pl.ds(self.start_col, self.cols)]
                target = self.dest.at[t, pl.ds(row, self.rows)]
                made.append(pltpu.make_async_copy(src, target, self.sems.at[t, i * self.m + j]))
        return made

    def start(self):
        for t in range(self.n):
            for copy in self.copies(t):
                copy.start()

    def wait(self, t):
        for u in range(self.n):

            @pl.when(t == u)
            def _():
                for copy in self.copies(u):
                    copy.wait()


ANY = pl.BlockSpec(memory_space=pl.ANY)
SCALARS = pl.BlockSpec(memory_space=pltpu.SMEM)


def slot(*shape):
    zeros = (0,) * len(shape)
    return pl.BlockSpec((1,) + shape, lambda t: (t,) + zeros)


def fixed(*shape):
    zeros = (0,) * len(shape)
    return pl.BlockSpec(shape, lambda *_: zeros)


def call(body, grid, in_specs, out_specs, outs, scratch, name, flops=0):
    return pl.pallas_call(
        body,
        grid=grid,
        in_specs=in_specs,
        out_specs=out_specs,
        out_shape=[jax.ShapeDtypeStruct(s, d) for s, d in outs],
        scratch_shapes=scratch,
        compiler_params=pltpu.CompilerParams(
            dimension_semantics=("arbitrary",) * len(grid), vmem_limit_bytes=60 * 1024 * 1024
        ),
        name=name,
    )


def norm_stats(res):
    mean = jnp.mean(res, axis=-1, keepdims=True)
    centered = res - mean
    var = jnp.mean(centered * centered, axis=-1, keepdims=True)
    inverse = lax.rsqrt(var + 1e-05)
    return centered * inverse, inverse


def norm_back(normal, inverse, gain, upstream):
    scaled = upstream * gain
    inner = (
        scaled
        - jnp.mean(scaled, axis=-1, keepdims=True)
        - normal * jnp.mean(scaled * normal, axis=-1, keepdims=True)
    )
    return inner * inverse


def as_rows(vectors, first):
    width = vectors[0].shape[1]
    row = iota((8, width), 0)
    total = jnp.zeros((8, width), F)
    for i, vector in enumerate(vectors):
        total = jnp.where(row == first + i, vector, total)
    return total


def store_split(value, where, keep, give, m):
    rows = value.shape[0] // (2 * m)
    s, c = where[0], where[1]
    for half in range(2):
        parts = [value[(2 * i + half) * rows : (2 * i + half + 1) * rows].astype(B) for i in range(m)]

        @pl.when(c == half)
        def _():
            for i in range(m):
                keep[s ^ i, 0] = parts[i]

        @pl.when(c != half)
        def _():
            for i in range(m):
                give[s ^ i, 0] = parts[i]


class Shape:
    def __init__(self, sizes, features, tokens, b_up):
        self.n, self.m = sizes["tensor"], sizes["shard"]
        self.hl, self.feats, self.hd = features.shape
        self.chunk, self.width = tokens.shape[1], tokens.shape[2]
        self.span = self.chunk * self.n
        self.share = self.width // self.m
        self.rows = self.share // 2
        self.oc = self.hl * self.hd
        self.qc = 3 * self.oc
        self.hm = self.hl * self.feats
        self.ff = b_up.size * self.m
        self.q_cols = self.qc + 64
        self.mid_cols = self.ff + self.oc + 64
        self.scale = self.hd ** (-0.25)


def project(z, where, pieces, x, feat, valid):
    n, span, hl, feats, hd = z.n, z.span, z.hl, z.feats, z.hd

    def body(where, *refs):
        pcs, refs = refs[:10], refs[10:]
        x, feat, valid, q_out, k_out, v_out, qf_out, kf_out, st_out, top_out, w, sems = refs
        t = pl.program_id(0)
        fetch = Pieces(n, z.m, where, pcs, w, sems, 0, z.q_cols)
        pl.when(t == 0)(fetch.start)
        fetch.wait(t)
        bias = jnp.zeros((16, 64), F)
        for s in range(z.m):
            bias = bias + w[t, s * z.share : s * z.share + 16, z.qc :].astype(F)
        qkv = dot(x[...], w[t, :, : z.qc]) + rows_to_lanes(bias.astype(B), z.qc)
        q = (qkv[:, : z.oc] * z.scale).astype(B)
        k = (qkv[:, z.oc : 2 * z.oc] * z.scale).astype(B)
        v = qkv[:, 2 * z.oc :].astype(B)
        q_out[0], k_out[0], v_out[0] = q, k, v
        table = block_diagonal(feat[0], hl)
        qd, kd = dot(q, table), dot(k, table)
        qs, ks = q.astype(F), k.astype(F)
        qs, ks = qs * qs, ks * ks
        live = valid[...] > 0
        kfs, tops = [], []
        for h in range(hl):
            seg, cols = slice(h * hd, (h + 1) * hd), slice(h * feats, (h + 1) * feats)
            dash = qd[:, cols] - 0.5 * jnp.sum(qs[:, seg], axis=-1, keepdims=True)
            qf_out[0, :, cols] = jnp.exp(
                dash - jnp.floor(jnp.max(dash, axis=-1, keepdims=True))
            ).astype(B)
            dash = kd[:, cols] - 0.5 * jnp.sum(ks[:, seg], axis=-1, keepdims=True)
            top = jnp.max(jnp.where(live, dash, -1e30), axis=0, keepdims=True)
            top = jnp.floor(jnp.max(top, axis=1, keepdims=True))
            kf = jnp.where(live, jnp.exp(dash - top), 0.0).astype(B)
            kf_out[0, :, cols] = kf
            kfs.append(kf)
            tops.append(jnp.broadcast_to(top, (8, feats)))
        top_out[0] = jnp.concatenate(tops, axis=1)
        vx = jnp.concatenate([v, jnp.ones((span, 64), B)], axis=1)
        state = dot(vx, jnp.concatenate(kfs, axis=1), 0, 0)
        st_out[0] = jnp.concatenate(
            [diagonal_blocks(state[: z.oc], hl), state[z.oc : z.oc + 8]], axis=0
        ).astype(B)

    return call(
        body,
        (n,),
        [SCALARS] + [ANY] * 10 + [fixed(span, z.width), slot(hd, z.hm), fixed(span, 1)],
        [slot(span, z.oc)] * 3 + [slot(span, z.hm)] * 2 + [slot(hd + 8, z.hm), slot(8, z.hm)],
        [((n, span, z.oc), B)] * 3
        + [((n, span, z.hm), B)] * 2
        + [((n, hd + 8, z.hm), B), ((n, 8, z.hm), F)],
        [pltpu.VMEM((n, z.width, z.q_cols), B), pltpu.SemaphoreType.DMA((n, 2 * z.m))],
        "project",
    )(where, *pieces, x, feat, valid)


def attend(z, where, pieces, x, qf, state):
    n, span, hl, hd = z.n, z.span, z.hl, z.hd

    def body(where, *refs):
        pcs, refs = refs[:10], refs[10:]
        x, qf, state, mixed_out, den_out, normal_out, inverse_out, vec_out, bup_out, w, acc, sems = refs
        t = pl.program_id(0)
        fetch = Pieces(n, z.m, where, pcs, w, sems, z.ff, z.oc + 64)
        pl.when(t == 0)(fetch.start)
        compact = state[0, :hd]
        total = jnp.broadcast_to(state[0, hd : hd + 1], (hd, z.hm))
        table = stacked(compact, total, hl)
        both = dot(qf[0], table, 1, 1)
        den = both[:, second_start(z.oc) :]
        mixed = (both[:, : z.oc] / den).astype(B)
        mixed_out[0] = mixed
        den_out[0] = den
        fetch.wait(t)
        part = dot(mixed, w[t, :, : z.oc], 1, 1)

        @pl.when(t == 0)
        def _():
            acc[...] = part

        @pl.when(t > 0)
        def _():
            acc[...] += part

        bias = jnp.zeros((16, 64), F)
        for s in range(z.m):
            bias = bias + w[t, s * z.share + 24 : s * z.share + 40, z.oc :].astype(F)
        bup_out[0] = jnp.broadcast_to(rows_to_lanes(bias.astype(B), z.ff), (8, z.ff))

        @pl.when(t == n - 1)
        def _():
            lanes = z.width
            per = z.share // 64
            tile = (iota((64, lanes), 1) % 64 == iota((64, lanes), 0)).astype(F).astype(B)
            found = jnp.zeros((24, lanes), F)
            for s in range(z.m):
                spread = dot(w[0, s * z.share : s * z.share + 24, z.oc :], tile)
                hit = iota((24, lanes), 1) // 64 == per * s + iota((24, lanes), 0) % per
                found = found + jnp.where(hit, spread, 0.0)
            pick = (iota((8, 24), 1) // per == iota((8, 24), 0)).astype(F).astype(B)
            vec = dot(pick, found.astype(B))
            vec_out[...] = vec
            res = acc[...] + vec[0:1] + x[...].astype(F)
            normal, inverse = norm_stats(res)
            normal_out[...] = normal
            inverse_out[...] = inverse

    return call(
        body,
        (n,),
        [SCALARS] + [ANY] * 10 + [fixed(span, z.width), slot(span, z.hm), slot(hd + 8, z.hm)],
        [
            slot(span, z.oc),
            slot(span, z.oc),
            fixed(span, z.width),
            fixed(span, 1),
            fixed(8, z.width),
            slot(8, z.ff),
        ],
        [
            ((n, span, z.oc), B),
            ((n, span, z.oc), F),
            ((span, z.width), F),
            ((span, 1), F),
            ((8, z.width), F),
            ((n, 8, z.ff), F),
        ],
        [
            pltpu.VMEM((n, z.width, z.oc + 64), B),
            pltpu.VMEM((span, z.width), F),
            pltpu.SemaphoreType.DMA((n, 2 * z.m)),
        ],
        "attend",
    )(where, *pieces, x, qf, state)


def widen(z, where, pieces, normal, vec, bup):
    n, span = z.n, z.span

    def body(where, *refs):
        pcs, refs = refs[:10], refs[10:]
        normal, vec, bup, act_out, slope_out, w, low, sems = refs
        t = pl.program_id(0)
        fetch = Pieces(n, z.m, where, pcs, w, sems, 0, z.ff)

        @pl.when(t == 0)
        def _():
            fetch.start()
            low[...] = (normal[...] * vec[1:2] + vec[2:3]).astype(B)

        fetch.wait(t)
        up = dot(low[...], w[t]) + bup[0, 0:1]
        share = 0.5 * (1.0 + lax.erf(up * 0.7071067811865476))
        act_out[0] = (up * share).astype(B)
        slope_out[0] = (share + up * jnp.exp(-0.5 * up * up) * 0.3989422804014327).astype(B)

    return call(
        body,
        (n,),
        [SCALARS] + [ANY] * 10 + [fixed(span, z.width), fixed(8, z.width), slot(8, z.ff)],
        [slot(span, z.ff)] * 2,
        [((n, span, z.ff), B)] * 2,
        [
            pltpu.VMEM((n, z.width, z.ff), B),
            pltpu.VMEM((span, z.width), B),
            pltpu.SemaphoreType.DMA((n, 2 * z.m)),
        ],
        "widen",
    )(where, *pieces, normal, vec, bup)


def narrow(z, where, pieces, normal, vec, cot, act, slope):
    n, span, rows, m = z.n, z.span, z.rows, z.m

    def body(where, *refs):
        pcs, refs = refs[:10], refs[10:]
        normal, vec, cot, act, slope = refs[:5]
        out, dres_out, keep, give, dup_out, small_out = refs[5:11]
        w, acc, low, low_t, sems = refs[11:]
        p, t = pl.program_id(0), pl.program_id(1)
        fetch = Pieces(n, m, where, pcs, w, sems, 0, z.ff)

        @pl.when((p == 0) & (t == 0))
        def _():
            fetch.start()

        @pl.when(p == 0)
        def _():
            fetch.wait(t)
            part = dot(act[0], w[t], 1, 1)

            @pl.when(t == 0)
            def _():
                acc[...] = part

            @pl.when(t > 0)
            def _():
                acc[...] += part

        @pl.when((p == 0) & (t == n - 1))
        def _():
            normed = normal[...] * vec[1:2] + vec[2:3]
            second, inverse = norm_stats(acc[...] + vec[3:4] + normed)
            out[...] = (second * vec[4:5] + vec[5:6]).astype(B)
            up = cot[...].astype(F)
            dres = norm_back(second, inverse, vec[4:5], up)
            dres_out[...] = dres
            low[...] = dres.astype(B)
            low_t[...] = dres.T.astype(B)
            small_out[...] = as_rows(
                [
                    jnp.sum(dres, axis=0, keepdims=True),
                    jnp.sum(up * second, axis=0, keepdims=True),
                    jnp.sum(up, axis=0, keepdims=True),
                ],
                3,
            )

        @pl.when(p == 1)
        def _():
            dup_out[0] = (dot(low[...], w[t]) * slope[0].astype(F)).astype(B)
            store_split(dot(low_t[...], act[0]), where, keep, give, m)

    second = lambda *shape: pl.BlockSpec((1,) + shape, lambda p, t: (p * t,) + (0,) * len(shape))
    grads = pl.BlockSpec((m, 1, rows, z.ff), lambda p, t: (0, p * t, 0, 0))
    return call(
        body,
        (2, n),
        [SCALARS]
        + [ANY] * 10
        + [
            fixed(span, z.width),
            fixed(8, z.width),
            fixed(span, z.width),
            pl.BlockSpec((1, span, z.ff), lambda p, t: (t, 0, 0)),
            second(span, z.ff),
        ],
        [fixed(span, z.width), fixed(span, z.width), grads, grads, second(span, z.ff), fixed(8, z.width)],
        [
            ((span, z.width), B),
            ((span, z.width), F),
            ((m, n, rows, z.ff), B),
            ((m, n, rows, z.ff), B),
            ((n, span, z.ff), B),
            ((8, z.width), F),
        ],
        [
            pltpu.VMEM((n, z.width, z.ff), B),
            pltpu.VMEM((span, z.width), F),
            pltpu.VMEM((span, z.width), B),
            pltpu.VMEM((z.width, span), B),
            pltpu.SemaphoreType.DMA((n, 2 * m)),
        ],
        "narrow",
    )(where, *pieces, normal, vec, cot, act, slope)


def widen_back(z, where, pieces, normal, inverse, vec, dup, dres):
    n, span = z.n, z.span

    def body(where, *refs):
        pcs, refs = refs[:10], refs[10:]
        normal, inverse, vec, dup, dres, out, small_out, w, acc, sems = refs
        t = pl.program_id(0)
        fetch = Pieces(n, z.m, where, pcs, w, sems, 0, z.ff)
        pl.when(t == 0)(fetch.start)
        fetch.wait(t)
        part = dot(dup[0], w[t], 1, 1)

        @pl.when(t == 0)
        def _():
            acc[...] = part + dres[...]

        @pl.when(t > 0)
        def _():
            acc[...] += part

        @pl.when(t == n - 1)
        def _():
            up = acc[...]
            back = norm_back(normal[...], inverse[...], vec[1:2], up)
            out[...] = back
            small_out[...] = as_rows(
                [
                    jnp.sum(back, axis=0, keepdims=True),
                    jnp.sum(up * normal[...], axis=0, keepdims=True),
                    jnp.sum(up, axis=0, keepdims=True),
                ],
                0,
            )

    return call(
        body,
        (n,),
        [SCALARS]
        + [ANY] * 10
        + [
            fixed(span, z.width),
            fixed(span, 1),
            fixed(8, z.width),
            slot(span, z.ff),
            fixed(span, z.width),
        ],
        [fixed(span, z.width), fixed(8, z.width)],
        [((span, z.width), F), ((8, z.width), F)],
        [
            pltpu.VMEM((n, z.width, z.ff), B),
            pltpu.VMEM((span, z.width), F),
            pltpu.SemaphoreType.DMA((n, 2 * z.m)),
        ],
        "widen_back",
    )(where, *pieces, normal, inverse, vec, dup, dres)


def attend_back(z, where, pieces, dres, normal, vec, small_a, small_b, dup, mixed, den, qf, q, state, feat):
    n, span, hl, hd, m, rows = z.n, z.span, z.hl, z.hd, z.m, z.rows

    def body(where, *refs):
        pcs, refs = refs[:10], refs[10:]
        dres, normal, vec, small_a, small_b, dup, mixed, den, qf, q, state, feat = refs[:12]
        keep, give, dq_out, dstate_out, w, low, low_t, normed_t, sems = refs[12:]
        t = pl.program_id(0)
        fetch = Pieces(n, m, where, pcs, w, sems, z.ff, z.oc + 64)

        @pl.when(t == 0)
        def _():
            fetch.start()
            low[...] = dres[...].astype(B)
            low_t[...] = dres[...].T.astype(B)
            normed_t[...] = (normal[...] * vec[1:2] + vec[2:3]).T.astype(B)

        fetch.wait(t)
        start = second_start(z.oc)
        d_mixed = dot(low[...], w[t, :, : z.oc]).astype(B).astype(F)
        d_num = d_mixed / den[0]
        d_den = -(d_num * mixed[0].astype(F))
        pair = beside(d_num.astype(B), d_den.astype(B))
        full = dot(pair, qf[0], 0, 0)
        row = jnp.concatenate(
            [
                jnp.sum(
                    full[start + h * hd : start + (h + 1) * hd, h * z.feats : (h + 1) * z.feats],
                    axis=0,
                    keepdims=True,
                )
                for h in range(hl)
            ],
            axis=1,
        )
        dstate_out[0] = jnp.concatenate(
            [diagonal_blocks(full[: z.oc], hl), jnp.broadcast_to(row, (8, z.hm))], axis=0
        ).astype(B)
        compact = state[0, :hd]
        total = jnp.broadcast_to(state[0, hd : hd + 1], (hd, z.hm))
        dash = (dot(pair, stacked(compact, total, hl)) * qf[0].astype(F)).astype(B)
        back = dot(dash, stacked(feat[0], jnp.ones((hd, z.hm), B), hl), 1, 1)
        dq = (back[:, : z.oc] - q[0].astype(F) * back[:, start:]) * z.scale
        dq_out[0] = dq.astype(B)
        grad_up = dot(normed_t[...], dup[0])
        grad_out = dot(low_t[...], mixed[0])
        b_up = jnp.sum(dup[0].astype(F), axis=0, keepdims=True)
        packed = small_a[...] + small_b[...] + as_rows([b_up], 6)
        per = z.width // 64
        one = (iota((rows, 8), 0) // per == iota((rows, 8), 1)).astype(F).astype(B)
        laid = dot(one, packed.astype(B))
        laid = jnp.where(iota(laid.shape, 1) // 64 == iota(laid.shape, 0) % per, laid, 0.0)
        fold = (iota((z.width, 64), 0) % 64 == iota((z.width, 64), 1)).astype(F).astype(B)
        tail = dot(laid.astype(B), fold)
        tail = jnp.concatenate([tail] * (2 * m), axis=0)
        store_split(
            jnp.concatenate([grad_up, jnp.concatenate([grad_out, tail], axis=1)], axis=1),
            where,
            keep,
            give,
            m,
        )

    grads = pl.BlockSpec((m, 1, rows, z.mid_cols), lambda t: (0, t, 0, 0))
    return call(
        body,
        (n,),
        [SCALARS]
        + [ANY] * 10
        + [
            fixed(span, z.width),
            fixed(span, z.width),
            fixed(8, z.width),
            fixed(8, z.width),
            fixed(8, z.width),
            slot(span, z.ff),
            slot(span, z.oc),
            slot(span, z.oc),
            slot(span, z.hm),
            slot(span, z.oc),
            slot(hd + 8, z.hm),
            slot(hd, z.hm),
        ],
        [grads, grads, slot(span, z.oc), slot(hd + 8, z.hm)],
        [
            ((m, n, rows, z.mid_cols), B),
            ((m, n, rows, z.mid_cols), B),
            ((n, span, z.oc), B),
            ((n, hd + 8, z.hm), B),
        ],
        [
            pltpu.VMEM((n, z.width, z.oc + 64), B),
            pltpu.VMEM((span, z.width), B),
            pltpu.VMEM((z.width, span), B),
            pltpu.VMEM((z.width, span), B),
            pltpu.SemaphoreType.DMA((n, 2 * m)),
        ],
        "attend_back",
    )(where, *pieces, dres, normal, vec, small_a, small_b, dup, mixed, den, qf, q, state, feat)


def project_back(z, where, pieces, x, dres, dq, k, v, kf, dstate, feat):
    n, span, hl, hd, m, rows = z.n, z.span, z.hl, z.hd, z.m, z.rows

    def body(where, *refs):
        pcs, refs = refs[:10], refs[10:]
        x, dres, dq, k, v, kf, dstate, feat = refs[:8]
        keep, give, out, w, x_t, acc, sems = refs[8:]
        t = pl.program_id(0)
        fetch = Pieces(n, m, where, pcs, w, sems, 0, z.q_cols)

        @pl.when(t == 0)
        def _():
            fetch.start()
            x_t[...] = x[...].astype(F).T.astype(B)

        start = second_start(z.oc)
        table = block_diagonal(dstate[0, :hd], hl)
        total = dstate[0, hd : hd + 1].astype(F)
        dash = ((dot(v[0], table) + total) * kf[0].astype(F)).astype(B)
        dv = dot(kf[0], table, 1, 1)
        back = dot(dash, stacked(feat[0], jnp.ones((hd, z.hm), B), hl), 1, 1)
        dk = (back[:, : z.oc] - k[0].astype(F) * back[:, start:]) * z.scale
        dqkv = jnp.concatenate(
            [dq[0], dk.astype(B), dv.astype(B), jnp.zeros((span, 64), B)], axis=1
        )
        bias = jnp.sum(dqkv.astype(F), axis=0, keepdims=True)
        laid = jnp.broadcast_to(bias, (rows, z.q_cols))
        laid = jnp.where(iota(laid.shape, 1) // 64 == iota(laid.shape, 0), laid, 0.0)
        a, b = iota((z.q_cols, z.q_cols), 0), iota((z.q_cols, z.q_cols), 1)
        fold = ((b >= z.qc) & (a % 64 == b - z.qc)).astype(F).astype(B)
        tail = dot(laid.astype(B), fold)
        grad = dot(x_t[...], dqkv)
        store_split(grad + jnp.concatenate([tail] * (2 * m), axis=0), where, keep, give, m)
        fetch.wait(t)
        part = dot(dqkv, w[t], 1, 1)

        @pl.when(t == 0)
        def _():
            acc[...] = part + dres[...]

        @pl.when(t > 0)
        def _():
            acc[...] += part

        @pl.when(t == n - 1)
        def _():
            out[...] = acc[...].astype(B)

    grads = pl.BlockSpec((m, 1, rows, z.q_cols), lambda t: (0, t, 0, 0))
    return call(
        body,
        (n,),
        [SCALARS]
        + [ANY] * 10
        + [
            fixed(span, z.width),
            fixed(span, z.width),
            slot(span, z.oc),
            slot(span, z.oc),
            slot(span, z.oc),
            slot(span, z.hm),
            slot(hd + 8, z.hm),
            slot(hd, z.hm),
        ],
        [grads, grads, fixed(span, z.width)],
        [
            ((m, n, rows, z.q_cols), B),
            ((m, n, rows, z.q_cols), B),
            ((span, z.width), B),
        ],
        [
            pltpu.VMEM((n, z.width, z.q_cols), B),
            pltpu.VMEM((z.width, span), B),
            pltpu.VMEM((span, z.width), F),
            pltpu.SemaphoreType.DMA((n, 2 * m)),
        ],
        "project_back",
    )(where, *pieces, x, dres, dq, k, v, kf, dstate, feat)


def place(part, axis, index, count):
    shape = list(part.shape)
    shape[axis] *= count
    return lax.dynamic_update_slice_in_dim(
        jnp.zeros(shape, part.dtype), part, index * part.shape[axis], axis
    )


def on_device(
    sizes,
    tokens,
    lengths,
    features,
    w_qkv,
    b_qkv,
    w_out,
    b_out,
    gain_one,
    shift_one,
    w_up,
    b_up,
    w_down,
    b_down,
    gain_two,
    shift_two,
    cotangent,
):
    links = Links(sizes)
    z = Shape(sizes, features, tokens, b_up)
    n, m, share = z.n, z.m, z.share
    where = jnp.stack([links.s, links.core]).astype(jnp.int32)
    spare = place(b_qkv, 2, links.s, m).reshape(3 * z.hl, z.hd)
    spare = jnp.pad(spare, ((0, share - 3 * z.hl), (0, 0)))
    local = jnp.concatenate([w_qkv.reshape(share, z.qc), spare], axis=1)
    pieces_qkv = links.spread(links.half(local))
    x = links.deal(tokens)
    feat_t = features.transpose(2, 0, 1).reshape(z.hd, z.hm)
    feat_half = links.half(feat_t)
    feat_mine = jnp.stack([feat_half] + [links.perm_t(feat_half, d) for d in range(1, n)])
    feat_other = links.perm_c(feat_mine)
    feat_low = jnp.where(links.core == 0, feat_mine, feat_other)
    feat_high = jnp.where(links.core == 0, feat_other, feat_mine)
    feat = jnp.concatenate([feat_low, feat_high], axis=1)
    vectors = jnp.stack([b_out, gain_one, shift_one, b_down, gain_two, shift_two])
    vectors = jnp.pad(vectors.reshape(6 * share // 64, 64), ((0, 24 - 6 * share // 64), (0, 0)))
    up_bias = place(b_up, 1, links.s, m).reshape(-1, 64)
    spare = jnp.concatenate([vectors, up_bias])
    spare = jnp.pad(spare, ((0, share - spare.shape[0]), (0, 0)))
    local = jnp.concatenate([w_up, w_out.T, spare], axis=1)
    pieces_mid = links.spread(links.half(local))
    pieces_down = links.spread(links.half(w_down.T))
    cot = links.deal(cotangent)
    length = lax.dynamic_index_in_dim(lengths, links.t, 0, keepdims=False)
    order = (links.t - jnp.arange(n)) % n
    position = links.c * z.span + order[:, None] * z.chunk + jnp.arange(z.chunk)[None]
    valid = (position.reshape(-1, 1) < length).astype(F)
    q, k, v, qf, kf, state, top = project(z, where, pieces_qkv, x, feat, valid)
    own_top = top[:, :1]
    most, mask = own_top, 1
    while mask < sizes["context"]:
        other, other_top = links.perm_c(state, mask), links.perm_c(top, mask)[:, :1]
        joint = jnp.maximum(most, other_top)
        state = (
            state.astype(F) * jnp.exp(most - joint) + other.astype(F) * jnp.exp(other_top - joint)
        ).astype(B)
        most, mask = joint, 2 * mask
        top = jnp.broadcast_to(most, top.shape)
    mixed, den, normal, inverse, vec, bup = attend(z, where, pieces_mid, x, qf, state)
    act, slope = widen(z, where, pieces_mid, normal, vec, bup)
    out, d_res_two, keep, give, dup, small_b = narrow(
        z, where, pieces_down, normal, vec, cot, act, slope
    )
    result = links.undeal(out)
    own_down = links.collect(keep, give)
    d_res_one, small_a = widen_back(z, where, pieces_mid, normal, inverse, vec, dup, d_res_two)
    keep, give, dq, d_state = attend_back(
        z, where, pieces_mid, d_res_one, normal, vec, small_a, small_b, dup, mixed, den, qf, q, state, feat
    )
    mask = 1
    while mask < sizes["context"]:
        d_state = wide_add(d_state, links.perm_c(d_state, mask)).astype(B)
        mask *= 2
    d_state = (d_state.astype(F) * jnp.exp(own_top - most)).astype(B)
    own_mid = links.collect(keep, give)
    keep, give, grad_x = project_back(z, where, pieces_qkv, x, d_res_one, dq, k, v, kf, d_state, feat)
    own_qkv = links.collect(keep, give)
    grad_tokens = links.undeal(grad_x).astype(F)
    def mine(value, axis):
        size = value.shape[axis] // m
        return lax.dynamic_slice_in_dim(value, links.s * size, size, axis).astype(F)

    own_b_qkv = mine(own_qkv[: 3 * z.hl, z.qc :].reshape(3, z.hl, z.hd), 2)
    tail = own_mid[: z.rows, z.ff + z.oc :]
    vecs = mine(tail[: 6 * z.width // 64].reshape(6, z.width), 1)
    first = 6 * z.width // 64
    own_b_up = mine(tail[first : first + z.ff // 64].reshape(b_up.shape[0], -1), 1)
    return (
        result,
        grad_tokens,
        own_qkv[:, : z.qc].reshape(w_qkv.shape).astype(F),
        own_b_qkv,
        own_mid[:, z.ff : z.ff + z.oc].T.astype(F),
        vecs[0],
        vecs[1],
        vecs[2],
        own_mid[:, : z.ff].astype(F),
        own_b_up,
        own_down.T.astype(F),
        vecs[3],
        vecs[4],
        vecs[5],
    )


def solution(mesh):
    sizes = dict(mesh.shape)
    in_specs = (
        P("shard", ("context", "tensor"), None),
        P("shard"),
        P("tensor", None, None),
        P("shard", None, "tensor", None),
        P(None, "tensor", "shard"),
        P("tensor", "shard"),
        P("shard"),
        P("shard"),
        P("shard"),
        P("shard", "tensor"),
        P("tensor", "shard"),
        P("tensor", "shard"),
        P("shard"),
        P("shard"),
        P("shard"),
        P("shard", ("context", "tensor"), None),
    )
    out_specs = (
        P("shard", ("context", "tensor"), None),
        P("shard", ("context", "tensor"), None),
        P("shard", None, "tensor", None),
        P(None, "tensor", "shard"),
        P("tensor", "shard"),
        P("shard"),
        P("shard"),
        P("shard"),
        P("shard", "tensor"),
        P("tensor", "shard"),
        P("tensor", "shard"),
        P("shard"),
        P("shard"),
        P("shard"),
    )
    return jax.shard_map(
        functools.partial(on_device, sizes),
        mesh=mesh,
        in_specs=in_specs,
        out_specs=out_specs,
        check_vma=False,
    )
```

time: 918 us -> 408 us (0.44)
  Pallas kernels: 464 us -> 109 us
  matrix products: 72.3 us -> 0 us
  local copies, waits for them, and re-layouts: 81.5 us -> 30.6 us
  waiting for transfers between devices: 102 us -> 143 us
  other arithmetic: 65.2 us -> 24.7 us
  between operations: 15.9 us -> 2.24 us
    pallas_call x3 -> x7, Pallas kernels: 464 us -> 109 us  [the longest x1 22.1 us: project(): call(body, (n,), [SCALARS] + [ANY] * 10 + [fixed(span, z.width), slot(hd,...]
    dot_general x23 -> x0, matrix products: 71.5 us -> none  [the longest x1 5.75 us: on_device(): dot('rhk,hmk->rhm', values, d_state) + d_total[None]]
    ppermute x33, waiting for transfers between devices: 35.1 us -> 71.9 us  [perm_t(): lax.ppermute(value, 'tensor', [(i, (i + step) % n) for i in range(n)])]
    convert_element_type x11 -> x10, other arithmetic: 23.4 us -> 7.27 us  [the longest x1 2.07 us: on_device(): state = (state.astype(F) * jnp.exp(most - joint) + other.astype(F) * jnp....]
    reduce_sum x9 -> x0, other arithmetic: 14.9 us -> none  [the longest x1 4.46 us: on_device(): key_total = jnp.sum(key_feat, axis=0, dtype=F)]
    ppermute x33, starting transfers between devices: 73.5 us -> 60.9 us  [perm_t(): lax.ppermute(value, 'tensor', [(i, (i + step) % n) for i in range(n)])]
    concatenate x3 -> x0, local copies, waits for them, and re-layouts: 12.6 us -> none  [the longest x1 8.36 us: on_device(): own_mid = links.collect(jnp.concatenate([grad_out, grad_up], axis=2))]
    convert_element_type x6 -> x2, local copies, waits for them, and re-layouts: 12.1 us -> 1.89 us  [the longest x1 1.03 us: on_device(): own_qkv[:, :z.qc].reshape(w_qkv.shape).astype(F)]
  transfers between devices with their start and end apart: 81 -> 82, of which waited for: 29 -> 28; matrix products, arithmetic and copies ran while one was open for 20% -> 11% of each run, Pallas kernels for 51% -> 22%
where the time goes in v2:
time: 408 us; the launch traced here: 402 us
  waiting for transfers between devices  143 us (35%)
  Pallas kernels  109 us (27%)
  starting transfers between devices  92 us (23%)
  local copies, waits for them, and re-layouts  30.6 us (8%)
  other arithmetic  24.7 us (6%)
    ppermute x33, waiting for transfers between devices, perm_t(): lax.ppermute(value, 'tensor', [(i, (i + step) % n) for i in range(n)])  71.9 us
    ppermute x24, waiting for transfers between devices, perm_s(): return lax.ppermute(value, 'shard', [(i, i ^ mask) for i in range(n)])  69.5 us
    ppermute x33, starting transfers between devices, perm_t(): lax.ppermute(value, 'tensor', [(i, (i + step) % n) for i in range(n)])  60.9 us
    ppermute x24, starting transfers between devices, perm_s(): return lax.ppermute(value, 'shard', [(i, i ^ mask) for i in range(n)])  26.3 us
    pallas_call x1, Pallas kernels, project(): call(body, (n,), [SCALARS] + [ANY] * 10 + [fixed(span, z.width), slot(hd,...  22.1 us
    pallas_call x1, Pallas kernels, project_back(): call(body, (n,), [SCALARS] + [ANY] * 10 + [fixed(span, z.width), fixed(sp...  19.1 us
    pallas_call x1, Pallas kernels, attend_back(): call(body, (n,), [SCALARS] + [ANY] * 10 + [fixed(span, z.width), fixed(sp...  19 us
    pallas_call x1, Pallas kernels, narrow(): call(body, (2, n), [SCALARS] + [ANY] * 10 + [fixed(span, z.width), fixed(...  18.8 us
  transfers between devices with their start and end apart: 82, of which 28 were waited for; matrix products, arithmetic and copies ran while one was open for 11% of the time, Pallas kernels for 22%

profile of v2, /device:TPU:0, one launch (start us, length us, event | category | flops | bytes accessed | tf_op | source)
XLA Modules:
  0.0 401.9 jit_solution(11922477719582443615)
XLA Ops:
  1.6 3.1 collective-permute-start.39
  4.8 2.6 collective-permute-start.40
  13.9 2.8 collective-permute-start.29
  18.8 1.5 collective-permute-start.1
  20.4 2.9 collective-permute-start.2
  23.3 4.0 %collective-permute-done.28 = bf16[96,640]{1,0:T(8,128)(2,1)S(1)} collective-permute-done((bf16[96,640]{1,0:T(8,128)(2,1)S(1)}, bf16[96,640]{1,0:T(8,128)(2,1)S(1)}, u32[]{:S(2)}, u32[]{:S(2)}) %collective-permute-start.28) | collective-permute-done | bytes 122912 | tf_op jit(solution)/shard_map/ppermute | solution.py:31
  28.0 3.2 collective-permute-start.25
  32.0 3.9 collective-permute-start.26
  35.8 7.0 %collective-permute-done.1 = bf16[96,768]{1,0:T(8,128)(2,1)S(1)} collective-permute-done((bf16[96,768]{1,0:T(8,128)(2,1)S(1)}, bf16[96,768]{1,0:T(8,128)(2,1)S(1)}, u32[]{:S(2)}, u32[]{:S(2)}) %collective-permute-start.1) | collective-permute-done | bytes 147488 | tf_op jit(solution)/shard_map/ppermute | solution.py:31
  44.0 8.1 %collective-permute-start.14 = (bf16[96,1024]{1,0:T(8,128)(2,1)S(1)}, bf16[96,1024]{1,0:T(8,128)(2,1)S(1)}, u32[]{:S(2)}, u32[]{:S(2)}) collective-permute-start(bf16[96,1024]{1,0:T(8,128)(2,1)S(1)} %fusion.25), channel_id=1, source_target_pairs={{0,3},{1,0},{2,1},{3,2},{4,7},{5,4},{6,5},{7,6},{8,11},{9,8},{10,9... | collective-permute-start | bytes 589832 | tf_op jit(solution)/shard_map/ppermute | solution.py:31
  52.1 2.3 collective-permute-start.12
  54.4 2.2 collective-permute-done.25
  57.3 1.9 collective-permute-start.30
  59.9 4.3 %collective-permute-start.45 = (bf16[128,768]{1,0:T(8,128)(2,1)S(1)}, bf16[128,768]{1,0:T(8,128)(2,1)S(1)}, u32[]{:S(2)}, u32[]{:S(2)}) collective-permute-start(bf16[128,768]{1,0:T(8,128)(2,1)S(1)} %get-tuple-element.130), channel_id=1, source_target_pairs={{0,1},{1,2},{2,3},{3,0},{4,5},{5,6},{6,7},{7,4},{8,9},{9,10},{10,1... | collective-permute-start | bytes 589832 | tf_op jit(solution)/shard_map/ppermute | solution.py:31
  64.2 11.4 %collective-permute-done.13 = bf16[96,1024]{1,0:T(8,128)(2,1)S(1)} collective-permute-done((bf16[96,1024]{1,0:T(8,128)(2,1)S(1)}, bf16[96,1024]{1,0:T(8,128)(2,1)S(1)}, u32[]{:S(2)}, u32[]{:S(2)}) %collective-permute-start.13) | collective-permute-done | bytes 196640 | tf_op jit(solution)/shard_map/ppermute | solution.py:31
  77.7 2.0 collective-permute-start.3
  79.6 4.6 %collective-permute-done.46 = bf16[128,768]{1,0:T(8,128)(2,1)S(1)} collective-permute-done((bf16[128,768]{1,0:T(8,128)(2,1)S(1)}, bf16[128,768]{1,0:T(8,128)(2,1)S(1)}, u32[]{:S(2)}, u32[]{:S(2)}) %collective-permute-start.46) | collective-permute-done | bytes 196640 | tf_op jit(solution)/shard_map/ppermute | solution.py:31
  84.3 1.9 collective-permute-start.4
  86.2 1.5 collective-permute-done.47
  87.7 1.9 collective-permute-start.31
  89.8 1.6 collective-permute-start.15
  91.4 17.3 %collective-permute-done.31.refs_2_ = bf16[4,96,640]{2,1,0:T(8,128)(2,1)S(1)} collective-permute-done((bf16[4,96,640]{2,1,0:T(8,128)(2,1)S(1)}, bf16[4,96,640]{2,1,0:T(8,128)(2,1)S(1)}, u32[]{:S(2)}, u32[]{:S(2)}) %collective-permute-start.31) | collective-permute-done | bytes 491552 | tf_op jit(solution)/shard_map/ppermute | solution.py:35
  108.6 1.7 collective-permute-start.16
  113.5 1.5 collective-permute-start.33
  115.0 16.2 %collective-permute-done.32.refs_3_ = bf16[2,96,640]{2,1,0:T(8,128)(2,1)} collective-permute-done((bf16[2,96,640]{2,1,0:T(8,128)(2,1)}, bf16[2,96,640]{2,1,0:T(8,128)(2,1)}, u32[]{:S(2)}, u32[]{:S(2)}) %collective-permute-start.32) | collective-permute-done | bytes 245792 | tf_op jit(solution)/shard_map/ppermute | solution.py:35
  132.3 1.7 slice.342
  134.0 1.6 collective-permute-start.5
  138.3 2.0 pad_maximum_fusion.1.refs_10_
  140.3 1.7 slice.343
  143.6 1.5 collective-permute-start.6
  148.4 22.1 %project.1 = (bf16[4,512,192]{2,1,0:T(8,128)(2,1)}, bf16[4,512,192]{2,1,0:T(8,128)(2,1)}, bf16[4,512,192]{2,1,0:T(8,128)(2,1)}, bf16[4,512,768]{2,1,0:T(8,128)(2...) custom-call(s32[2]{0:T(128)} %pad_add_fusion.where, ...), custom_call_target="tpu_custom_call" | custom-call | tf_op jit(solution)/shard_map/project/pallas_call | solution.py:316
  170.6 1.5 collective-permute-done.43
  173.3 2.2 pad_maximum_fusion.2.refs_12_
  177.7 2.1 add_convert_fusion.4.refs_12_.refs_20_
  179.8 10.5 %attend.1 = (bf16[4,512,192]{2,1,0:T(8,128)(2,1)}, f32[4,512,192]{2,1,0:T(8,128)}, f32[512,768]{1,0:T(8,128)}, f32[512,1]{1,0:T(8,128)}, f32[8,768]{1,0:T(8,128)}, /*index=5*/f32[4,8,768]{2,1,0:T(8,128)}) custom-call(s32[2]{0:T(128)} %pad_add_fusion.where, bf16[4,96,1024]{2,1,0:T(8,128)(2,1)} %copy-done, bf16[4,96,1024]{2,1,0:T(8,128)(2,1)} %copy-done.1, ...), custom_call_target="tpu_custom_call" | custom-call | tf_op jit(solution)/shard_map/attend/pallas_call | solution.py:380
  190.3 9.3 %widen.1 = (bf16[4,512,768]{2,1,0:T(8,128)(2,1)}, bf16[4,512,768]{2,1,0:T(8,128)(2,1)}) custom-call(s32[2]{0:T(128)} %pad_add_fusion.where, bf16[4,96,1024]{2,1,0:T(8,128)(2,1)} %copy-done, bf16[4,96,1024]{2,1,0:T(8,128)(2,1)} %copy-done.1, bf16[4,96,1024]{2,1,0:T(8,128)(2,1)} %copy-done.2, bf16[2,96,1024]{2,1,0:T(8,128)(2,1)} %copy-done.6, ...), custom_call_target="tpu_custom_call" | custom-call | tf_op jit(solution)/shard_map/widen/pallas_call | solution.py:429
  200.5 18.8 %narrow.1 = (bf16[512,768]{1,0:T(8,128)(2,1)}, f32[512,768]{1,0:T(8,128)}, bf16[4,4,96,768]{3,2,1,0:T(8,128)(2,1)}, bf16[4,4,96,768]{3,2,1,0:T(8,128)(2,1)}, bf1...) custom-call(s32[2]{0:T(128)} %pad_add_fusion.where, bf16[4,96,768]{2,1,0:T(8,128)(2,1)} %copy-done.11, ...), custom_call_target="tpu_custom_call" | custom-call | tf_op jit(solution)/shard_map/narrow/pallas_call | solution.py:498
  219.6 10.2 %widen_back.1 = (f32[512,768]{1,0:T(8,128)}, f32[8,768]{1,0:T(8,128)}) custom-call(s32[2]{0:T(128)} %pad_add_fusion.where, bf16[4,96,1024]{2,1,0:T(8,128)(2,1)} %copy-done, bf16[4,96,1024]{2,1,0:T(8,128)(2,1)} %copy-done.1, bf16[4,96,1024]{2,1,0:T(8,128)(2,1)} %copy-done.2, bf16[2,96,1024]{2,1,0:T(8,128)(2,1)} %copy-done.6, ...), custom_call_target="tpu_custom_call" | custom-call | tf_op jit(solution)/shard_map/widen_back/pallas_call | solution.py:564
  229.8 19.0 %attend_back.1 = (bf16[4,4,96,1024]{3,2,1,0:T(8,128)(2,1)}, bf16[4,4,96,1024]{3,2,1,0:T(8,128)(2,1)}, bf16[4,512,192]{2,1,0:T(8,128)(2,1)}, bf16[4,72,768]{2,1,0:T(8,128)(2,1)}) custom-call(s32[2]{0:T(128)} %pad_add_fusion.where, bf16[4,96,1024]{2,1,0:T(8,128)(2,1)} %copy-done, bf16[4,96,1024]{2,1,0:T(8,128)(2,1)} %copy-done.1, ...), custom_call_target="tpu_custom_call" | custom-call | tf_op jit(solution)/shard_map/attend_back/pallas_call | solution.py:651
  250.1 4.8 %collective-permute-start.48 = (bf16[128,768]{1,0:T(8,128)(2,1)S(1)}, bf16[128,768]{1,0:T(8,128)(2,1)S(1)}, u32[]{:S(2)}, u32[]{:S(2)}) collective-permute-start(bf16[128,768]{1,0:T(8,128)(2,1)S(1)} %get-tuple-element.128), channel_id=1, source_target_pairs={{0,3},{1,0},{2,1},{3,2},{4,7},{5,4},{6,5},{7,6},{8,11},{9,8},{10,9... | collective-permute-start | bytes 589832 | tf_op jit(solution)/shard_map/ppermute | solution.py:31
  256.6 3.7 collective-permute-done.48
  261.9 19.1 %project_back.1 = (bf16[4,4,96,640]{3,2,1,0:T(8,128)(2,1)}, bf16[4,4,96,640]{3,2,1,0:T(8,128)(2,1)}, bf16[512,768]{1,0:T(8,128)(2,1)}) custom-call(s32[2]{0:T(128)} %pad_add_fusion.where, bf16[4,96,640]{2,1,0:T(8,128)(2,1)} %copy-done.7, bf16[4,96,640]{2,1,0:T(8,128)(2,1)} %copy-done.9, bf16[4,96,640]{2,1,0:T(8,128)(2,1)} %copy-done.10, ...), custom_call_target="tpu_custom_call" | custom-call | tf_op jit(solution)/shard_map/project_back/pallas_call | solution.py:737
  281.0 1.6 bitcast_dynamic-update-slice_fusion.5
  284.5 4.4 %collective-permute-start.52 = (bf16[128,768]{1,0:T(8,128)(2,1)S(1)}, bf16[128,768]{1,0:T(8,128)(2,1)S(1)}, u32[]{:S(2)}, u32[]{:S(2)}) collective-permute-start(bf16[128,768]{1,0:T(8,128)(2,1)S(1)} %get-tuple-element.125), channel_id=1, source_target_pairs={{0,3},{1,0},{2,1},{3,2},{4,7},{5,4},{6,5},{7,6},{8,11},{9,8},{10,9... | collective-permute-start | bytes 589832 | tf_op jit(solution)/shard_map/ppermute | solution.py:31
  290.7 3.5 collective-permute-done.52
  294.2 1.8 collective-permute-start.54
  296.0 11.6 %collective-permute-done.53 = bf16[128,768]{1,0:T(8,128)(2,1)S(1)} collective-permute-done((bf16[128,768]{1,0:T(8,128)(2,1)S(1)}, bf16[128,768]{1,0:T(8,128)(2,1)S(1)}, u32[]{:S(2)}, u32[]{:S(2)}) %collective-permute-start.53) | collective-permute-done | bytes 196640 | tf_op jit(solution)/shard_map/ppermute | solution.py:31
  309.0 2.5 add_convert_fusion.1
  314.4 2.0 collective-permute-start.76
  316.4 4.6 %collective-permute-done.56 = bf16[2,96,640]{2,1,0:T(8,128)(2,1)S(1)} collective-permute-done((bf16[2,96,640]{2,1,0:T(8,128)(2,1)S(1)}, bf16[2,96,640]{2,1,0:T(8,128)(2,1)S(1)}, u32[]{:S(2)}, u32[]{:S(2)}) %collective-permute-start.56) | collective-permute-done | bytes 245792 | tf_op jit(solution)/shard_map/ppermute | solution.py:35
  323.5 3.8 collective-permute-done.74
  329.8 1.5 add_convert_fusion
  332.8 6.3 %collective-permute-done.57 = bf16[4,96,640]{2,1,0:T(8,128)(2,1)S(1)} collective-permute-done((bf16[4,96,640]{2,1,0:T(8,128)(2,1)S(1)}, bf16[4,96,640]{2,1,0:T(8,128)(2,1)S(1)}, u32[]{:S(2)}, u32[]{:S(2)}) %collective-permute-start.57) | collective-permute-done | bytes 491552 | tf_op jit(solution)/shard_map/ppermute | solution.py:35
  340.5 11.2 %collective-permute-done.75 = bf16[4,96,768]{2,1,0:T(8,128)(2,1)S(1)} collective-permute-done((bf16[4,96,768]{2,1,0:T(8,128)(2,1)S(1)}, bf16[4,96,768]{2,1,0:T(8,128)(2,1)S(1)}, u32[]{:S(2)}, u32[]{:S(2)}) %collective-permute-start.75) | collective-permute-done | bytes 589856 | tf_op jit(solution)/shard_map/ppermute | solution.py:35
  351.7 2.1 collective-permute-start.61
  354.0 3.8 collective-permute-done.65
  360.9 2.0 collective-permute-start.79
  362.9 1.9 collective-permute-start.80
  364.9 1.5 collective-permute-done.78
  366.4 8.5 %collective-permute-done.79 = bf16[96,768]{1,0:T(8,128)(2,1)S(1)} collective-permute-done((bf16[96,768]{1,0:T(8,128)(2,1)S(1)}, bf16[96,768]{1,0:T(8,128)(2,1)S(1)}, u32[]{:S(2)}, u32[]{:S(2)}) %collective-permute-start.79) | collective-permute-done | bytes 147488 | tf_op jit(solution)/shard_map/ppermute | solution.py:31
  375.2 2.3 collective-permute-done.66
  378.4 2.4 collective-permute-start.70
  380.8 1.9 collective-permute-start.71
  385.0 11.5 %collective-permute-done.70 = bf16[96,1024]{1,0:T(8,128)(2,1)S(1)} collective-permute-done((bf16[96,1024]{1,0:T(8,128)(2,1)S(1)}, bf16[96,1024]{1,0:T(8,128)(2,1)S(1)}, u32[]{:S(2)}, u32[]{:S(2)}) %collective-permute-start.70) | collective-permute-done | bytes 196640 | tf_op jit(solution)/shard_map/ppermute | solution.py:31
  (325 shorter events, 63.8 us)
Async XLA Ops:
  1.6 12.3 %collective-permute-start.39 = (bf16[32,768]{1,0:T(8,128)(2,1)S(1)}, bf16[32,768]{1,0:T(8,128)(2,1)S(1)}, u32[]{:S(2)}, u32[]{:S(2)}) collective-permute-start(bf16[32,768]{1,0:T(8,128)(2,1)S(1)} %constant_dynamic-slice_fusion.3), channel_id=1, source_target_pairs={{0,1},{1,2},{2,3},{3,0},{4,5},{5,6},{6,7},{7,4},{8,9},{9,10},{10,1... | collective-permute-start | bytes 147464 | tf_op jit(solution)/shard_map/ppermute | solution.py:31
  4.8 13.4 %collective-permute-start.40 = (bf16[32,768]{1,0:T(8,128)(2,1)S(1)}, bf16[32,768]{1,0:T(8,128)(2,1)S(1)}, u32[]{:S(2)}, u32[]{:S(2)}) collective-permute-start(bf16[32,768]{1,0:T(8,128)(2,1)S(1)} %constant_dynamic-slice_fusion.3), channel_id=1, source_target_pairs={{0,2},{1,3},{2,0},{3,1},{4,6},{5,7},{6,4},{7,5},{8,10},{9,11},{10,... | collective-permute-start | bytes 147464 | tf_op jit(solution)/shard_map/ppermute | solution.py:31
  7.3 11.4 %collective-permute-start.41 = (bf16[32,768]{1,0:T(8,128)(2,1)S(1)}, bf16[32,768]{1,0:T(8,128)(2,1)S(1)}, u32[]{:S(2)}, u32[]{:S(2)}) collective-permute-start(bf16[32,768]{1,0:T(8,128)(2,1)S(1)} %constant_dynamic-slice_fusion.3), channel_id=1, source_target_pairs={{0,3},{1,0},{2,1},{3,2},{4,7},{5,4},{6,5},{7,6},{8,11},{9,8},{10,9... | collective-permute-start | bytes 147464 | tf_op jit(solution)/shard_map/ppermute | solution.py:31
  11.5 15.8 %collective-permute-start.28 = (bf16[96,640]{1,0:T(8,128)(2,1)S(1)}, bf16[96,640]{1,0:T(8,128)(2,1)S(1)}, u32[]{:S(2)}, u32[]{:S(2)}) collective-permute-start(bf16[96,640]{1,0:T(8,128)(2,1)S(1)} %fusion.27), channel_id=1, source_target_pairs={{0,2},{1,3},{2,0},{3,1},{4,6},{5,7},{6,4},{7,5},{8,10},{9,11},{10,... | collective-permute-start | bytes 368648 | tf_op jit(solution)/shard_map/ppermute | solution.py:31
  13.9 14.1 %collective-permute-start.29 = (bf16[96,640]{1,0:T(8,128)(2,1)S(1)}, bf16[96,640]{1,0:T(8,128)(2,1)S(1)}, u32[]{:S(2)}, u32[]{:S(2)}) collective-permute-start(bf16[96,640]{1,0:T(8,128)(2,1)S(1)} %fusion.27), channel_id=1, source_target_pairs={{0,3},{1,0},{2,1},{3,2},{4,7},{5,4},{6,5},{7,6},{8,11},{9,8},{10,9... | collective-permute-start | bytes 368648 | tf_op jit(solution)/shard_map/ppermute | solution.py:31
  18.2 13.1 %collective-permute-start = (bf16[96,768]{1,0:T(8,128)(2,1)S(1)}, bf16[96,768]{1,0:T(8,128)(2,1)S(1)}, u32[]{:S(2)}, u32[]{:S(2)}) collective-permute-start(bf16[96,768]{1,0:T(8,128)(2,1)S(1)} %get-tuple-element.150), channel_id=1, source_target_pairs={{0,1},{1,2},{2,3},{3,0},{4,5},{5,6},{6,7},{7,4},{8,9},{9,10},{10,1... | collective-permute-start | bytes 442376 | tf_op jit(solution)/shard_map/ppermute | solution.py:31
  18.8 24.1 %collective-permute-start.1 = (bf16[96,768]{1,0:T(8,128)(2,1)S(1)}, bf16[96,768]{1,0:T(8,128)(2,1)S(1)}, u32[]{:S(2)}, u32[]{:S(2)}) collective-permute-start(bf16[96,768]{1,0:T(8,128)(2,1)S(1)} %get-tuple-element.150), channel_id=1, source_target_pairs={{0,2},{1,3},{2,0},{3,1},{4,6},{5,7},{6,4},{7,5},{8,10},{9,11},{10,... | collective-permute-start | bytes 442376 | tf_op jit(solution)/shard_map/ppermute | solution.py:31
  20.4 23.6 %collective-permute-start.2 = (bf16[96,768]{1,0:T(8,128)(2,1)S(1)}, bf16[96,768]{1,0:T(8,128)(2,1)S(1)}, u32[]{:S(2)}, u32[]{:S(2)}) collective-permute-start(bf16[96,768]{1,0:T(8,128)(2,1)S(1)} %get-tuple-element.150), channel_id=1, source_target_pairs={{0,3},{1,0},{2,1},{3,2},{4,7},{5,4},{6,5},{7,6},{8,11},{9,8},{10,9... | collective-permute-start | bytes 442376 | tf_op jit(solution)/shard_map/ppermute | solution.py:31
  28.0 24.1 %collective-permute-start.24 = (bf16[128,768]{1,0:T(8,128)(2,1)S(1)}, bf16[128,768]{1,0:T(8,128)(2,1)S(1)}, u32[]{:S(2)}, u32[]{:S(2)}) collective-permute-start(bf16[128,768]{1,0:T(8,128)(2,1)S(1)} %get-tuple-element.134), channel_id=1, source_target_pairs={{0,1},{1,2},{2,3},{3,0},{4,5},{5,6},{6,7},{7,4},{8,9},{9,10},{10,1... | collective-permute-start | bytes 589832 | tf_op jit(solution)/shard_map/ppermute | solution.py:31
  28.0 28.6 %collective-permute-start.25 = (bf16[128,768]{1,0:T(8,128)(2,1)S(1)}, bf16[128,768]{1,0:T(8,128)(2,1)S(1)}, u32[]{:S(2)}, u32[]{:S(2)}) collective-permute-start(bf16[128,768]{1,0:T(8,128)(2,1)S(1)} %get-tuple-element.136), channel_id=1, source_target_pairs={{0,2},{1,3},{2,0},{3,1},{4,6},{5,7},{6,4},{7,5},{8,10},{9,11},{10,... | collective-permute-start | bytes 589832 | tf_op jit(solution)/shard_map/ppermute | solution.py:31
  32.0 27.2 %collective-permute-start.26 = (bf16[128,768]{1,0:T(8,128)(2,1)S(1)}, bf16[128,768]{1,0:T(8,128)(2,1)S(1)}, u32[]{:S(2)}, u32[]{:S(2)}) collective-permute-start(bf16[128,768]{1,0:T(8,128)(2,1)S(1)} %get-tuple-element.135), channel_id=1, source_target_pairs={{0,3},{1,0},{2,1},{3,2},{4,7},{5,4},{6,5},{7,6},{8,11},{9,8},{10,9... | collective-permute-start | bytes 589832 | tf_op jit(solution)/shard_map/ppermute | solution.py:31
  42.9 32.7 %collective-permute-start.13 = (bf16[96,1024]{1,0:T(8,128)(2,1)S(1)}, bf16[96,1024]{1,0:T(8,128)(2,1)S(1)}, u32[]{:S(2)}, u32[]{:S(2)}) collective-permute-start(bf16[96,1024]{1,0:T(8,128)(2,1)S(1)} %fusion.25), channel_id=1, source_target_pairs={{0,2},{1,3},{2,0},{3,1},{4,6},{5,7},{6,4},{7,5},{8,10},{9,11},{10,... | collective-permute-start | bytes 589832 | tf_op jit(solution)/shard_map/ppermute | solution.py:31
  44.0 32.4 %collective-permute-start.14 = (bf16[96,1024]{1,0:T(8,128)(2,1)S(1)}, bf16[96,1024]{1,0:T(8,128)(2,1)S(1)}, u32[]{:S(2)}, u32[]{:S(2)}) collective-permute-start(bf16[96,1024]{1,0:T(8,128)(2,1)S(1)} %fusion.25), channel_id=1, source_target_pairs={{0,3},{1,0},{2,1},{3,2},{4,7},{5,4},{6,5},{7,6},{8,11},{9,8},{10,9... | collective-permute-start | bytes 589832 | tf_op jit(solution)/shard_map/ppermute | solution.py:31
  52.1 24.4 %collective-permute-start.12 = (bf16[96,1024]{1,0:T(8,128)(2,1)S(1)}, bf16[96,1024]{1,0:T(8,128)(2,1)S(1)}, u32[]{:S(2)}, u32[]{:S(2)}) collective-permute-start(bf16[96,1024]{1,0:T(8,128)(2,1)S(1)} %fusion.25), channel_id=1, source_target_pairs={{0,1},{1,2},{2,3},{3,0},{4,5},{5,6},{6,7},{7,4},{8,9},{9,10},{10,1... | collective-permute-start | bytes 589832 | tf_op jit(solution)/shard_map/ppermute | solution.py:31
  57.3 32.5 %collective-permute-start.30 = (bf16[4,96,640]{2,1,0:T(8,128)(2,1)S(1)}, bf16[4,96,640]{2,1,0:T(8,128)(2,1)S(1)}, u32[]{:S(2)}, u32[]{:S(2)}) collective-permute-start(bf16[4,96,640]{2,1,0:T(8,128)(2,1)S(1)} %pad_maximum_fusion.8.refs_0_), channel_id=1, source_target_pairs={{0,8},{8,0},{16,24},{24,16},{1,9},{9,1},{17,25},{25,17},{2,10},{10... | collective-permute-start | bytes 1474568 | tf_op jit(solution)/shard_map/ppermute | solution.py:35
  59.9 17.8 %collective-permute-start.45 = (bf16[128,768]{1,0:T(8,128)(2,1)S(1)}, bf16[128,768]{1,0:T(8,128)(2,1)S(1)}, u32[]{:S(2)}, u32[]{:S(2)}) collective-permute-start(bf16[128,768]{1,0:T(8,128)(2,1)S(1)} %get-tuple-element.130), channel_id=1, source_target_pairs={{0,1},{1,2},{2,3},{3,0},{4,5},{5,6},{6,7},{7,4},{8,9},{9,10},{10,1... | collective-permute-start | bytes 589832 | tf_op jit(solution)/shard_map/ppermute | solution.py:31
  76.4 11.3 %collective-permute-start.47 = (bf16[128,768]{1,0:T(8,128)(2,1)S(1)}, bf16[128,768]{1,0:T(8,128)(2,1)}, u32[]{:S(2)}, u32[]{:S(2)}) collective-permute-start(bf16[128,768]{1,0:T(8,128)(2,1)S(1)} %get-tuple-element.131), channel_id=1, source_target_pairs={{0,3},{1,0},{2,1},{3,2},{4,7},{5,4},{6,5},{7,6},{8,11},{9,8},{10,9... | collective-permute-start | bytes 589832 | tf_op jit(solution)/shard_map/ppermute | solution.py:31
  76.5 13.1 %collective-permute-start.42 = (bf16[4,32,768]{2,1,0:T(8,128)(2,1)S(1)}, bf16[4,32,768]{2,1,0:T(8,128)(2,1)S(1)}, u32[]{:S(2)}, u32[]{:S(2)}) collective-permute-start(bf16[4,32,768]{2,1,0:T(8,128)(2,1)S(1)} %pad_maximum_fusion.14), channel_id=1, source_target_pairs={{0,4},{4,0},{1,5},{5,1},{2,6},{6,2},{3,7},{7,3},{8,12},{12,8},{9,1... | collective-permute-start | bytes 589832 | tf_op jit(solution)/shard_map/ppermute | solution.py:39
  77.7 34.2 %collective-permute-start.3 = (bf16[4,96,768]{2,1,0:T(8,128)(2,1)S(1)}, bf16[4,96,768]{2,1,0:T(8,128)(2,1)S(1)}, u32[]{:S(2)}, u32[]{:S(2)}) collective-permute-start(bf16[4,96,768]{2,1,0:T(8,128)(2,1)S(1)} %pad_maximum_fusion.5.refs_0_), channel_id=1, source_target_pairs={{0,8},{8,0},{16,24},{24,16},{1,9},{9,1},{17,25},{25,17},{2,10},{10... | collective-permute-start | bytes 1769480 | tf_op jit(solution)/shard_map/ppermute | solution.py:35
  84.3 27.9 %collective-permute-start.4 = (bf16[4,96,768]{2,1,0:T(8,128)(2,1)S(1)}, bf16[4,96,768]{2,1,0:T(8,128)(2,1)S(1)}, u32[]{:S(2)}, u32[]{:S(2)}) collective-permute-start(bf16[4,96,768]{2,1,0:T(8,128)(2,1)S(1)} %pad_maximum_fusion.5.refs_0_), channel_id=1, source_target_pairs={{0,16},{8,24},{16,0},{24,8},{1,17},{9,25},{17,1},{25,9},{2,18},{10... | collective-permute-start | bytes 1769480 | tf_op jit(solution)/shard_map/ppermute | solution.py:35
  87.7 20.9 %collective-permute-start.31 = (bf16[4,96,640]{2,1,0:T(8,128)(2,1)S(1)}, bf16[4,96,640]{2,1,0:T(8,128)(2,1)S(1)}, u32[]{:S(2)}, u32[]{:S(2)}) collective-permute-start(bf16[4,96,640]{2,1,0:T(8,128)(2,1)S(1)} %pad_maximum_fusion.8.refs_0_), channel_id=1, source_target_pairs={{0,16},{8,24},{16,0},{24,8},{1,17},{9,25},{17,1},{25,9},{2,18},{10... | collective-permute-start | bytes 1474568 | tf_op jit(solution)/shard_map/ppermute | solution.py:35
  89.6 20.8 %collective-permute-start.34 = (bf16[4,96,640]{2,1,0:T(8,128)(2,1)S(1)}, bf16[4,96,640]{2,1,0:T(8,128)(2,1)}, u32[]{:S(2)}, u32[]{:S(2)}) collective-permute-start(bf16[4,96,640]{2,1,0:T(8,128)(2,1)S(1)} %pad_maximum_fusion.8.refs_0_), channel_id=1, source_target_pairs={{0,4},{4,0},{1,5},{5,1},{2,6},{6,2},{3,7},{7,3},{8,12},{12,8},{9,1... | collective-permute-start | bytes 1474568 | tf_op jit(solution)/shard_map/ppermute | solution.py:39
  89.8 44.2 %collective-permute-start.15 = (bf16[4,96,1024]{2,1,0:T(8,128)(2,1)S(1)}, bf16[4,96,1024]{2,1,0:T(8,128)(2,1)S(1)}, u32[]{:S(2)}, u32[]{:S(2)}) collective-permute-start(bf16[4,96,1024]{2,1,0:T(8,128)(2,1)S(1)} %pad_maximum_fusion.refs_0_), channel_id=1, source_target_pairs={{0,8},{8,0},{16,24},{24,16},{1,9},{9,1},{17,25},{25,17},{2,10},{10... | collective-permute-start | bytes 2359304 | tf_op jit(solution)/shard_map/ppermute | solution.py:35
  108.6 29.1 %collective-permute-start.16 = (bf16[4,96,1024]{2,1,0:T(8,128)(2,1)S(1)}, bf16[4,96,1024]{2,1,0:T(8,128)(2,1)S(1)}, u32[]{:S(2)}, u32[]{:S(2)}) collective-permute-start(bf16[4,96,1024]{2,1,0:T(8,128)(2,1)S(1)} %pad_maximum_fusion.refs_0_), channel_id=1, source_target_pairs={{0,16},{8,24},{16,0},{24,8},{1,17},{9,25},{17,1},{25,9},{2,18},{10... | collective-permute-start | bytes 2359304 | tf_op jit(solution)/shard_map/ppermute | solution.py:35
  110.4 27.4 %collective-permute-start.19 = (bf16[4,96,1024]{2,1,0:T(8,128)(2,1)S(1)}, bf16[4,96,1024]{2,1,0:T(8,128)(2,1)S(1)}, u32[]{:S(2)}, u32[]{:S(2)}) collective-permute-start(bf16[4,96,1024]{2,1,0:T(8,128)(2,1)S(1)} %pad_maximum_fusion.refs_0_), channel_id=1, source_target_pairs={{0,4},{4,0},{1,5},{5,1},{2,6},{6,2},{3,7},{7,3},{8,12},{12,8},{9,1... | collective-permute-start | bytes 2359304 | tf_op jit(solution)/shard_map/ppermute | solution.py:39
  111.9 19.3 %collective-permute-start.32 = (bf16[2,96,640]{2,1,0:T(8,128)(2,1)}, bf16[2,96,640]{2,1,0:T(8,128)(2,1)}, u32[]{:S(2)}, u32[]{:S(2)}) collective-permute-start(bf16[2,96,640]{2,1,0:T(8,128)(2,1)} %slice.346), channel_id=1, source_target_pairs={{0,16},{8,24},{16,0},{24,8},{1,17},{9,25},{17,1},{25,9},{2,18},{10... | collective-permute-start | bytes 737288 | tf_op jit(solution)/shard_map/ppermute | solution.py:35
  113.5 17.7 %collective-permute-start.33 = (bf16[2,96,640]{2,1,0:T(8,128)(2,1)}, bf16[2,96,640]{2,1,0:T(8,128)(2,1)}, u32[]{:S(2)}, u32[]{:S(2)}) collective-permute-start(bf16[2,96,640]{2,1,0:T(8,128)(2,1)} %slice.347), channel_id=1, source_target_pairs={{0,8},{8,0},{16,24},{24,16},{1,9},{9,1},{17,25},{25,17},{2,10},{10... | collective-permute-start | bytes 737288 | tf_op jit(solution)/shard_map/ppermute | solution.py:35
  131.2 13.9 %collective-permute-start.35 = (bf16[4,96,640]{2,1,0:T(8,128)(2,1)}, bf16[4,96,640]{2,1,0:T(8,128)(2,1)}, u32[]{:S(2)}, u32[]{:S(2)}) collective-permute-start(bf16[4,96,640]{2,1,0:T(8,128)(2,1)} %copy-done.9), channel_id=1, source_target_pairs={{0,4},{4,0},{1,5},{5,1},{2,6},{6,2},{3,7},{7,3},{8,12},{12,8},{9,1... | collective-permute-start | bytes 1474568 | tf_op jit(solution)/shard_map/ppermute | solution.py:39
  131.2 15.1 %collective-permute-start.36 = (bf16[4,96,640]{2,1,0:T(8,128)(2,1)}, bf16[4,96,640]{2,1,0:T(8,128)(2,1)}, u32[]{:S(2)}, u32[]{:S(2)}) collective-permute-start(bf16[4,96,640]{2,1,0:T(8,128)(2,1)} %copy-done.10), channel_id=1, source_target_pairs={{0,4},{4,0},{1,5},{5,1},{2,6},{6,2},{3,7},{7,3},{8,12},{12,8},{9,1... | collective-permute-start | bytes 1474568 | tf_op jit(solution)/shard_map/ppermute | solution.py:39
  143.6 26.9 %collective-permute-start.6 = (bf16[2,96,768]{2,1,0:T(8,128)(2,1)}, bf16[2,96,768]{2,1,0:T(8,128)(2,1)}, u32[]{:S(2)}, u32[]{:S(2)}) collective-permute-start(bf16[2,96,768]{2,1,0:T(8,128)(2,1)} %slice.343), channel_id=1, source_target_pairs={{0,8},{8,0},{16,24},{24,16},{1,9},{9,1},{17,25},{25,17},{2,10},{10... | collective-permute-start | bytes 884744 | tf_op jit(solution)/shard_map/ppermute | solution.py:35
  145.1 27.2 %collective-permute-start.17 = (bf16[2,96,1024]{2,1,0:T(8,128)(2,1)}, bf16[2,96,1024]{2,1,0:T(8,128)(2,1)S(1)}, u32[]{:S(2)}, u32[]{:S(2)}) collective-permute-start(bf16[2,96,1024]{2,1,0:T(8,128)(2,1)} %slice.344), channel_id=1, source_target_pairs={{0,16},{8,24},{16,0},{24,8},{1,17},{9,25},{17,1},{25,9},{2,18},{10... | collective-permute-start | bytes 1179656 | tf_op jit(solution)/shard_map/ppermute | solution.py:35
  146.3 26.6 %collective-permute-start.18 = (bf16[2,96,1024]{2,1,0:T(8,128)(2,1)}, bf16[2,96,1024]{2,1,0:T(8,128)(2,1)}, u32[]{:S(2)}, u32[]{:S(2)}) collective-permute-start(bf16[2,96,1024]{2,1,0:T(8,128)(2,1)} %slice.345), channel_id=1, source_target_pairs={{0,8},{8,0},{16,24},{24,16},{1,9},{9,1},{17,25},{25,17},{2,10},{10... | collective-permute-start | bytes 1179656 | tf_op jit(solution)/shard_map/ppermute | solution.py:35
  147.0 30.1 %collective-permute-start.20 = (bf16[4,96,1024]{2,1,0:T(8,128)(2,1)S(1)}, bf16[4,96,1024]{2,1,0:T(8,128)(2,1)S(1)}, u32[]{:S(2)}, u32[]{:S(2)}) collective-permute-start(bf16[4,96,1024]{2,1,0:T(8,128)(2,1)S(1)} %collective-permute-done.15.refs_1_), channel_id=1, source_target_pairs={{0,4},{4,0},{1,5},{5,1},{2,6},{6,2},{3,7},{7,3},{8,12},{12,8},{9,1... | collective-permute-start | bytes 2359304 | tf_op jit(solution)/shard_map/ppermute | solution.py:39
  147.1 30.5 %collective-permute-start.21 = (bf16[4,96,1024]{2,1,0:T(8,128)(2,1)S(1)}, bf16[4,96,1024]{2,1,0:T(8,128)(2,1)S(1)}, u32[]{:S(2)}, u32[]{:S(2)}) collective-permute-start(bf16[4,96,1024]{2,1,0:T(8,128)(2,1)S(1)} %collective-permute-done.16.refs_2_), channel_id=1, source_target_pairs={{0,4},{4,0},{1,5},{5,1},{2,6},{6,2},{3,7},{7,3},{8,12},{12,8},{9,1... | collective-permute-start | bytes 2359304 | tf_op jit(solution)/shard_map/ppermute | solution.py:39
  175.5 24.1 %collective-permute-start.7 = (bf16[4,96,768]{2,1,0:T(8,128)(2,1)}, bf16[4,96,768]{2,1,0:T(8,128)(2,1)}, u32[]{:S(2)}, u32[]{:S(2)}) collective-permute-start(bf16[4,96,768]{2,1,0:T(8,128)(2,1)} %copy-done.11), channel_id=1, source_target_pairs={{0,4},{4,0},{1,5},{5,1},{2,6},{6,2},{3,7},{7,3},{8,12},{12,8},{9,1... | collective-permute-start | bytes 1769480 | tf_op jit(solution)/shard_map/ppermute | solution.py:39
  175.6 24.0 %collective-permute-start.8 = (bf16[4,96,768]{2,1,0:T(8,128)(2,1)}, bf16[4,96,768]{2,1,0:T(8,128)(2,1)}, u32[]{:S(2)}, u32[]{:S(2)}) collective-permute-start(bf16[4,96,768]{2,1,0:T(8,128)(2,1)} %copy-done.14), channel_id=1, source_target_pairs={{0,4},{4,0},{1,5},{5,1},{2,6},{6,2},{3,7},{7,3},{8,12},{12,8},{9,1... | collective-permute-start | bytes 1769480 | tf_op jit(solution)/shard_map/ppermute | solution.py:39
  176.0 23.6 %collective-permute-start.9 = (bf16[4,96,768]{2,1,0:T(8,128)(2,1)}, bf16[4,96,768]{2,1,0:T(8,128)(2,1)}, u32[]{:S(2)}, u32[]{:S(2)}) collective-permute-start(bf16[4,96,768]{2,1,0:T(8,128)(2,1)} %copy-done.15), channel_id=1, source_target_pairs={{0,4},{4,0},{1,5},{5,1},{2,6},{6,2},{3,7},{7,3},{8,12},{12,8},{9,1... | collective-permute-start | bytes 1769480 | tf_op jit(solution)/shard_map/ppermute | solution.py:39
  177.1 22.5 %collective-permute-start.10 = (bf16[2,96,768]{2,1,0:T(8,128)(2,1)}, bf16[2,96,768]{2,1,0:T(8,128)(2,1)S(1)}, u32[]{:S(2)}, u32[]{:S(2)}) collective-permute-start(bf16[2,96,768]{2,1,0:T(8,128)(2,1)} %collective-permute-done.5.refs_3_), channel_id=1, source_target_pairs={{0,4},{4,0},{1,5},{5,1},{2,6},{6,2},{3,7},{7,3},{8,12},{12,8},{9,1... | collective-permute-start | bytes 884744 | tf_op jit(solution)/shard_map/ppermute | solution.py:39
  177.6 22.1 %collective-permute-start.11 = (bf16[2,96,768]{2,1,0:T(8,128)(2,1)}, bf16[2,96,768]{2,1,0:T(8,128)(2,1)S(1)}, u32[]{:S(2)}, u32[]{:S(2)}) collective-permute-start(bf16[2,96,768]{2,1,0:T(8,128)(2,1)} %collective-permute-done.6.refs_4_), channel_id=1, source_target_pairs={{0,4},{4,0},{1,5},{5,1},{2,6},{6,2},{3,7},{7,3},{8,12},{12,8},{9,1... | collective-permute-start | bytes 884744 | tf_op jit(solution)/shard_map/ppermute | solution.py:39
  219.3 89.7 %collective-permute-start.73 = (bf16[4,4,96,768]{3,2,1,0:T(8,128)(2,1)}, bf16[4,4,96,768]{3,2,1,0:T(8,128)(2,1)}, u32[]{:S(2)}, u32[]{:S(2)}) collective-permute-start(bf16[4,4,96,768]{3,2,1,0:T(8,128)(2,1)} %get-tuple-element.73), channel_id=1, source_target_pairs={{0,4},{4,0},{1,5},{5,1},{2,6},{6,2},{3,7},{7,3},{8,12},{12,8},{9,1... | collective-permute-start | bytes 7077896 | tf_op jit(solution)/shard_map/ppermute | solution.py:39
  248.9 81.0 %collective-permute-start.64 = (bf16[4,4,96,1024]{3,2,1,0:T(8,128)(2,1)}, bf16[4,4,96,1024]{3,2,1,0:T(8,128)(2,1)S(1)}, u32[]{:S(2)}, u32[]{:S(2)}) collective-permute-start(bf16[4,4,96,1024]{3,2,1,0:T(8,128)(2,1)} %get-tuple-element.71), channel_id=1, source_target_pairs={{0,4},{4,0},{1,5},{5,1},{2,6},{6,2},{3,7},{7,3},{8,12},{12,8},{9,1... | collective-permute-start | bytes 9437192 | tf_op jit(solution)/shard_map/ppermute | solution.py:39
  249.2 11.8 %collective-permute-start.51 = (bf16[4,72,768]{2,1,0:T(8,128)(2,1)}, bf16[4,72,768]{2,1,0:T(8,128)(2,1)S(1)}, u32[]{:S(2)}, u32[]{:S(2)}) collective-permute-start(bf16[4,72,768]{2,1,0:T(8,128)(2,1)} %get-tuple-element.66), channel_id=1, source_target_pairs={{0,4},{4,0},{1,5},{5,1},{2,6},{6,2},{3,7},{7,3},{8,12},{12,8},{9,1... | collective-permute-start | bytes 1327112 | tf_op jit(solution)/shard_map/ppermute | solution.py:39
  250.1 10.1 %collective-permute-start.48 = (bf16[128,768]{1,0:T(8,128)(2,1)S(1)}, bf16[128,768]{1,0:T(8,128)(2,1)S(1)}, u32[]{:S(2)}, u32[]{:S(2)}) collective-permute-start(bf16[128,768]{1,0:T(8,128)(2,1)S(1)} %get-tuple-element.128), channel_id=1, source_target_pairs={{0,3},{1,0},{2,1},{3,2},{4,7},{5,4},{6,5},{7,6},{8,11},{9,8},{10,9... | collective-permute-start | bytes 589832 | tf_op jit(solution)/shard_map/ppermute | solution.py:31
  254.9 26.1 %collective-permute-start.49 = (bf16[128,768]{1,0:T(8,128)(2,1)}, bf16[128,768]{1,0:T(8,128)(2,1)}, u32[]{:S(2)}, u32[]{:S(2)}) collective-permute-start(bf16[128,768]{1,0:T(8,128)(2,1)} %get-tuple-element.127), channel_id=1, source_target_pairs={{0,2},{1,3},{2,0},{3,1},{4,6},{5,7},{6,4},{7,5},{8,10},{9,11},{10,... | collective-permute-start | bytes 589832 | tf_op jit(solution)/shard_map/ppermute | solution.py:31
  260.3 22.4 %collective-permute-start.50 = (bf16[128,768]{1,0:T(8,128)(2,1)S(1)}, bf16[128,768]{1,0:T(8,128)(2,1)S(1)}, u32[]{:S(2)}, u32[]{:S(2)}) collective-permute-start(bf16[128,768]{1,0:T(8,128)(2,1)S(1)} %get-tuple-element.126), channel_id=1, source_target_pairs={{0,1},{1,2},{2,3},{3,0},{4,5},{5,6},{6,7},{7,4},{8,9},{9,10},{10,1... | collective-permute-start | bytes 589832 | tf_op jit(solution)/shard_map/ppermute | solution.py:31
  281.0 30.6 %collective-permute-start.55 = (bf16[4,4,96,640]{3,2,1,0:T(8,128)(2,1)}, bf16[4,4,96,640]{3,2,1,0:T(8,128)(2,1)S(1)}, u32[]{:S(2)}, u32[]{:S(2)}) collective-permute-start(bf16[4,4,96,640]{3,2,1,0:T(8,128)(2,1)} %get-tuple-element.69), channel_id=1, source_target_pairs={{0,4},{4,0},{1,5},{5,1},{2,6},{6,2},{3,7},{7,3},{8,12},{12,8},{9,1... | collective-permute-start | bytes 5898248 | tf_op jit(solution)/shard_map/ppermute | solution.py:39
  288.9 18.7 %collective-permute-start.53 = (bf16[128,768]{1,0:T(8,128)(2,1)S(1)}, bf16[128,768]{1,0:T(8,128)(2,1)S(1)}, u32[]{:S(2)}, u32[]{:S(2)}) collective-permute-start(bf16[128,768]{1,0:T(8,128)(2,1)S(1)} %get-tuple-element.124), channel_id=1, source_target_pairs={{0,2},{1,3},{2,0},{3,1},{4,6},{5,7},{6,4},{7,5},{8,10},{9,11},{10,... | collective-permute-start | bytes 589832 | tf_op jit(solution)/shard_map/ppermute | solution.py:31
  294.2 13.4 %collective-permute-start.54 = (bf16[128,768]{1,0:T(8,128)(2,1)S(1)}, bf16[128,768]{1,0:T(8,128)(2,1)S(1)}, u32[]{:S(2)}, u32[]{:S(2)}) collective-permute-start(bf16[128,768]{1,0:T(8,128)(2,1)S(1)} %get-tuple-element.123), channel_id=1, source_target_pairs={{0,1},{1,2},{2,3},{3,0},{4,5},{5,6},{6,7},{7,4},{8,9},{9,10},{10,1... | collective-permute-start | bytes 589832 | tf_op jit(solution)/shard_map/ppermute | solution.py:31
  313.5 13.8 %collective-permute-start.74 = (bf16[2,96,768]{2,1,0:T(8,128)(2,1)S(1)}, bf16[2,96,768]{2,1,0:T(8,128)(2,1)S(1)}, u32[]{:S(2)}, u32[]{:S(2)}) collective-permute-start(bf16[2,96,768]{2,1,0:T(8,128)(2,1)S(1)} %get-tuple-element.110), channel_id=1, source_target_pairs={{0,16},{8,24},{16,0},{24,8},{1,17},{9,25},{17,1},{25,9},{2,18},{10... | collective-permute-start | bytes 884744 | tf_op jit(solution)/shard_map/ppermute | solution.py:35
  314.4 14.1 %collective-permute-start.76 = (bf16[2,96,768]{2,1,0:T(8,128)(2,1)S(1)}, bf16[2,96,768]{2,1,0:T(8,128)(2,1)S(1)}, u32[]{:S(2)}, u32[]{:S(2)}) collective-permute-start(bf16[2,96,768]{2,1,0:T(8,128)(2,1)S(1)} %get-tuple-element.111), channel_id=1, source_target_pairs={{0,8},{8,0},{16,24},{24,16},{1,9},{9,1},{17,25},{25,17},{2,10},{10... | collective-permute-start | bytes 884744 | tf_op jit(solution)/shard_map/ppermute | solution.py:35
  322.4 16.7 %collective-permute-start.57 = (bf16[4,96,640]{2,1,0:T(8,128)(2,1)S(1)}, bf16[4,96,640]{2,1,0:T(8,128)(2,1)S(1)}, u32[]{:S(2)}, u32[]{:S(2)}) collective-permute-start(bf16[4,96,640]{2,1,0:T(8,128)(2,1)S(1)} %pad_maximum_fusion.9), channel_id=1, source_target_pairs={{0,8},{8,0},{16,24},{24,16},{1,9},{9,1},{17,25},{25,17},{2,10},{10... | collective-permute-start | bytes 1474568 | tf_op jit(solution)/shard_map/ppermute | solution.py:35
  322.6 16.5 %collective-permute-start.59 = (bf16[4,96,640]{2,1,0:T(8,128)(2,1)S(1)}, bf16[4,96,640]{2,1,0:T(8,128)(2,1)S(1)}, u32[]{:S(2)}, u32[]{:S(2)}) collective-permute-start(bf16[4,96,640]{2,1,0:T(8,128)(2,1)S(1)} %pad_maximum_fusion.10), channel_id=1, source_target_pairs={{0,16},{8,24},{16,0},{24,8},{1,17},{9,25},{17,1},{25,9},{2,18},{10... | collective-permute-start | bytes 1474568 | tf_op jit(solution)/shard_map/ppermute | solution.py:35
  328.8 23.0 %collective-permute-start.75 = (bf16[4,96,768]{2,1,0:T(8,128)(2,1)S(1)}, bf16[4,96,768]{2,1,0:T(8,128)(2,1)S(1)}, u32[]{:S(2)}, u32[]{:S(2)}) collective-permute-start(bf16[4,96,768]{2,1,0:T(8,128)(2,1)S(1)} %pad_maximum_fusion.6), channel_id=1, source_target_pairs={{0,8},{8,0},{16,24},{24,16},{1,9},{9,1},{17,25},{25,17},{2,10},{10... | collective-permute-start | bytes 1769480 | tf_op jit(solution)/shard_map/ppermute | solution.py:35
  328.9 24.9 %collective-permute-start.77 = (bf16[4,96,768]{2,1,0:T(8,128)(2,1)S(1)}, bf16[4,96,768]{2,1,0:T(8,128)(2,1)S(1)}, u32[]{:S(2)}, u32[]{:S(2)}) collective-permute-start(bf16[4,96,768]{2,1,0:T(8,128)(2,1)S(1)} %pad_maximum_fusion.7), channel_id=1, source_target_pairs={{0,16},{8,24},{16,0},{24,8},{1,17},{9,25},{17,1},{25,9},{2,18},{10... | collective-permute-start | bytes 1769480 | tf_op jit(solution)/shard_map/ppermute | solution.py:35
  331.5 26.3 %collective-permute-start.65 = (bf16[2,96,1024]{2,1,0:T(8,128)(2,1)S(1)}, bf16[2,96,1024]{2,1,0:T(8,128)(2,1)S(1)}, u32[]{:S(2)}, u32[]{:S(2)}) collective-permute-start(bf16[2,96,1024]{2,1,0:T(8,128)(2,1)S(1)} %get-tuple-element.104), channel_id=1, source_target_pairs={{0,16},{8,24},{16,0},{24,8},{1,17},{9,25},{17,1},{25,9},{2,18},{10... | collective-permute-start | bytes 1179656 | tf_op jit(solution)/shard_map/ppermute | solution.py:35
  339.1 19.7 %collective-permute-start.67 = (bf16[2,96,1024]{2,1,0:T(8,128)(2,1)S(1)}, bf16[2,96,1024]{2,1,0:T(8,128)(2,1)S(1)}, u32[]{:S(2)}, u32[]{:S(2)}) collective-permute-start(bf16[2,96,1024]{2,1,0:T(8,128)(2,1)S(1)} %get-tuple-element.105), channel_id=1, source_target_pairs={{0,8},{8,0},{16,24},{24,16},{1,9},{9,1},{17,25},{25,17},{2,10},{10... | collective-permute-start | bytes 1179656 | tf_op jit(solution)/shard_map/ppermute | solution.py:35
  339.3 21.2 %collective-permute-start.60 = (bf16[96,640]{1,0:T(8,128)(2,1)S(1)}, bf16[96,640]{1,0:T(8,128)(2,1)S(1)}, u32[]{:S(2)}, u32[]{:S(2)}) collective-permute-start(bf16[96,640]{1,0:T(8,128)(2,1)S(1)} %get-tuple-element.140), channel_id=1, source_target_pairs={{0,3},{1,0},{2,1},{3,2},{4,7},{5,4},{6,5},{7,6},{8,11},{9,8},{10,9... | collective-permute-start | bytes 368648 | tf_op jit(solution)/shard_map/ppermute | solution.py:31
  359.2 18.3 %collective-permute-start.66 = (bf16[4,96,1024]{2,1,0:T(8,128)(2,1)S(1)}, bf16[4,96,1024]{2,1,0:T(8,128)(2,1)S(1)}, u32[]{:S(2)}, u32[]{:S(2)}) collective-permute-start(bf16[4,96,1024]{2,1,0:T(8,128)(2,1)S(1)} %pad_maximum_fusion.3), channel_id=1, source_target_pairs={{0,8},{8,0},{16,24},{24,16},{1,9},{9,1},{17,25},{25,17},{2,10},{10... | collective-permute-start | bytes 2359304 | tf_op jit(solution)/shard_map/ppermute | solution.py:35
  359.6 18.3 %collective-permute-start.68 = (bf16[4,96,1024]{2,1,0:T(8,128)(2,1)S(1)}, bf16[4,96,1024]{2,1,0:T(8,128)(2,1)S(1)}, u32[]{:S(2)}, u32[]{:S(2)}) collective-permute-start(bf16[4,96,1024]{2,1,0:T(8,128)(2,1)S(1)} %pad_maximum_fusion.4), channel_id=1, source_target_pairs={{0,16},{8,24},{16,0},{24,8},{1,17},{9,25},{17,1},{25,9},{2,18},{10... | collective-permute-start | bytes 2359304 | tf_op jit(solution)/shard_map/ppermute | solution.py:35
  360.9 14.0 %collective-permute-start.79 = (bf16[96,768]{1,0:T(8,128)(2,1)S(1)}, bf16[96,768]{1,0:T(8,128)(2,1)S(1)}, u32[]{:S(2)}, u32[]{:S(2)}) collective-permute-start(bf16[96,768]{1,0:T(8,128)(2,1)S(1)} %get-tuple-element.139), channel_id=1, source_target_pairs={{0,2},{1,3},{2,0},{3,1},{4,6},{5,7},{6,4},{7,5},{8,10},{9,11},{10,... | collective-permute-start | bytes 442376 | tf_op jit(solution)/shard_map/ppermute | solution.py:31
  362.9 12.0 %collective-permute-start.80 = (bf16[96,768]{1,0:T(8,128)(2,1)S(1)}, bf16[96,768]{1,0:T(8,128)(2,1)S(1)}, u32[]{:S(2)}, u32[]{:S(2)}) collective-permute-start(bf16[96,768]{1,0:T(8,128)(2,1)S(1)} %get-tuple-element.138), channel_id=1, source_target_pairs={{0,1},{1,2},{2,3},{3,0},{4,5},{5,6},{6,7},{7,4},{8,9},{9,10},{10,1... | collective-permute-start | bytes 442376 | tf_op jit(solution)/shard_map/ppermute | solution.py:31
  374.9 21.8 %collective-permute-start.81 = (bf16[96,768]{1,0:T(8,128)(2,1)S(1)}, bf16[96,768]{1,0:T(8,128)(2,1)S(1)}, u32[]{:S(2)}, u32[]{:S(2)}) collective-permute-start(bf16[96,768]{1,0:T(8,128)(2,1)S(1)} %fusion.19), channel_id=1, source_target_pairs={{0,4},{4,0},{1,5},{5,1},{2,6},{6,2},{3,7},{7,3},{8,12},{12,8},{9,1... | collective-permute-start | bytes 442376 | tf_op jit(solution)/shard_map/ppermute | solution.py:39
  378.4 18.1 %collective-permute-start.70 = (bf16[96,1024]{1,0:T(8,128)(2,1)S(1)}, bf16[96,1024]{1,0:T(8,128)(2,1)S(1)}, u32[]{:S(2)}, u32[]{:S(2)}) collective-permute-start(bf16[96,1024]{1,0:T(8,128)(2,1)S(1)} %get-tuple-element.122), channel_id=1, source_target_pairs={{0,2},{1,3},{2,0},{3,1},{4,6},{5,7},{6,4},{7,5},{8,10},{9,11},{10,... | collective-permute-start | bytes 589832 | tf_op jit(solution)/shard_map/ppermute | solution.py:31
  380.8 15.7 %collective-permute-start.71 = (bf16[96,1024]{1,0:T(8,128)(2,1)S(1)}, bf16[96,1024]{1,0:T(8,128)(2,1)S(1)}, u32[]{:S(2)}, u32[]{:S(2)}) collective-permute-start(bf16[96,1024]{1,0:T(8,128)(2,1)S(1)} %get-tuple-element.121), channel_id=1, source_target_pairs={{0,1},{1,2},{2,3},{3,0},{4,5},{5,6},{6,7},{7,4},{8,9},{9,10},{10,1... | collective-permute-start | bytes 589832 | tf_op jit(solution)/shard_map/ppermute | solution.py:31
  (75 other events, 919.3 us)
